TPU v7x, 128 devices: a whole 4x4x4 slice. The times are simulated.
128 devices in a mesh: shard: 16 (over y, x), tensor: 8 (over z, core).
Axes of the slice: x: 4, y: 4, z: 4, core: 2. Of those that a mesh axis runs over, the one named last changes fastest.
Arguments:
- gradients: bfloat16 [4, 512, 6144], P(None, ('shard', 'tensor')), may hold values from -6 to 6
- adam_mean: float32 [4, 512, 6144], P(None, ('shard', 'tensor')), may hold values from -14 to 14
- adam_square: float32 [4, 512, 6144], P(None, ('shard', 'tensor')), may hold values from 0.001 to 0.05
- stat_left: float32 [128, 3, 512, 512], P(('shard', 'tensor')), may hold values from -2 to 30, as said below
- stat_right: float32 [128, 3, 128, 128], P(('shard', 'tensor')), may hold values from -12 to 120, as said below
- root_left: float32 [128, 3, 512, 512], P(('shard', 'tensor')), may hold values from -0.1 to 0.6, as said below
- root_right: float32 [128, 3, 128, 128], P(('shard', 'tensor')), may hold values from -0.1 to 0.4, as said below
- owners: int32 [192], replicated, may hold values from 0 to 127, as said below
- small_grad: float32 [6336], replicated, may hold values from -1.2 to 1.2
- small_mean: float32 [6336], replicated, may hold values from -0.6 to 0.6
- small_square: float32 [6336], replicated, may hold values from 0.001 to 0.05
Outputs:
- updates: float32 [4, 512, 6144], P(None, ('shard', 'tensor'))
- mean_out: float32 [4, 512, 6144], P(None, ('shard', 'tensor'))
- square_out: float32 [4, 512, 6144], P(None, ('shard', 'tensor'))
- left_out: float32 [128, 3, 512, 512], P(('shard', 'tensor'))
- right_out: float32 [128, 3, 128, 128], P(('shard', 'tensor'))
- small_update: float32 [6336], replicated
- small_mean_out: float32 [6336], replicated
- small_square_out: float32 [6336], replicated
Inputs may be any that keep to these rules, and one draw needn't show every extreme that they name: `owners`: no device owns more than 3 blocks, and some device owns exactly 3. `stat_left`: symmetric. `stat_right`: symmetric. `root_left`: symmetric. `root_right`: symmetric.
All inputs are finite; a program needn't handle non-finite values.
Results may differ from a plain program's by a relative error of at most 0.00095.
Values may be sent and summed in bfloat16 or wider, within the bound.
A program may use at most 64 MiB of HBM per device.

v0:
```python
import jax
import jax.numpy as jnp
from jax import lax
from jax.sharding import PartitionSpec as P

BLOCK = 128


PRECISE = lax.Precision.HIGHEST


def adam_moments(grad_wide, mean_old, square_old):
    mean_new = 0.9 * mean_old + 0.1 * grad_wide
    square_new = 0.95 * square_old + 0.05 * grad_wide * grad_wide
    return (mean_new, square_new, mean_new / (jnp.sqrt(square_new) + 1e-08))


def per_device(
    gradients,
    adam_mean,
    adam_square,
    stat_left,
    stat_right,
    root_left,
    root_right,
    owners,
    small_grad,
    small_mean,
    small_square,
):
    layer_count, row_count, col_count = gradients.shape
    block_count = col_count // BLOCK
    devices = lax.axis_size(("shard", "tensor"))
    slot_count = stat_left.shape[1]
    total_blocks = owners.shape[0]
    positions = jnp.arange(total_blocks, dtype=jnp.int32)
    earlier = (owners[:, None] == owners[None, :]) & (positions[None, :] < positions[:, None])
    slot_index = jnp.sum(earlier.astype(jnp.int32), axis=1)
    target = slot_index * devices + owners
    places = jnp.arange(slot_count * devices, dtype=jnp.int32)
    picker = (
        (places[:, None] == target[None, :])
        .astype(jnp.bfloat16)
        .reshape(slot_count * devices, layer_count, block_count)
    )
    grad_wide = gradients.astype(jnp.float32)
    mean_out, square_out, direction = adam_moments(grad_wide, adam_mean, adam_square)
    adam_part = jnp.sum(
        jnp.square(direction).reshape(layer_count, row_count, block_count, BLOCK), axis=(1, 3)
    )
    adam_sums = lax.psum(adam_part, ("shard", "tensor"))
    pieces = gradients.reshape(layer_count, row_count, block_count, BLOCK)
    outgoing = jnp.einsum(
        "qln,lrnb->qrb", picker, pieces, preferred_element_type=jnp.float32
    ).astype(jnp.bfloat16)
    outgoing = outgoing.reshape(slot_count, devices, row_count, BLOCK)
    incoming = lax.all_to_all(
        outgoing, ("shard", "tensor"), split_axis=1, concat_axis=1, tiled=True
    )
    block_grads = incoming.reshape(slot_count, devices * row_count, BLOCK)
    left_out = (
        stat_left
        + jnp.einsum("cib,cjb->cij", block_grads, block_grads, preferred_element_type=jnp.float32)[
            None
        ]
    )
    right_out = (
        stat_right
        + jnp.einsum("cib,cid->cbd", block_grads, block_grads, preferred_element_type=jnp.float32)[
            None
        ]
    )
    left_applied = jnp.einsum(
        "cij,cjb->cib", root_left[0], block_grads.astype(jnp.float32), precision=PRECISE
    )
    precond = jnp.einsum("cib,cbd->cid", left_applied, root_right[0], precision=PRECISE)
    shaped = precond.reshape(slot_count, devices, row_count, BLOCK)
    returned = lax.all_to_all(shaped, ("shard", "tensor"), split_axis=1, concat_axis=1, tiled=True)
    returned = returned.reshape(slot_count * devices, row_count, BLOCK)
    own_rows = jnp.take(returned, target, axis=0).reshape(
        layer_count, block_count, row_count, BLOCK
    )
    precond_part = jnp.sum(jnp.square(own_rows), axis=(2, 3))
    precond_sums = lax.psum(precond_part, ("shard", "tensor"))
    graft_ratio = jnp.sqrt(adam_sums / (precond_sums + 1e-06))
    updates = (
        (own_rows * graft_ratio[:, :, None, None])
        .transpose(0, 2, 1, 3)
        .reshape(layer_count, row_count, col_count)
    )
    small_mean_out, small_square_out, small_update = adam_moments(
        small_grad, small_mean, small_square
    )
    return (
        updates,
        mean_out,
        square_out,
        left_out,
        right_out,
        small_update,
        small_mean_out,
        small_square_out,
    )


def solution(mesh):
    in_specs = (
        P(None, ("shard", "tensor"), None),
        P(None, ("shard", "tensor"), None),
        P(None, ("shard", "tensor"), None),
        P(("shard", "tensor"), None, None, None),
        P(("shard", "tensor"), None, None, None),
        P(("shard", "tensor"), None, None, None),
        P(("shard", "tensor"), None, None, None),
        P(),
        P(),
        P(),
        P(),
    )
    out_specs = (
        P(None, ("shard", "tensor"), None),
        P(None, ("shard", "tensor"), None),
        P(None, ("shard", "tensor"), None),
        P(("shard", "tensor"), None, None, None),
        P(("shard", "tensor"), None, None, None),
        P(),
        P(),
        P(),
    )
    return jax.shard_map(
        per_device, mesh=mesh, in_specs=in_specs, out_specs=out_specs, check_vma=False
    )
```

profile of v0, /device:TPU:1, one launch (start us, length us, event | category | flops | bytes accessed | tf_op | source)
XLA Modules:
  0.0 130.2 jit_solution(13839298927316737262)
XLA Ops:
  0.6 0.0 copy-start
  0.6 0.0 copy-start.1
  0.7 1.2 reshape.75
  1.9 0.9 convert_reduce_fusion
  2.8 0.7 compare_and_fusion
  3.5 0.1 eq.48
  3.6 0.4 fusion.2
  4.0 1.1 copy.52
  5.1 11.9 %all-to-all-start = ((bf16[3,128,4,128]{3,2,0,1:T(4,128)(2,1)}), bf16[3,128,4,128]{3,2,0,1:T(4,128)(2,1)}, u32[]{:S(2)}, u32[]{:S(2)}) async-start(bf16[3,128,4,128]{3,2,0,1:T(4,128)(2,1)} %copy.52), calls=%async_computation | async-start | bytes 786432 | tf_op jit(solution)/shard_map/all_to_all | solution.py:57
  16.9 1.4 %add_divide_fusion = (f32[6336]{0:T(1024)}, f32[6336]{0:T(1024)}, f32[6336]{0:T(1024)}) fusion(f32[6336]{0:T(1024)} %param.19, f32[6336]{0:T(1024)} %param.21, f32[6336]{0:T(1024)} %param.20), kind=kLoop, calls=%fused_computation.26 | loop fusion | flops 57024 | bytes 152064 | tf_op jit(solution)/shard_map/div | solution.py:15
  18.4 3.2 %multiply_reduce_fusion.1 = (f32[4,6144]{1,0:T(4,128)}, f32[4,4,6144]{2,1,0:T(4,128)}, f32[4,4,6144]{2,1,0:T(4,128)}) fusion(bf16[4,4,6144]{2,1,0:T(4,128)(2,1)S(1)} %copy-done.1, f32[4,4,6144]{2,1,0:T(4,128)} %param.13, f32[4,4,6144]{2,1,0:T(4,128)} %param.12), kind=kLoop, calls=%fused_computation.14 | loop fusion | flops 1155072 | bytes 1867776 | tf_op jit(solution)/shard_map/reduce_sum | solution.py:48
  21.5 7.3 %all-to-all-done = bf16[3,128,4,128]{3,2,0,1:T(4,128)(2,1)} async-done(((bf16[3,128,4,128]{3,2,0,1:T(4,128)(2,1)}), bf16[3,128,4,128]{3,2,0,1:T(4,128)(2,1)}, u32[]{:S(2)}, u32[]{:S(2)}) %all-to-all-start) | async-done | bytes 393248 | tf_op jit(solution)/shard_map/all_to_all | solution.py:57
  28.8 1.1 copy.53
  30.0 0.0 copy-done
  30.0 1.6 %fusion = f32[3,128,512]{1,2,0:T(8,128)S(1)} fusion(bf16[3,512,128]{2,1,0:T(8,128)(2,1)S(1)} %bitcast.46, f32[1,3,512,512]{3,2,1,0:T(8,128)S(1)} %copy-done), kind=kOutput, calls=%fused_computation.2 | convolution fusion | flops 1207959552 | bytes 4325376 | tf_op jit(solution)/shard_map/cij,cjb->cib/dot_general | solution.py:73
  31.5 1.7 %fusion.8 = f32[3,512,128]{2,1,0:T(8,128)S(1)} fusion(f32[3,128,512]{1,2,0:T(8,128)S(1)} %fusion, f32[1,3,128,128]{3,2,1,0:T(8,128)} %param.17), kind=kOutput, calls=%fused_computation.17 | convolution fusion | flops 301989888 | bytes 1769472 | tf_op jit(solution)/shard_map/cib,cbd->cid/dot_general | solution.py:76
  33.3 1.0 copy.56
  34.3 5.6 %all-to-all-start.1 = ((f32[3,128,4,128]{3,2,0,1:T(4,128)}), f32[3,128,4,128]{3,2,0,1:T(4,128)}, u32[]{:S(2)}, u32[]{:S(2)}) async-start(f32[3,128,4,128]{3,2,0,1:T(4,128)} %copy.56), calls=%async_computation.1 | async-start | bytes 1572864 | tf_op jit(solution)/shard_map/all_to_all | solution.py:78
  39.9 0.1 broadcast_in_dim.31
  40.0 1.0 bitcast_reduce_fusion
  41.0 1.9 %fusion.3 = f32[1,3,128,128]{3,2,1,0:T(8,128)} fusion(f32[1,3,128,128]{3,2,1,0:T(8,128)} %param.15, bf16[3,512,128]{2,1,0:T(8,128)(2,1)S(1)} %bitcast.47), kind=kOutput, calls=%fused_computation.7 | convolution fusion | flops 50380800 | bytes 786432 | tf_op jit(solution)/shard_map/cib,cid->cbd/dot_general | solution.py:69
  42.9 4.1 %bitcast_add_fusion = f32[1,3,512,512]{3,2,1,0:T(8,128)} fusion(f32[1,3,512,512]{3,2,1,0:T(8,128)} %param.14, bf16[3,512,128]{2,1,0:T(8,128)(2,1)S(1)} %bitcast.48), kind=kOutput, calls=%fused_computation.1 | convolution fusion | flops 202113024 | bytes 6684672 | tf_op jit(solution)/shard_map/cib,cjb->cij/dot_general | solution.py:63
  47.1 8.9 %all-to-all-done.1 = f32[3,128,4,128]{3,2,0,1:T(4,128)} async-done(((f32[3,128,4,128]{3,2,0,1:T(4,128)}), f32[3,128,4,128]{3,2,0,1:T(4,128)}, u32[]{:S(2)}, u32[]{:S(2)}) %all-to-all-start.1) | async-done | bytes 786464 | tf_op jit(solution)/shard_map/all_to_all | solution.py:78
  56.0 2.2 %copy.57 = f32[3,128,4,128]{3,2,1,0:T(4,128)} copy(f32[3,128,4,128]{3,2,0,1:T(4,128)} %all-to-all-done.1) | data formatting | bytes 1572864 | tf_op jit(solution)/shard_map/all_to_all | solution.py:78
  58.2 2.0 %gather_fusion = f32[192,4,128]{2,1,0:T(4,128)S(1)} fusion(f32[384,4,128]{2,1,0:T(4,128)} %bitcast.50, s32[1024]{0:T(1024)S(1)} %pad_clamp_fusion), kind=kCustom, calls=%fused_computation | custom fusion | bytes 787200 | tf_op jit(solution)/shard_map/jit(_take)/gather | solution.py:80
  60.2 0.8 copy.58
  61.0 2.0 %multiply_reduce_fusion = f32[192]{0:T(256)S(1)} fusion(f32[192,4,128]{2,1,0:T(4,128)S(1)} %gather_fusion, pred[192]{0:T(512)(128)(4,1)S(1)} %get-tuple-element.53), kind=kLoop, calls=%fused_computation.13 | loop fusion | flops 294720 | bytes 394176 | tf_op jit(solution)/shard_map/reduce_sum | solution.py:83
  63.0 0.1 reduce_sum.41
  63.1 63.1 %all-reduce = (f32[4,48]{1,0:T(4,128)S(1)}, f32[4,48]{1,0:T(4,128)S(1)}) all-reduce(f32[4,48]{1,0:T(4,128)S(1)} %bitcast_reduce_fusion, f32[4,48]{1,0:T(4,128)S(1)} %reduce_sum.41), channel_id=1, replica_groups=mesh['shard'=16,'tensor'=8] {'shard','tensor'}, use_global_device_ids=true, to_apply=%region_3.4 | all-reduce | flops 384 | bytes 3072 | tf_op jit(solution)/shard_map/psum | solution.py:51
  126.2 1.9 %multiply_bitcast_fusion = f32[4,4,48,128]{3,2,0,1:T(8,128)} fusion(f32[4,48,4,128]{3,1,0,2:T(8,128)} %bitcast.51, f32[4,48]{1,0:T(4,128)S(1)} %fusion.13, pred[4,48]{1,0:T(4,128)(4,1)S(1)} %broadcast_in_dim.31), kind=kLoop, calls=%fused_computation.12 | loop fusion | flops 196608 | bytes 787392 | tf_op jit(solution)/shard_map/transpose | solution.py:88
  128.1 1.1 reshape.80
  129.2 1.0 copy.60
  (4 shorter events, 0.0 us)
Async XLA Ops:
  0.6 29.3 %copy-start = (f32[1,3,512,512]{3,2,1,0:T(8,128)S(1)}, f32[1,3,512,512]{3,2,1,0:T(8,128)}, u32[]{:S(2)}) copy-start(f32[1,3,512,512]{3,2,1,0:T(8,128)} %param.16) | copy-start | bytes 9437188
  0.6 17.7 %copy-start.1 = (bf16[4,4,6144]{2,1,0:T(4,128)(2,1)S(1)}, bf16[4,4,6144]{2,1,0:T(4,128)(2,1)}, u32[]{:S(2)}) copy-start(bf16[4,4,6144]{2,1,0:T(4,128)(2,1)} %param.11) | copy-start | bytes 589828
  5.1 23.8 %all-to-all-start = ((bf16[3,128,4,128]{3,2,0,1:T(4,128)(2,1)}), bf16[3,128,4,128]{3,2,0,1:T(4,128)(2,1)}, u32[]{:S(2)}, u32[]{:S(2)}) async-start(bf16[3,128,4,128]{3,2,0,1:T(4,128)(2,1)} %copy.52), calls=%async_computation | async-start | bytes 786432 | tf_op jit(solution)/shard_map/all_to_all | solution.py:57
  34.3 21.7 %all-to-all-start.1 = ((f32[3,128,4,128]{3,2,0,1:T(4,128)}), f32[3,128,4,128]{3,2,0,1:T(4,128)}, u32[]{:S(2)}, u32[]{:S(2)}) async-start(f32[3,128,4,128]{3,2,0,1:T(4,128)} %copy.56), calls=%async_computation.1 | async-start | bytes 1572864 | tf_op jit(solution)/shard_map/all_to_all | solution.py:78
where the time goes:
time: 131 us; the launch traced here: 130 us
  blocking collectives  63.1 us (48%)
  starting transfers between devices  17.5 us (13%)
  waiting for transfers between devices  16.2 us (12%)
  local copies, waits for them, and re-layouts  11.8 us (9%)
  other arithmetic  11.1 us (8%)
  matrix products  9.73 us (7%)
    psum x1, blocking collectives, per_device(): adam_sums = lax.psum(adam_part, ('shard', 'tensor'))  63.1 us
    all_to_all x1, starting transfers between devices, per_device(): lax.all_to_all(outgoing, ('shard', 'tensor'), split_axis=1, concat_axis=1...  11.9 us
    all_to_all x1, waiting for transfers between devices, per_device(): lax.all_to_all(shaped, ('shard', 'tensor'), split_axis=1, concat_axis=1,...  8.95 us
    all_to_all x1, waiting for transfers between devices, per_device(): lax.all_to_all(outgoing, ('shard', 'tensor'), split_axis=1, concat_axis=1...  7.29 us
    all_to_all x1, starting transfers between devices, per_device(): lax.all_to_all(shaped, ('shard', 'tensor'), split_axis=1, concat_axis=1,...  5.61 us
    reduce_sum x2, other arithmetic, per_device(): jnp.sum(jnp.square(direction).reshape(layer_count, row_count, block_count...  4.15 us
    dot_general x1, matrix products, per_device(): jnp.einsum('cib,cjb->cij', block_grads, block_grads, preferred_element_ty...  4.12 us
    gather x2, local copies, waits for them, and re-layouts, per_device(): jnp.take(returned, target, axis=0)  2.79 us
  transfers between devices with their start and end apart: 2, of which 2 were waited for; matrix products, arithmetic and copies ran while one was open for 9% of the time, Pallas kernels for 0%

commit v1 on v0

--- a/solution.py
+++ b/solution.py
@@ -48,16 +48,32 @@
     adam_part = jnp.sum(
         jnp.square(direction).reshape(layer_count, row_count, block_count, BLOCK), axis=(1, 3)
     )
-    adam_sums = lax.psum(adam_part, ("shard", "tensor"))
+    part_by_place = jnp.zeros((slot_count * devices,), jnp.float32).at[target].set(
+        adam_part.reshape(total_blocks)
+    )
+    part_hi = part_by_place.astype(jnp.bfloat16)
+    part_lo = (part_by_place - part_hi.astype(jnp.float32)).astype(jnp.bfloat16)
+    lane = jnp.arange(BLOCK, dtype=jnp.int32)
+    extra = jnp.where(
+        lane[None, :] == 0,
+        part_hi[:, None],
+        jnp.where(lane[None, :] == 1, part_lo[:, None], jnp.zeros((), jnp.bfloat16)),
+    )[:, None, :]
     pieces = gradients.reshape(layer_count, row_count, block_count, BLOCK)
     outgoing = jnp.einsum(
         "qln,lrnb->qrb", picker, pieces, preferred_element_type=jnp.float32
     ).astype(jnp.bfloat16)
-    outgoing = outgoing.reshape(slot_count, devices, row_count, BLOCK)
+    outgoing = jnp.concatenate([outgoing, extra], axis=1)
+    outgoing = outgoing.reshape(slot_count, devices, row_count + 1, BLOCK)
     incoming = lax.all_to_all(
         outgoing, ("shard", "tensor"), split_axis=1, concat_axis=1, tiled=True
     )
-    block_grads = incoming.reshape(slot_count, devices * row_count, BLOCK)
+    block_grads = incoming[:, :, :row_count, :].reshape(slot_count, devices * row_count, BLOCK)
+    adam_sums = jnp.sum(
+        incoming[:, :, row_count, 0].astype(jnp.float32)
+        + incoming[:, :, row_count, 1].astype(jnp.float32),
+        axis=1,
+    )
     left_out = (
         stat_left
         + jnp.einsum("cib,cjb->cij", block_grads, block_grads, preferred_element_type=jnp.float32)[
@@ -74,20 +90,16 @@
         "cij,cjb->cib", root_left[0], block_grads.astype(jnp.float32), precision=PRECISE
     )
     precond = jnp.einsum("cib,cbd->cid", left_applied, root_right[0], precision=PRECISE)
-    shaped = precond.reshape(slot_count, devices, row_count, BLOCK)
+    precond_sums = jnp.sum(jnp.square(precond), axis=(1, 2))
+    graft_ratio = jnp.sqrt(adam_sums / (precond_sums + 1e-06))
+    scaled = precond * graft_ratio[:, None, None]
+    shaped = scaled.reshape(slot_count, devices, row_count, BLOCK)
     returned = lax.all_to_all(shaped, ("shard", "tensor"), split_axis=1, concat_axis=1, tiled=True)
     returned = returned.reshape(slot_count * devices, row_count, BLOCK)
     own_rows = jnp.take(returned, target, axis=0).reshape(
         layer_count, block_count, row_count, BLOCK
     )
-    precond_part = jnp.sum(jnp.square(own_rows), axis=(2, 3))
-    precond_sums = lax.psum(precond_part, ("shard", "tensor"))
-    graft_ratio = jnp.sqrt(adam_sums / (precond_sums + 1e-06))
-    updates = (
-        (own_rows * graft_ratio[:, :, None, None])
-        .transpose(0, 2, 1, 3)
-        .reshape(layer_count, row_count, col_count)
-    )
+    updates = own_rows.transpose(0, 2, 1, 3).reshape(layer_count, row_count, col_count)
     small_mean_out, small_square_out, small_update = adam_moments(
         small_grad, small_mean, small_square
     )

time: 131 us -> 69.4 us (0.53)
  blocking collectives: 63.1 us -> 26.2 us
  starting transfers between devices: 17.5 us -> 5.7 us
  waiting for transfers between devices: 16.2 us -> 8.53 us
  other arithmetic: 11.1 us -> 7.96 us
    psum x1 -> x0, blocking collectives: 63.1 us -> none  [per_device(): adam_sums = lax.psum(adam_part, ('shard', 'tensor'))]
    all_to_all x0 -> x1, blocking collectives: none -> 26.2 us  [per_device(): lax.all_to_all(outgoing, ('shard', 'tensor'), split_axis=1, concat_axis=1...]
    all_to_all x1 -> x0, starting transfers between devices: 11.9 us -> none  [per_device(): lax.all_to_all(outgoing, ('shard', 'tensor'), split_axis=1, concat_axis=1...]
    all_to_all x1 -> x0, waiting for transfers between devices: 7.29 us -> none  [per_device(): lax.all_to_all(outgoing, ('shard', 'tensor'), split_axis=1, concat_axis=1...]
    reduce_sum x1, other arithmetic: 2.02 us -> 0.32 us  [per_device(): jnp.sum(incoming[:, :, row_count, 0].astype(jnp.float32) + incoming[:, :,...]
    reduce_sum x2, other arithmetic: 4.15 us -> 2.72 us  [per_device(): jnp.sum(jnp.square(direction).reshape(layer_count, row_count, block_count...]
  transfers between devices with their start and end apart: 2 -> 1, of which waited for: 2 -> 1; matrix products, arithmetic and copies ran while one was open for 9% -> 11% of each run, Pallas kernels for 0% -> 0%
where the time goes in v1:
time: 69.4 us; the launch traced here: 68.9 us
  blocking collectives  26.2 us (38%)
  local copies, waits for them, and re-layouts  10.9 us (16%)
  matrix products  8.9 us (13%)
  waiting for transfers between devices  8.53 us (12%)
  other arithmetic  7.96 us (11%)
  starting transfers between devices  5.7 us (8%)
  between operations  0.79 us (1%)
    all_to_all x1, blocking collectives, per_device(): lax.all_to_all(outgoing, ('shard', 'tensor'), split_axis=1, concat_axis=1...  26.2 us
    all_to_all x1, waiting for transfers between devices, per_device(): lax.all_to_all(shaped, ('shard', 'tensor'), split_axis=1, concat_axis=1,...  8.53 us
    all_to_all x1, starting transfers between devices, per_device(): lax.all_to_all(shaped, ('shard', 'tensor'), split_axis=1, concat_axis=1,...  5.7 us
    dot_general x1, matrix products, per_device(): jnp.einsum('cib,cjb->cij', block_grads, block_grads, preferred_element_ty...  4.13 us
    reduce_sum x2, other arithmetic, per_device(): jnp.sum(jnp.square(direction).reshape(layer_count, row_count, block_count...  2.72 us
    all_to_all x1, local copies, waits for them, and re-layouts, per_device(): lax.all_to_all(shaped, ('shard', 'tensor'), split_axis=1, concat_axis=1,...  2.17 us
    gather x2, local copies, waits for them, and re-layouts, per_device(): jnp.take(returned, target, axis=0)  2.05 us
    dot_general x1, matrix products, per_device(): jnp.einsum('cib,cid->cbd', block_grads, block_grads, preferred_element_ty...  1.92 us
  transfers between devices with their start and end apart: 1, of which 1 were waited for; matrix products, arithmetic and copies ran while one was open for 11% of the time, Pallas kernels for 0%

profile of v1, /device:TPU:1, one launch (start us, length us, event | category | flops | bytes accessed | tf_op | source)
XLA Modules:
  0.0 68.9 jit_solution(8222431398543022892)
XLA Ops:
  0.7 1.0 %convert_reduce_fusion = s32[192]{0:T(256)S(1)} fusion(s32[192]{0:T(256)} %param.18), kind=kLoop, calls=%fused_computation.23 | loop fusion | flops 184128 | bytes 1536 | tf_op jit(solution)/shard_map/reduce_sum | solution.py:38
  1.7 0.7 %compare_and_fusion = (pred[192]{0:T(512)(128)(4,1)S(1)}, s32[192]{0:T(256)S(1)}) fusion(s32[192]{0:T(256)} %param.18, s32[192]{0:T(256)S(1)} %convert_reduce_fusion), kind=kLoop, calls=%fused_computation.36 | loop fusion | flops 1536 | bytes 2496 | tf_op jit(solution)/shard_map/jit(_take)/and | solution.py:99
  2.4 0.1 eq.70
  2.5 1.1 %reshape.132 = bf16[4,4,48,128]{3,2,1,0:T(8,128)(2,1)S(1)} reshape(bf16[4,4,6144]{2,1,0:T(4,128)(2,1)} %param.11) | data formatting | bytes 393216 | tf_op jit(solution)/shard_map/reshape | solution.py:62
  3.5 2.6 %multiply_reduce_fusion.1 = (f32[4,6144]{1,0:T(4,128)S(1)}, f32[4,4,6144]{2,1,0:T(4,128)}, f32[4,4,6144]{2,1,0:T(4,128)}) fusion(bf16[4,4,6144]{2,1,0:T(4,128)(2,1)} %param.11, f32[4,4,6144]{2,1,0:T(4,128)} %param.13, f32[4,4,6144]{2,1,0:T(4,128)} %param.12), kind=kLoop, calls=%fused_computation.17 | loop fusion | flops 1155072 | bytes 1867776 | tf_op jit(solution)/shard_map/reduce_sum | solution.py:48
  6.2 0.1 bitcast_reduce_fusion
  6.3 1.2 %scatter_custom_fusion = f32[384]{0:T(512)S(1)} fusion(s32[192]{0:T(256)S(1)} %compare_select_fusion, f32[192]{0:T(256)S(1)} %reshape.150, f32[]{:T(128)} %constant.18.clone.1), kind=kCustom, calls=%fused_computation.38 | custom fusion | bytes 1540 | tf_op jit(solution)/shard_map/scatter | solution.py:51
  7.6 0.1 copy.65
  7.7 0.1 copy.64
  7.8 0.4 fusion.2
  8.2 0.3 copy.66
  8.6 0.3 select_select_fusion
  8.9 0.4 pad_maximum_fusion
  9.4 26.2 %all_to_all.10 = bf16[3,128,5,128]{3,0,2,1:T(4,128)(2,1)S(1)} all-to-all(bf16[3,128,5,128]{3,0,2,1:T(4,128)(2,1)S(1)} %pad_maximum_fusion), channel_id=1, replica_groups=mesh['shard'=16,'tensor'=8] {'shard','tensor'}, dimensions={1} | all-to-all | bytes 983040 | tf_op jit(solution)/shard_map/all_to_all | solution.py:68
  35.5 0.2 slice.14
  35.7 0.2 copy.67
  35.9 1.6 %fusion = f32[3,128,512]{1,2,0:T(8,128)S(1)} fusion(bf16[3,512,128]{2,1,0:T(8,128)(2,1)S(1)} %bitcast.52, f32[1,3,512,512]{3,2,1,0:T(8,128)S(1)} %copy-done), kind=kOutput, calls=%fused_computation.3 | convolution fusion | flops 1207959552 | bytes 4325376 | tf_op jit(solution)/shard_map/cij,cjb->cib/dot_general | solution.py:89
  37.5 0.9 %multiply_reduce_fusion = (f32[3]{0:T(128)S(1)}, f32[3,512,128]{2,1,0:T(8,128)S(1)}) fusion(f32[3,128,512]{1,2,0:T(8,128)S(1)} %fusion, f32[1,3,128,128]{3,2,1,0:T(8,128)S(1)} %copy-done.1), kind=kOutput, calls=%fused_computation.9 | convolution fusion | flops 302383104 | bytes 1769484 | tf_op jit(solution)/shard_map/cib,cbd->cid/dot_general | solution.py:92
  38.4 0.3 add_reduce_fusion
  38.7 0.1 broadcast_multiply_fusion
  38.9 1.0 %copy.70 = f32[3,128,4,128]{3,2,0,1:T(4,128)} copy(f32[3,128,4,128]{3,2,1,0:T(4,128)S(1)} %bitcast.55) | data formatting | bytes 1572864 | tf_op jit(solution)/shard_map/reshape | solution.py:96
  39.9 5.7 %all-to-all-start.1 = ((f32[3,128,4,128]{3,2,0,1:T(4,128)}), f32[3,128,4,128]{3,2,0,1:T(4,128)}, u32[]{:S(2)}, u32[]{:S(2)}) async-start(f32[3,128,4,128]{3,2,0,1:T(4,128)} %copy.70), calls=%async_computation.1 | async-start | bytes 1572864 | tf_op jit(solution)/shard_map/all_to_all | solution.py:97
  45.6 1.4 %add_divide_fusion = (f32[6336]{0:T(1024)}, f32[6336]{0:T(1024)}, f32[6336]{0:T(1024)}) fusion(f32[6336]{0:T(1024)} %param.19, f32[6336]{0:T(1024)} %param.21, f32[6336]{0:T(1024)} %param.20), kind=kLoop, calls=%fused_computation.31 | loop fusion | flops 57024 | bytes 152064 | tf_op jit(solution)/shard_map/div | solution.py:15
  47.0 0.1 broadcast_in_dim.76
  47.1 1.9 %fusion.3 = f32[1,3,128,128]{3,2,1,0:T(8,128)} fusion(f32[1,3,128,128]{3,2,1,0:T(8,128)} %param.15, bf16[3,512,128]{2,1,0:T(8,128)(2,1)S(1)} %bitcast.53), kind=kOutput, calls=%fused_computation.8 | convolution fusion | flops 50380800 | bytes 786432 | tf_op jit(solution)/shard_map/cib,cid->cbd/dot_general | solution.py:85
  49.0 4.1 %bitcast_add_fusion = f32[1,3,512,512]{3,2,1,0:T(8,128)} fusion(f32[1,3,512,512]{3,2,1,0:T(8,128)} %param.14, bf16[3,512,128]{2,1,0:T(8,128)(2,1)S(1)} %bitcast.54), kind=kOutput, calls=%fused_computation.2 | convolution fusion | flops 202113024 | bytes 6684672 | tf_op jit(solution)/shard_map/cib,cjb->cij/dot_general | solution.py:79
  53.2 8.5 %all-to-all-done.1 = f32[3,128,4,128]{3,2,0,1:T(4,128)} async-done(((f32[3,128,4,128]{3,2,0,1:T(4,128)}), f32[3,128,4,128]{3,2,0,1:T(4,128)}, u32[]{:S(2)}, u32[]{:S(2)}) %all-to-all-start.1) | async-done | bytes 786464 | tf_op jit(solution)/shard_map/all_to_all | solution.py:97
  61.7 2.2 %copy.71 = f32[3,128,4,128]{3,2,1,0:T(4,128)} copy(f32[3,128,4,128]{3,2,0,1:T(4,128)} %all-to-all-done.1) | data formatting | bytes 1572864 | tf_op jit(solution)/shard_map/all_to_all | solution.py:97
  63.9 2.0 %gather_fusion = f32[192,4,128]{2,1,0:T(4,128)S(1)} fusion(f32[384,4,128]{2,1,0:T(4,128)} %bitcast.56, s32[1024]{0:T(1024)S(1)} %pad_clamp_fusion), kind=kCustom, calls=%fused_computation | custom fusion | bytes 787200 | tf_op jit(solution)/shard_map/jit(_take)/gather | solution.py:99
  65.9 0.8 %select_bitcast_fusion = f32[4,4,48,128]{3,2,0,1:T(8,128)} fusion(f32[4,48,4,128]{3,1,0,2:T(8,128)S(1)} %bitcast.57, pred[4,48]{1,0:T(4,128)(4,1)S(1)} %broadcast_in_dim.76), kind=kLoop, calls=%fused_computation.15 | loop fusion | flops 98304 | bytes 786624 | tf_op jit(solution)/shard_map/transpose | solution.py:102
  66.8 1.1 %reshape.137 = f32[4,4,6144]{2,0,1:T(4,128)S(1)} reshape(f32[4,4,48,128]{3,2,0,1:T(8,128)} %select_bitcast_fusion) | data formatting | bytes 786432 | tf_op jit(solution)/shard_map/reshape | solution.py:102
  67.9 1.0 %copy.74 = f32[4,4,6144]{2,1,0:T(4,128)} copy(f32[4,4,6144]{2,0,1:T(4,128)S(1)} %reshape.137) | data formatting | bytes 786432
  (11 shorter events, 0.2 us)
Async XLA Ops:
  0.6 35.3 %copy-start = (f32[1,3,512,512]{3,2,1,0:T(8,128)S(1)}, f32[1,3,512,512]{3,2,1,0:T(8,128)}, u32[]{:S(2)}) copy-start(f32[1,3,512,512]{3,2,1,0:T(8,128)} %param.16) | copy-start | bytes 9437188
  35.5 2.0 %copy-start.1 = (f32[1,3,128,128]{3,2,1,0:T(8,128)S(1)}, f32[1,3,128,128]{3,2,1,0:T(8,128)}, u32[]{:S(2)}) copy-start(f32[1,3,128,128]{3,2,1,0:T(8,128)} %param.17) | copy-start | bytes 589828
  39.9 21.8 %all-to-all-start.1 = ((f32[3,128,4,128]{3,2,0,1:T(4,128)}), f32[3,128,4,128]{3,2,0,1:T(4,128)}, u32[]{:S(2)}, u32[]{:S(2)}) async-start(f32[3,128,4,128]{3,2,0,1:T(4,128)} %copy.70), calls=%async_computation.1 | async-start | bytes 1572864 | tf_op jit(solution)/shard_map/all_to_all | solution.py:97

commit v2 on v1

--- a/solution.py
+++ b/solution.py
@@ -1,9 +1,14 @@
+import functools
+
 import jax
 import jax.numpy as jnp
 from jax import lax
+from jax.experimental import pallas as pl
+from jax.experimental.pallas import tpu as pltpu
 from jax.sharding import PartitionSpec as P
 
 BLOCK = 128
+MESH = pl.DeviceIdType.MESH
 
 
 PRECISE = lax.Precision.HIGHEST
@@ -13,6 +18,60 @@
     mean_new = 0.9 * mean_old + 0.1 * grad_wide
     square_new = 0.95 * square_old + 0.05 * grad_wide * grad_wide
     return (mean_new, square_new, mean_new / (jnp.sqrt(square_new) + 1e-08))
+
+
+def _a2a_kernel(n, width, x_ref, y_ref, send_sem, recv_sem):
+    me = lax.axis_index("shard") * width + lax.axis_index("tensor")
+
+    def where(d):
+        return (lax.div(d, width), lax.rem(d, width))
+
+    barrier = pltpu.get_barrier_semaphore()
+
+    def greet(j, c):
+        pl.semaphore_signal(
+            barrier, inc=1, device_id=where(lax.rem(me + j, n)), device_id_type=MESH
+        )
+        return c
+
+    lax.fori_loop(1, n, greet, 0)
+    pl.semaphore_wait(barrier, n - 1)
+
+    def send(j, c):
+        d = lax.rem(me + j, n)
+        pltpu.make_async_remote_copy(
+            src_ref=x_ref.at[pl.ds(d, 1)],
+            dst_ref=y_ref.at[pl.ds(me, 1)],
+            send_sem=send_sem,
+            recv_sem=recv_sem,
+            device_id=where(d),
+            device_id_type=MESH,
+        ).start()
+        return c
+
+    lax.fori_loop(1, n, send, 0)
+    y_ref[pl.ds(me, 1)] = x_ref[pl.ds(me, 1)]
+    every = pltpu.make_async_remote_copy(
+        src_ref=x_ref.at[pl.ds(0, n - 1)],
+        dst_ref=y_ref.at[pl.ds(0, n - 1)],
+        send_sem=send_sem,
+        recv_sem=recv_sem,
+        device_id=where(lax.rem(me + 1, n)),
+        device_id_type=MESH,
+    )
+    every.wait_send()
+    every.wait_recv()
+
+
+def exchange(x, n, width, cid):
+    return pl.pallas_call(
+        functools.partial(_a2a_kernel, n, width),
+        out_shape=jax.ShapeDtypeStruct(x.shape, x.dtype),
+        in_specs=[pl.BlockSpec(memory_space=pltpu.VMEM)],
+        out_specs=pl.BlockSpec(memory_space=pltpu.VMEM),
+        scratch_shapes=[pltpu.SemaphoreType.DMA, pltpu.SemaphoreType.DMA],
+        compiler_params=pltpu.CompilerParams(collective_id=cid, has_side_effects=True),
+    )(x)
 
 
 def per_device(
@@ -31,48 +90,58 @@
     layer_count, row_count, col_count = gradients.shape
     block_count = col_count // BLOCK
     devices = lax.axis_size(("shard", "tensor"))
+    width = lax.axis_size("tensor")
     slot_count = stat_left.shape[1]
     total_blocks = owners.shape[0]
     positions = jnp.arange(total_blocks, dtype=jnp.int32)
     earlier = (owners[:, None] == owners[None, :]) & (positions[None, :] < positions[:, None])
     slot_index = jnp.sum(earlier.astype(jnp.int32), axis=1)
-    target = slot_index * devices + owners
-    places = jnp.arange(slot_count * devices, dtype=jnp.int32)
+    target = owners * slot_count + slot_index
+    places = jnp.arange(devices * slot_count, dtype=jnp.int32)
     picker = (
         (places[:, None] == target[None, :])
         .astype(jnp.bfloat16)
-        .reshape(slot_count * devices, layer_count, block_count)
+        .reshape(devices * slot_count, layer_count, block_count)
     )
     grad_wide = gradients.astype(jnp.float32)
     mean_out, square_out, direction = adam_moments(grad_wide, adam_mean, adam_square)
     adam_part = jnp.sum(
         jnp.square(direction).reshape(layer_count, row_count, block_count, BLOCK), axis=(1, 3)
     )
-    part_by_place = jnp.zeros((slot_count * devices,), jnp.float32).at[target].set(
-        adam_part.reshape(total_blocks)
+    part_by_place = (
+        jnp.zeros((devices * slot_count,), jnp.float32)
+        .at[target]
+        .set(adam_part.reshape(total_blocks))
+        .reshape(devices, slot_count)
     )
     part_hi = part_by_place.astype(jnp.bfloat16)
     part_lo = (part_by_place - part_hi.astype(jnp.float32)).astype(jnp.bfloat16)
-    lane = jnp.arange(BLOCK, dtype=jnp.int32)
-    extra = jnp.where(
-        lane[None, :] == 0,
-        part_hi[:, None],
-        jnp.where(lane[None, :] == 1, part_lo[:, None], jnp.zeros((), jnp.bfloat16)),
-    )[:, None, :]
+    extra_rows = 16 - slot_count * row_count
+    pad = ((0, 0), (0, BLOCK - slot_count))
+    extra = jnp.stack(
+        [jnp.pad(part_hi, pad), jnp.pad(part_lo, pad)]
+        + [jnp.zeros((devices, BLOCK), jnp.bfloat16)] * (extra_rows - 2),
+        axis=1,
+    )
     pieces = gradients.reshape(layer_count, row_count, block_count, BLOCK)
     outgoing = jnp.einsum(
         "qln,lrnb->qrb", picker, pieces, preferred_element_type=jnp.float32
     ).astype(jnp.bfloat16)
-    outgoing = jnp.concatenate([outgoing, extra], axis=1)
-    outgoing = outgoing.reshape(slot_count, devices, row_count + 1, BLOCK)
-    incoming = lax.all_to_all(
-        outgoing, ("shard", "tensor"), split_axis=1, concat_axis=1, tiled=True
-    )
-    block_grads = incoming[:, :, :row_count, :].reshape(slot_count, devices * row_count, BLOCK)
+    outgoing = jnp.concatenate(
+        [outgoing.reshape(devices, slot_count * row_count, BLOCK), extra], axis=1
+    )
+    incoming = exchange(outgoing, devices, width, 0)
+    block_grads = (
+        incoming[:, : slot_count * row_count]
+        .reshape(devices, slot_count, row_count, BLOCK)
+        .transpose(1, 0, 2, 3)
+        .reshape(slot_count, devices * row_count, BLOCK)
+    )
+    tail = slot_count * row_count
     adam_sums = jnp.sum(
-        incoming[:, :, row_count, 0].astype(jnp.float32)
-        + incoming[:, :, row_count, 1].astype(jnp.float32),
-        axis=1,
+        incoming[:, tail, :slot_count].astype(jnp.float32)
+        + incoming[:, tail + 1, :slot_count].astype(jnp.float32),
+        axis=0,
     )
     left_out = (
         stat_left
@@ -93,9 +162,13 @@
     precond_sums = jnp.sum(jnp.square(precond), axis=(1, 2))
     graft_ratio = jnp.sqrt(adam_sums / (precond_sums + 1e-06))
     scaled = precond * graft_ratio[:, None, None]
-    shaped = scaled.reshape(slot_count, devices, row_count, BLOCK)
-    returned = lax.all_to_all(shaped, ("shard", "tensor"), split_axis=1, concat_axis=1, tiled=True)
-    returned = returned.reshape(slot_count * devices, row_count, BLOCK)
+    shaped = (
+        scaled.reshape(slot_count, devices, row_count, BLOCK)
+        .transpose(1, 0, 2, 3)
+        .reshape(devices, slot_count * row_count, BLOCK)
+    )
+    returned = exchange(shaped, devices, width, 1)
+    returned = returned.reshape(devices * slot_count, row_count, BLOCK)
     own_rows = jnp.take(returned, target, axis=0).reshape(
         layer_count, block_count, row_count, BLOCK
     )

time: 69.4 us -> 76 us (1.095)
  Pallas kernels: 0 us -> 42.5 us
  blocking collectives: 26.2 us -> 0 us
  waiting for transfers between devices: 8.53 us -> 0 us
  starting transfers between devices: 5.7 us -> 0 us
  other arithmetic: 7.96 us -> 10.8 us
  local copies, waits for them, and re-layouts: 10.9 us -> 13.5 us
  matrix products: 8.9 us -> 8.01 us
    pallas_call x0 -> x2, Pallas kernels: none -> 42.5 us  [exchange(): pl.pallas_call(functools.partial(_a2a_kernel, n, width), out_shape=jax.Sh...]
    all_to_all x1 -> x0, blocking collectives: 26.2 us -> none  [per_device(): lax.all_to_all(outgoing, ('shard', 'tensor'), split_axis=1, concat_axis=1...]
    all_to_all x1 -> x0, waiting for transfers between devices: 8.53 us -> none  [per_device(): lax.all_to_all(shaped, ('shard', 'tensor'), split_axis=1, concat_axis=1,...]
    all_to_all x1 -> x0, starting transfers between devices: 5.7 us -> none  [per_device(): lax.all_to_all(shaped, ('shard', 'tensor'), split_axis=1, concat_axis=1,...]
    reshape x2 -> x5, local copies, waits for them, and re-layouts: 2.18 us -> 4.94 us  [the longest x1 2.34 us: per_device(): returned = returned.reshape(devices * slot_count, row_count, BLOCK)]
    all_to_all x1 -> x0, local copies, waits for them, and re-layouts: 2.17 us -> none  [per_device(): lax.all_to_all(shaped, ('shard', 'tensor'), split_axis=1, concat_axis=1,...]
    reshape x0 -> x1, other arithmetic: none -> 2.01 us  [per_device(): own_rows.transpose(0, 2, 1, 3).reshape(layer_count, row_count, col_count)]
    concatenate x1, other arithmetic: 0.44 us -> 2.37 us  [per_device(): jnp.concatenate([outgoing.reshape(devices, slot_count * row_count, BLOCK)...]
  transfers between devices with their start and end apart: 1 -> 0, of which waited for: 1 -> 0; matrix products, arithmetic and copies ran while one was open for 11% -> 0% of each run, Pallas kernels for 0% -> 0%
where the time goes in v2:
time: 76 us; the launch traced here: 75.6 us
  Pallas kernels  42.5 us (56%)
  local copies, waits for them, and re-layouts  13.5 us (18%)
  other arithmetic  10.8 us (14%)
  matrix products  8.01 us (11%)
  between operations  0.79 us (1%)
    pallas_call x2, Pallas kernels, exchange(): pl.pallas_call(functools.partial(_a2a_kernel, n, width), out_shape=jax.Sh...  42.5 us
    dot_general x1, matrix products, per_device(): jnp.einsum('cib,cjb->cij', block_grads, block_grads, preferred_element_ty...  4.17 us
    gather x1, local copies, waits for them, and re-layouts, per_device(): jnp.take(returned, target, axis=0)  2.75 us
    reduce_sum x2, other arithmetic, per_device(): jnp.sum(jnp.square(direction).reshape(layer_count, row_count, block_count...  2.72 us
    concatenate x1, other arithmetic, per_device(): jnp.concatenate([outgoing.reshape(devices, slot_count * row_count, BLOCK)...  2.37 us
    reshape x1, local copies, waits for them, and re-layouts, per_device(): returned = returned.reshape(devices * slot_count, row_count, BLOCK)  2.34 us
    reshape x1, other arithmetic, per_device(): own_rows.transpose(0, 2, 1, 3).reshape(layer_count, row_count, col_count)  2.01 us
    dot_general x1, matrix products, per_device(): jnp.einsum('cij,cjb->cib', root_left[0], block_grads.astype(jnp.float32),...  1.57 us

profile of v2, /device:TPU:1, one launch (start us, length us, event | category | flops | bytes accessed | tf_op | source)
XLA Modules:
  0.0 75.6 jit_solution(15831100945434971436)
XLA Ops:
  0.6 1.0 %convert_reduce_fusion = s32[192]{0:T(256)S(1)} fusion(s32[192]{0:T(256)} %param.18), kind=kLoop, calls=%fused_computation.22 | loop fusion | flops 184128 | bytes 1536 | tf_op jit(solution)/shard_map/reduce_sum | solution.py:98
  1.7 0.7 compare_and_fusion
  2.4 2.6 %multiply_reduce_fusion.1 = (f32[4,6144]{1,0:T(4,128)S(1)}, f32[4,4,6144]{2,1,0:T(4,128)}, f32[4,4,6144]{2,1,0:T(4,128)}) fusion(bf16[4,4,6144]{2,1,0:T(4,128)(2,1)} %param.11, f32[4,4,6144]{2,1,0:T(4,128)} %param.13, f32[4,4,6144]{2,1,0:T(4,128)} %param.12), kind=kLoop, calls=%fused_computation.17 | loop fusion | flops 1155072 | bytes 1867776 | tf_op jit(solution)/shard_map/reduce_sum | solution.py:108
  5.0 0.1 bitcast_reduce_fusion
  5.1 0.1 reshape.115
  5.2 1.2 %scatter_custom_fusion = f32[384]{0:T(512)S(1)} fusion(s32[192]{0:T(256)S(1)} %compare_select_fusion, f32[192]{0:T(256)S(1)} %reshape.115, f32[]{:T(128)} %constant.17.clone.1), kind=kCustom, calls=%fused_computation.38 | custom fusion | bytes 1540 | tf_op jit(solution)/shard_map/scatter | solution.py:114
  6.4 0.2 reshape.96
  6.6 0.7 copy.63
  7.3 0.7 copy.62
  8.0 1.1 %reshape.93 = bf16[4,4,48,128]{3,2,1,0:T(8,128)(2,1)S(1)} reshape(bf16[4,4,6144]{2,1,0:T(4,128)(2,1)} %param.11) | data formatting | bytes 393216 | tf_op jit(solution)/shard_map/reshape | solution.py:126
  9.1 0.1 eq.48
  9.1 0.4 fusion.2
  9.5 0.3 copy.61
  9.9 0.9 %reshape.94 = bf16[128,12,128]{2,1,0:T(8,128)(2,1)} reshape(bf16[384,4,128]{2,1,0:T(4,128)(2,1)S(1)} %copy.61) | data formatting | bytes 786432 | tf_op jit(solution)/shard_map/reshape | solution.py:131
  10.7 0.1 pad.12.clone
  10.8 2.4 %maximum_maximum_fusion.x_ref = bf16[128,16,128]{2,1,0:T(8,128)(2,1)} fusion(bf16[128,1,128]{2,1,0:T(2,128)(2,1)} %copy.63, bf16[128,1,128]{2,1,0:T(2,128)(2,1)} %copy.62, bf16[128,12,128]{2,1,0:T(8,128)(2,1)} %reshape.94, bf16[16]{0:T(256)(128)(2,1)S(1)} %pad.12.clone), kind=kLoop, calls=%fused_computation.11 | loop fusion | flops 2097152 | bytes 983072 | tf_op jit(solution)/shard_map/concatenate | solution.py:130
  13.2 21.9 %shard_map.170 = bf16[128,16,128]{2,1,0:T(8,128)(2,1)} custom-call(bf16[128,16,128]{2,1,0:T(8,128)(2,1)} %maximum_maximum_fusion.x_ref), custom_call_target="tpu_custom_call" | custom-call | tf_op jit(solution)/shard_map/pallas_call | solution.py:67
  35.1 1.2 %copy.64 = bf16[128,12,128]{2,0,1:T(8,128)(2,1)S(1)} copy(bf16[128,12,128]{2,1,0:T(8,128)(2,1)} %bitcast.60) | data formatting | bytes 786432 | tf_op jit(solution)/shard_map/slice | solution.py:135
  36.3 0.3 copy.65
  36.6 1.6 %fusion = f32[3,128,512]{1,2,0:T(8,128)S(1)} fusion(bf16[3,512,128]{2,1,0:T(8,128)(2,1)S(1)} %bitcast.55, f32[1,3,512,512]{3,2,1,0:T(8,128)S(1)} %copy-done), kind=kOutput, calls=%fused_computation.3 | convolution fusion | flops 1207959552 | bytes 4325376 | tf_op jit(solution)/shard_map/cij,cjb->cib/dot_general | solution.py:158
  38.2 0.9 %multiply_reduce_fusion = (f32[3]{0:T(128)S(1)}, f32[3,512,128]{2,1,0:T(8,128)S(1)}) fusion(f32[3,128,512]{1,2,0:T(8,128)S(1)} %fusion, f32[1,3,128,128]{3,2,1,0:T(8,128)S(1)} %copy-done.2), kind=kOutput, calls=%fused_computation.9 | convolution fusion | flops 302383104 | bytes 1769484 | tf_op jit(solution)/shard_map/cib,cbd->cid/dot_general | solution.py:161
  39.1 1.2 %add_reduce_fusion = f32[3]{0:T(128)S(1)} fusion(bf16[128,16,128]{2,1,0:T(8,128)(2,1)} %shard_map.170), kind=kLoop, calls=%fused_computation.27 | loop fusion | flops 1533 | bytes 1548 | tf_op jit(solution)/shard_map/reduce_sum | solution.py:141
  40.3 0.1 broadcast_multiply_fusion
  40.5 1.4 %copy.69.x_ref = f32[128,12,128]{2,1,0:T(8,128)} copy(f32[128,12,128]{2,0,1:T(8,128)S(1)} %bitcast.58) | data formatting | bytes 1572864 | tf_op jit(solution)/shard_map/reshape | solution.py:168
  42.0 20.6 %shard_map.171 = f32[128,12,128]{2,1,0:T(8,128)} custom-call(f32[128,12,128]{2,1,0:T(8,128)} %copy.69.x_ref), custom_call_target="tpu_custom_call" | custom-call | tf_op jit(solution)/shard_map/pallas_call | solution.py:67
  62.6 2.3 %reshape.101 = f32[384,4,128]{2,1,0:T(4,128)} reshape(f32[128,12,128]{2,1,0:T(8,128)} %shard_map.171) | data formatting | bytes 1572864 | tf_op jit(solution)/shard_map/reshape | solution.py:171
  64.9 2.8 %gather_fusion = f32[192,4,128]{2,1,0:T(4,128)} fusion(f32[384,4,128]{2,1,0:T(4,128)} %reshape.101, s32[1024]{0:T(1024)S(1)} %pad_clamp_fusion), kind=kCustom, calls=%fused_computation | custom fusion | bytes 787200 | tf_op jit(solution)/shard_map/jit(_take)/gather | solution.py:172
  67.7 0.1 broadcast_in_dim.31
  67.8 2.0 %select_bitcast_fusion = f32[4,4,6144]{2,1,0:T(4,128)} fusion(f32[4,48,4,128]{3,2,1,0:T(4,128)} %bitcast.62, pred[4,48]{1,0:T(4,128)(4,1)S(1)} %broadcast_in_dim.31), kind=kLoop, calls=%fused_computation.15 | loop fusion | flops 98304 | bytes 786624 | tf_op jit(solution)/shard_map/reshape | solution.py:175
  69.8 4.2 %bitcast_add_fusion = f32[1,3,512,512]{3,2,1,0:T(8,128)} fusion(f32[1,3,512,512]{3,2,1,0:T(8,128)} %param.14, bf16[3,512,128]{2,1,0:T(8,128)(2,1)S(1)} %bitcast.56), kind=kOutput, calls=%fused_computation.2 | convolution fusion | flops 202113024 | bytes 6684672 | tf_op jit(solution)/shard_map/cib,cjb->cij/dot_general | solution.py:148
  74.0 1.0 %fusion.3 = f32[1,3,128,128]{3,2,1,0:T(8,128)} fusion(f32[1,3,128,128]{3,2,1,0:T(8,128)S(1)} %copy-done.1, bf16[3,512,128]{2,1,0:T(8,128)(2,1)S(1)} %bitcast.57), kind=kOutput, calls=%fused_computation.8 | convolution fusion | flops 50380800 | bytes 786432 | tf_op jit(solution)/shard_map/cib,cid->cbd/dot_general | solution.py:154
  75.0 0.6 add_divide_fusion
  (19 shorter events, 0.2 us)
Async XLA Ops:
  0.6 36.0 %copy-start = (f32[1,3,512,512]{3,2,1,0:T(8,128)S(1)}, f32[1,3,512,512]{3,2,1,0:T(8,128)}, u32[]{:S(2)}) copy-start(f32[1,3,512,512]{3,2,1,0:T(8,128)} %param.16) | copy-start | bytes 9437188
  35.1 3.1 %copy-start.2 = (f32[1,3,128,128]{3,2,1,0:T(8,128)S(1)}, f32[1,3,128,128]{3,2,1,0:T(8,128)}, u32[]{:S(2)}) copy-start(f32[1,3,128,128]{3,2,1,0:T(8,128)} %param.17) | copy-start | bytes 589828
  69.8 4.2 %copy-start.1 = (f32[1,3,128,128]{3,2,1,0:T(8,128)S(1)}, f32[1,3,128,128]{3,2,1,0:T(8,128)}, u32[]{:S(2)}) copy-start(f32[1,3,128,128]{3,2,1,0:T(8,128)} %param.15) | copy-start | bytes 589828
  69.8 5.2 %copy-start.3 = (f32[6336]{0:T(1024)S(1)}, f32[6336]{0:T(1024)}, u32[]{:S(2)}) copy-start(f32[6336]{0:T(1024)} %param.19) | copy-start | bytes 76036
  69.8 5.2 %copy-start.4 = (f32[6336]{0:T(1024)S(1)}, f32[6336]{0:T(1024)}, u32[]{:S(2)}) copy-start(f32[6336]{0:T(1024)} %param.21) | copy-start | bytes 76036
  69.8 5.2 %copy-start.5 = (f32[6336]{0:T(1024)S(1)}, f32[6336]{0:T(1024)}, u32[]{:S(2)}) copy-start(f32[6336]{0:T(1024)} %param.20) | copy-start | bytes 76036

commit v3 on v2

--- a/solution.py
+++ b/solution.py
@@ -20,58 +20,59 @@
     return (mean_new, square_new, mean_new / (jnp.sqrt(square_new) + 1e-08))
 
 
-def _a2a_kernel(n, width, x_ref, y_ref, send_sem, recv_sem):
-    me = lax.axis_index("shard") * width + lax.axis_index("tensor")
-
-    def where(d):
-        return (lax.div(d, width), lax.rem(d, width))
-
+def _a2a_kernel(S, W, x_ref, w_ref, z_ref, s1, r1, s2, r2, l1, l2):
+    s = lax.axis_index("shard")
+    t = lax.axis_index("tensor")
     barrier = pltpu.get_barrier_semaphore()
-
-    def greet(j, c):
-        pl.semaphore_signal(
-            barrier, inc=1, device_id=where(lax.rem(me + j, n)), device_id_type=MESH
-        )
-        return c
-
-    lax.fori_loop(1, n, greet, 0)
-    pl.semaphore_wait(barrier, n - 1)
-
-    def send(j, c):
-        d = lax.rem(me + j, n)
+    for j in range(1, W):
+        pl.semaphore_signal(barrier, inc=1, device_id=(s, lax.rem(t + j, W)), device_id_type=MESH)
+    for j in range(1, S):
+        pl.semaphore_signal(barrier, inc=1, device_id=(lax.rem(s + j, S), t), device_id_type=MESH)
+    pl.semaphore_wait(barrier, W - 1 + S - 1)
+    for j in range(1, W):
+        tp = lax.rem(t + j, W)
         pltpu.make_async_remote_copy(
-            src_ref=x_ref.at[pl.ds(d, 1)],
-            dst_ref=y_ref.at[pl.ds(me, 1)],
-            send_sem=send_sem,
-            recv_sem=recv_sem,
-            device_id=where(d),
-            device_id_type=MESH,
+            src_ref=x_ref.at[tp], dst_ref=z_ref.at[t], send_sem=s1, recv_sem=r1,
+            device_id=(s, tp), device_id_type=MESH,
         ).start()
-        return c
-
-    lax.fori_loop(1, n, send, 0)
-    y_ref[pl.ds(me, 1)] = x_ref[pl.ds(me, 1)]
-    every = pltpu.make_async_remote_copy(
-        src_ref=x_ref.at[pl.ds(0, n - 1)],
-        dst_ref=y_ref.at[pl.ds(0, n - 1)],
-        send_sem=send_sem,
-        recv_sem=recv_sem,
-        device_id=where(lax.rem(me + 1, n)),
-        device_id_type=MESH,
-    )
-    every.wait_send()
-    every.wait_recv()
-
-
-def exchange(x, n, width, cid):
-    return pl.pallas_call(
-        functools.partial(_a2a_kernel, n, width),
-        out_shape=jax.ShapeDtypeStruct(x.shape, x.dtype),
+    near = pltpu.make_async_copy(x_ref.at[t], z_ref.at[t], l1)
+    near.start()
+    first = pltpu.make_async_remote_copy(
+        src_ref=x_ref.at[pl.ds(0, W - 1)], dst_ref=z_ref.at[pl.ds(0, W - 1)], send_sem=s1, recv_sem=r1,
+        device_id=(s, lax.rem(t + 1, W)), device_id_type=MESH,
+    )
+    near.wait()
+    first.wait_send()
+    first.wait_recv()
+    for j in range(1, S):
+        sp = lax.rem(s + j, S)
+        pltpu.make_async_remote_copy(
+            src_ref=z_ref.at[:, sp], dst_ref=w_ref.at[s], send_sem=s2, recv_sem=r2,
+            device_id=(sp, t), device_id_type=MESH,
+        ).start()
+    home = pltpu.make_async_copy(z_ref.at[:, s], w_ref.at[s], l2)
+    home.start()
+    second = pltpu.make_async_remote_copy(
+        src_ref=w_ref.at[pl.ds(0, S - 1)], dst_ref=w_ref.at[pl.ds(0, S - 1)], send_sem=s2, recv_sem=r2,
+        device_id=(lax.rem(s + 1, S), t), device_id_type=MESH,
+    )
+    home.wait()
+    second.wait_send()
+    second.wait_recv()
+
+
+def exchange(x, S, W, cid):
+    n, rows, lanes = x.shape
+    xt = x.reshape(S, W, rows, lanes).transpose(1, 0, 2, 3)
+    w = pl.pallas_call(
+        functools.partial(_a2a_kernel, S, W),
+        out_shape=jax.ShapeDtypeStruct((S, W, rows, lanes), x.dtype),
         in_specs=[pl.BlockSpec(memory_space=pltpu.VMEM)],
         out_specs=pl.BlockSpec(memory_space=pltpu.VMEM),
-        scratch_shapes=[pltpu.SemaphoreType.DMA, pltpu.SemaphoreType.DMA],
+        scratch_shapes=[pltpu.VMEM((W, S, rows, lanes), x.dtype)] + [pltpu.SemaphoreType.DMA] * 6,
         compiler_params=pltpu.CompilerParams(collective_id=cid, has_side_effects=True),
-    )(x)
+    )(xt)
+    return w.reshape(n, rows, lanes)
 
 
 def per_device(
@@ -91,6 +92,7 @@
     block_count = col_count // BLOCK
     devices = lax.axis_size(("shard", "tensor"))
     width = lax.axis_size("tensor")
+    height = lax.axis_size("shard")
     slot_count = stat_left.shape[1]
     total_blocks = owners.shape[0]
     positions = jnp.arange(total_blocks, dtype=jnp.int32)
@@ -130,7 +132,7 @@
     outgoing = jnp.concatenate(
         [outgoing.reshape(devices, slot_count * row_count, BLOCK), extra], axis=1
     )
-    incoming = exchange(outgoing, devices, width, 0)
+    incoming = exchange(outgoing, height, width, 0)
     block_grads = (
         incoming[:, : slot_count * row_count]
         .reshape(devices, slot_count, row_count, BLOCK)
@@ -167,7 +169,7 @@
         .transpose(1, 0, 2, 3)
         .reshape(devices, slot_count * row_count, BLOCK)
     )
-    returned = exchange(shaped, devices, width, 1)
+    returned = exchange(shaped, height, width, 1)
     returned = returned.reshape(devices * slot_count, row_count, BLOCK)
     own_rows = jnp.take(returned, target, axis=0).reshape(
         layer_count, block_count, row_count, BLOCK

time: 76 us -> 87.6 us (1.15)
  Pallas kernels: 42.5 us -> 54.1 us
    pallas_call x2, Pallas kernels: 42.5 us -> 54.1 us  [exchange(): pl.pallas_call(functools.partial(_a2a_kernel, S, W), out_shape=jax.ShapeD...]
    reshape x3 -> x0, local copies, waits for them, and re-layouts: 4.67 us -> none  [the longest x1 2.34 us: per_device(): returned = returned.reshape(devices * slot_count, row_count, BLOCK)]
    another operation x3 -> x2, local copies, waits for them, and re-layouts: 1.38 us -> 3.79 us  [the longest x1 2.34 us: per_device(): returned = returned.reshape(devices * slot_count, row_count, BLOCK)]
    transpose x0 -> x1, other arithmetic: none -> 2.38 us  [exchange(): xt = x.reshape(S, W, rows, lanes).transpose(1, 0, 2, 3)]
    concatenate x1 -> x0, other arithmetic: 2.37 us -> none  [per_device(): jnp.concatenate([outgoing.reshape(devices, slot_count * row_count, BLOCK)...]
    concatenate x2 -> x6, local copies, waits for them, and re-layouts: 0.08 us -> 2.34 us  [per_device(): jnp.concatenate([outgoing.reshape(devices, slot_count * row_count, BLOCK)...]
    unnamed x12 -> x13, local copies, waits for them, and re-layouts: 0.03 us -> 1.21 us
    slice x1 -> x0, local copies, waits for them, and re-layouts: 1.18 us -> none  [per_device(): incoming[:, :slot_count * row_count]]
where the time goes in v3:
time: 87.6 us; the launch traced here: 87.2 us
  Pallas kernels  54.1 us (62%)
  local copies, waits for them, and re-layouts  13.5 us (15%)
  other arithmetic  10.8 us (12%)
  matrix products  8.01 us (9%)
    pallas_call x2, Pallas kernels, exchange(): pl.pallas_call(functools.partial(_a2a_kernel, S, W), out_shape=jax.ShapeD...  54.1 us
    dot_general x1, matrix products, per_device(): jnp.einsum('cib,cjb->cij', block_grads, block_grads, preferred_element_ty...  4.17 us
    gather x1, local copies, waits for them, and re-layouts, per_device(): jnp.take(returned, target, axis=0)  2.75 us
    reduce_sum x2, other arithmetic, per_device(): jnp.sum(jnp.square(direction).reshape(layer_count, row_count, block_count...  2.72 us
    transpose x1, other arithmetic, exchange(): xt = x.reshape(S, W, rows, lanes).transpose(1, 0, 2, 3)  2.38 us
    concatenate x6, local copies, waits for them, and re-layouts, per_device(): jnp.concatenate([outgoing.reshape(devices, slot_count * row_count, BLOCK)...  2.34 us
    another operation x1, local copies, waits for them, and re-layouts, per_device(): returned = returned.reshape(devices * slot_count, row_count, BLOCK)  2.34 us
    reshape x1, other arithmetic, per_device(): own_rows.transpose(0, 2, 1, 3).reshape(layer_count, row_count, col_count)  2.01 us

profile of v3, /device:TPU:1, one launch (start us, length us, event | category | flops | bytes accessed | tf_op | source)
XLA Modules:
  0.0 87.2 jit_solution(8460909115003337902)
XLA Ops:
  0.6 1.0 %convert_reduce_fusion = s32[192]{0:T(256)S(1)} fusion(s32[192]{0:T(256)} %param.18), kind=kLoop, calls=%fused_computation.23 | loop fusion | flops 184128 | bytes 1536 | tf_op jit(solution)/shard_map/reduce_sum | solution.py:100
  1.7 0.7 compare_and_fusion
  2.4 2.6 %multiply_reduce_fusion.1 = (f32[4,6144]{1,0:T(4,128)S(1)}, f32[4,4,6144]{2,1,0:T(4,128)}, f32[4,4,6144]{2,1,0:T(4,128)}) fusion(bf16[4,4,6144]{2,1,0:T(4,128)(2,1)} %param.11, f32[4,4,6144]{2,1,0:T(4,128)} %param.13, f32[4,4,6144]{2,1,0:T(4,128)} %param.12), kind=kLoop, calls=%fused_computation.18 | loop fusion | flops 1155072 | bytes 1867776 | tf_op jit(solution)/shard_map/reduce_sum | solution.py:110
  5.0 0.1 bitcast_reduce_fusion
  5.1 0.1 reshape.116
  5.2 1.2 %scatter_custom_fusion = f32[384]{0:T(512)S(1)} fusion(s32[192]{0:T(256)S(1)} %compare_select_fusion, f32[192]{0:T(256)S(1)} %reshape.116, f32[]{:T(128)} %constant.17.clone.1), kind=kCustom, calls=%fused_computation.42 | custom fusion | bytes 1540 | tf_op jit(solution)/shard_map/scatter | solution.py:116
  6.4 0.2 reshape.98
  6.6 0.7 copy.52
  7.3 0.7 copy.51
  8.0 0.1 pad.12.clone
  8.1 1.1 %reshape.96 = bf16[4,4,48,128]{3,2,1,0:T(8,128)(2,1)S(1)} reshape(bf16[4,4,6144]{2,1,0:T(4,128)(2,1)} %param.11) | data formatting | bytes 393216 | tf_op jit(solution)/shard_map/reshape | solution.py:128
  9.1 0.1 eq.48
  9.2 0.4 fusion.2
  9.6 0.3 copy.49
  9.9 0.9 %concatenate.13 = bf16[16,8,12,128]{3,2,1,0:T(8,128)(2,1)} reshape(bf16[384,4,128]{2,1,0:T(4,128)(2,1)S(1)} %copy.49) | data formatting | bytes 786432 | tf_op jit(solution)/shard_map/concatenate | solution.py:132
  10.8 2.4 %maximum_bitcast_fusion.x_ref = bf16[8,16,16,128]{3,2,1,0:T(8,128)(2,1)} fusion(bf16[16,8,1,128]{3,2,0,1:T(2,128)(2,1)} %copy.52, bf16[16,8,1,128]{3,2,0,1:T(2,128)(2,1)} %copy.51, bf16[16]{0:T(256)(128)(2,1)S(1)} %pad.12.clone, bf16[16,8,12,128]{3,2,1,0:T(8,128)(2,1)} %concatenate.13), kind=kLoop, calls=%fused_computation.12 | loop fusion | flops 2097152 | bytes 983072 | tf_op jit(solution)/shard_map/transpose | solution.py:66
  13.2 26.5 %shard_map.170 = bf16[16,8,16,128]{3,2,1,0:T(8,128)(2,1)} custom-call(bf16[8,16,16,128]{3,2,1,0:T(8,128)(2,1)} %maximum_bitcast_fusion.x_ref), custom_call_target="tpu_custom_call" | custom-call | tf_op jit(solution)/shard_map/pallas_call | solution.py:67
  39.7 1.2 %copy.65 = bf16[128,12,128]{2,0,1:T(8,128)(2,1)S(1)} copy(bf16[128,12,128]{2,1,0:T(8,128)(2,1)} %bitcast.67) | data formatting | bytes 786432
  40.9 0.3 copy.54
  41.2 1.6 %fusion = f32[3,128,512]{1,2,0:T(8,128)S(1)} fusion(bf16[3,512,128]{2,1,0:T(8,128)(2,1)S(1)} %bitcast.61, f32[1,3,512,512]{3,2,1,0:T(8,128)S(1)} %copy-done), kind=kOutput, calls=%fused_computation.3 | convolution fusion | flops 1207959552 | bytes 4325376 | tf_op jit(solution)/shard_map/cij,cjb->cib/dot_general | solution.py:160
  42.8 0.9 %multiply_reduce_fusion = (f32[3]{0:T(128)S(1)}, f32[3,512,128]{2,1,0:T(8,128)S(1)}) fusion(f32[3,128,512]{1,2,0:T(8,128)S(1)} %fusion, f32[1,3,128,128]{3,2,1,0:T(8,128)S(1)} %copy-done.2), kind=kOutput, calls=%fused_computation.10 | convolution fusion | flops 302383104 | bytes 1769484 | tf_op jit(solution)/shard_map/cib,cbd->cid/dot_general | solution.py:163
  43.7 1.2 %fusion.13 = f32[3]{0:T(128)S(1)} fusion(bf16[128,16,128]{2,1,0:T(8,128)(2,1)} %bitcast.68), kind=kLoop, calls=%fused_computation.32 | loop fusion | flops 1533 | bytes 1548 | tf_op jit(solution)/shard_map/reduce_sum | solution.py:143
  44.9 0.1 broadcast_multiply_fusion
  45.1 1.4 %copy.71 = f32[16,8,12,128]{3,2,0,1:T(8,128)} copy(f32[16,8,12,128]{3,1,0,2:T(8,128)S(1)} %bitcast.65) | data formatting | bytes 1572864 | tf_op jit(solution)/shard_map/reshape;reshape | solution.py:66
  46.6 27.6 %shard_map.171 = f32[16,8,12,128]{3,2,1,0:T(8,128)} custom-call(f32[8,16,12,128]{3,2,1,0:T(8,128)} %bitcast.64), custom_call_target="tpu_custom_call" | custom-call | tf_op jit(solution)/shard_map/pallas_call | solution.py:67
  74.2 2.3 %reshape_reshape.7 = f32[384,4,128]{2,1,0:T(4,128)} reshape(f32[16,8,12,128]{3,2,1,0:T(8,128)} %shard_map.171) | data formatting | bytes 1572864 | tf_op jit(solution)/shard_map/reshape;reshape | solution.py:173
  76.5 2.8 %gather_fusion = f32[192,4,128]{2,1,0:T(4,128)} fusion(f32[384,4,128]{2,1,0:T(4,128)} %reshape_reshape.7, s32[1024]{0:T(1024)S(1)} %pad_clamp_fusion), kind=kCustom, calls=%fused_computation | custom fusion | bytes 787200 | tf_op jit(solution)/shard_map/jit(_take)/gather | solution.py:174
  79.3 0.1 broadcast_in_dim.31
  79.4 2.0 %select_bitcast_fusion = f32[4,4,6144]{2,1,0:T(4,128)} fusion(f32[4,48,4,128]{3,2,1,0:T(4,128)} %bitcast.70, pred[4,48]{1,0:T(4,128)(4,1)S(1)} %broadcast_in_dim.31), kind=kLoop, calls=%fused_computation.16 | loop fusion | flops 98304 | bytes 786624 | tf_op jit(solution)/shard_map/reshape | solution.py:177
  81.4 4.2 %bitcast_add_fusion = f32[1,3,512,512]{3,2,1,0:T(8,128)} fusion(f32[1,3,512,512]{3,2,1,0:T(8,128)} %param.14, bf16[3,512,128]{2,1,0:T(8,128)(2,1)S(1)} %bitcast.62), kind=kOutput, calls=%fused_computation.2 | convolution fusion | flops 202113024 | bytes 6684672 | tf_op jit(solution)/shard_map/cib,cjb->cij/dot_general | solution.py:150
  85.5 1.0 %fusion.3 = f32[1,3,128,128]{3,2,1,0:T(8,128)} fusion(f32[1,3,128,128]{3,2,1,0:T(8,128)S(1)} %copy-done.1, bf16[3,512,128]{2,1,0:T(8,128)(2,1)S(1)} %bitcast.63), kind=kOutput, calls=%fused_computation.8 | convolution fusion | flops 50380800 | bytes 786432 | tf_op jit(solution)/shard_map/cib,cid->cbd/dot_general | solution.py:156
  86.5 0.6 add_divide_fusion
  (19 shorter events, 0.2 us)
Async XLA Ops:
  0.6 40.6 %copy-start = (f32[1,3,512,512]{3,2,1,0:T(8,128)S(1)}, f32[1,3,512,512]{3,2,1,0:T(8,128)}, u32[]{:S(2)}) copy-start(f32[1,3,512,512]{3,2,1,0:T(8,128)} %param.16) | copy-start | bytes 9437188
  39.7 3.1 %copy-start.2 = (f32[1,3,128,128]{3,2,1,0:T(8,128)S(1)}, f32[1,3,128,128]{3,2,1,0:T(8,128)}, u32[]{:S(2)}) copy-start(f32[1,3,128,128]{3,2,1,0:T(8,128)} %param.17) | copy-start | bytes 589828
  81.4 4.2 %copy-start.1 = (f32[1,3,128,128]{3,2,1,0:T(8,128)S(1)}, f32[1,3,128,128]{3,2,1,0:T(8,128)}, u32[]{:S(2)}) copy-start(f32[1,3,128,128]{3,2,1,0:T(8,128)} %param.15) | copy-start | bytes 589828
  81.4 5.2 %copy-start.3 = (f32[6336]{0:T(1024)S(1)}, f32[6336]{0:T(1024)}, u32[]{:S(2)}) copy-start(f32[6336]{0:T(1024)} %param.19) | copy-start | bytes 76036
  81.4 5.2 %copy-start.4 = (f32[6336]{0:T(1024)S(1)}, f32[6336]{0:T(1024)}, u32[]{:S(2)}) copy-start(f32[6336]{0:T(1024)} %param.21) | copy-start | bytes 76036
  81.4 5.2 %copy-start.5 = (f32[6336]{0:T(1024)S(1)}, f32[6336]{0:T(1024)}, u32[]{:S(2)}) copy-start(f32[6336]{0:T(1024)} %param.20) | copy-start | bytes 76036

commit v4 on v0

--- a/solution.py
+++ b/solution.py
@@ -48,7 +48,6 @@
     adam_part = jnp.sum(
         jnp.square(direction).reshape(layer_count, row_count, block_count, BLOCK), axis=(1, 3)
     )
-    adam_sums = lax.psum(adam_part, ("shard", "tensor"))
     pieces = gradients.reshape(layer_count, row_count, block_count, BLOCK)
     outgoing = jnp.einsum(
         "qln,lrnb->qrb", picker, pieces, preferred_element_type=jnp.float32
@@ -58,6 +57,16 @@
         outgoing, ("shard", "tensor"), split_axis=1, concat_axis=1, tiled=True
     )
     block_grads = incoming.reshape(slot_count, devices * row_count, BLOCK)
+    gathered = lax.all_gather(adam_part.reshape(total_blocks), ("shard", "tensor"))
+    block_sums = jnp.sum(gathered, axis=0)
+    me = lax.axis_index(("shard", "tensor"))
+    place_sums = (
+        jnp.zeros((slot_count * devices,), jnp.float32)
+        .at[target]
+        .set(block_sums)
+        .reshape(slot_count, devices)
+    )
+    adam_sums = lax.dynamic_index_in_dim(place_sums, me, axis=1, keepdims=False)
     left_out = (
         stat_left
         + jnp.einsum("cib,cjb->cij", block_grads, block_grads, preferred_element_type=jnp.float32)[
@@ -74,20 +83,16 @@
         "cij,cjb->cib", root_left[0], block_grads.astype(jnp.float32), precision=PRECISE
     )
     precond = jnp.einsum("cib,cbd->cid", left_applied, root_right[0], precision=PRECISE)
-    shaped = precond.reshape(slot_count, devices, row_count, BLOCK)
+    precond_sums = jnp.sum(jnp.square(precond), axis=(1, 2))
+    graft_ratio = jnp.sqrt(adam_sums / (precond_sums + 1e-06))
+    scaled = precond * graft_ratio[:, None, None]
+    shaped = scaled.reshape(slot_count, devices, row_count, BLOCK)
     returned = lax.all_to_all(shaped, ("shard", "tensor"), split_axis=1, concat_axis=1, tiled=True)
     returned = returned.reshape(slot_count * devices, row_count, BLOCK)
     own_rows = jnp.take(returned, target, axis=0).reshape(
         layer_count, block_count, row_count, BLOCK
     )
-    precond_part = jnp.sum(jnp.square(own_rows), axis=(2, 3))
-    precond_sums = lax.psum(precond_part, ("shard", "tensor"))
-    graft_ratio = jnp.sqrt(adam_sums / (precond_sums + 1e-06))
-    updates = (
-        (own_rows * graft_ratio[:, :, None, None])
-        .transpose(0, 2, 1, 3)
-        .reshape(layer_count, row_count, col_count)
-    )
+    updates = own_rows.transpose(0, 2, 1, 3).reshape(layer_count, row_count, col_count)
     small_mean_out, small_square_out, small_update = adam_moments(
         small_grad, small_mean, small_square
     )

time: 131 us -> 93.3 us (0.71)
  blocking collectives: 63.1 us -> 37 us
  waiting for transfers between devices: 16.2 us -> 8.4 us
  other arithmetic: 11.1 us -> 6.82 us
    psum x1 -> x0, blocking collectives: 63.1 us -> none  [per_device(): adam_sums = lax.psum(adam_part, ('shard', 'tensor'))]
    all_gather x0 -> x1, blocking collectives: none -> 37 us  [per_device(): lax.all_gather(adam_part.reshape(total_blocks), ('shard', 'tensor'))]
    all_to_all x1, waiting for transfers between devices: 7.29 us -> 0.01 us  [per_device(): lax.all_to_all(outgoing, ('shard', 'tensor'), split_axis=1, concat_axis=1...]
    reduce_sum x1, other arithmetic: 2.02 us -> 0.16 us  [per_device(): block_sums = jnp.sum(gathered, axis=0)]
    reduce_sum x2, other arithmetic: 4.15 us -> 2.62 us  [per_device(): jnp.sum(jnp.square(direction).reshape(layer_count, row_count, block_count...]
  transfers between devices with their start and end apart: 2 -> 2, of which waited for: 2 -> 1; matrix products, arithmetic and copies ran while one was open for 9% -> 13% of each run, Pallas kernels for 0% -> 0%
where the time goes in v4:
time: 93.3 us; the launch traced here: 92.7 us
  blocking collectives  37 us (40%)
  starting transfers between devices  17.5 us (19%)
  local copies, waits for them, and re-layouts  12.5 us (13%)
  matrix products  9.82 us (11%)
  waiting for transfers between devices  8.4 us (9%)
  other arithmetic  6.82 us (7%)
    all_gather x1, blocking collectives, per_device(): lax.all_gather(adam_part.reshape(total_blocks), ('shard', 'tensor'))  37 us
    all_to_all x1, starting transfers between devices, per_device(): lax.all_to_all(outgoing, ('shard', 'tensor'), split_axis=1, concat_axis=1...  11.9 us
    all_to_all x1, waiting for transfers between devices, per_device(): lax.all_to_all(shaped, ('shard', 'tensor'), split_axis=1, concat_axis=1,...  8.4 us
    all_to_all x1, starting transfers between devices, per_device(): lax.all_to_all(shaped, ('shard', 'tensor'), split_axis=1, concat_axis=1,...  5.62 us
    dot_general x1, matrix products, per_device(): jnp.einsum('cib,cjb->cij', block_grads, block_grads, preferred_element_ty...  4.12 us
    reduce_sum x2, other arithmetic, per_device(): jnp.sum(jnp.square(direction).reshape(layer_count, row_count, block_count...  2.62 us
    all_to_all x1, local copies, waits for them, and re-layouts, per_device(): lax.all_to_all(shaped, ('shard', 'tensor'), split_axis=1, concat_axis=1,...  2.17 us
    gather x2, local copies, waits for them, and re-layouts, per_device(): jnp.take(returned, target, axis=0)  2.05 us
  transfers between devices with their start and end apart: 2, of which 1 were waited for; matrix products, arithmetic and copies ran while one was open for 13% of the time, Pallas kernels for 0%

profile of v4, /device:TPU:1, one launch (start us, length us, event | category | flops | bytes accessed | tf_op | source)
XLA Modules:
  0.0 92.7 jit_solution(5222586895232383153)
XLA Ops:
  0.6 0.0 copy-start
  0.7 1.2 %reshape.83 = bf16[4,4,48,128]{3,2,1,0:T(8,128)(2,1)S(1)} reshape(bf16[4,4,6144]{2,1,0:T(4,128)(2,1)} %param.11) | data formatting | bytes 393216 | tf_op jit(solution)/shard_map/reshape | solution.py:51
  1.9 0.9 %convert_reduce_fusion = s32[192]{0:T(256)S(1)} fusion(s32[192]{0:T(256)} %param.18), kind=kLoop, calls=%fused_computation.21 | loop fusion | flops 184128 | bytes 1536 | tf_op jit(solution)/shard_map/reduce_sum | solution.py:38
  2.8 0.7 compare_and_fusion
  3.5 0.1 eq.48
  3.6 0.4 fusion.2
  4.0 1.1 %copy.52 = bf16[3,128,4,128]{3,2,0,1:T(4,128)(2,1)} copy(bf16[3,128,4,128]{3,1,0,2:T(8,128)(2,1)S(1)} %bitcast.56) | data formatting | bytes 786432 | tf_op jit(solution)/shard_map/reshape | solution.py:55
  5.1 11.9 %all-to-all-start = ((bf16[3,128,4,128]{3,2,0,1:T(4,128)(2,1)}), bf16[3,128,4,128]{3,2,0,1:T(4,128)(2,1)}, u32[]{:S(2)}, u32[]{:S(2)}) async-start(bf16[3,128,4,128]{3,2,0,1:T(4,128)(2,1)} %copy.52), calls=%async_computation | async-start | bytes 786432 | tf_op jit(solution)/shard_map/all_to_all | solution.py:56
  17.0 2.5 %multiply_reduce_fusion.1 = (f32[4,6144]{1,0:T(4,128)S(1)}, f32[4,4,6144]{2,1,0:T(4,128)}, f32[4,4,6144]{2,1,0:T(4,128)}) fusion(bf16[4,4,6144]{2,1,0:T(4,128)(2,1)S(1)} %copy-done.1, f32[4,4,6144]{2,1,0:T(4,128)} %param.13, f32[4,4,6144]{2,1,0:T(4,128)} %param.12), kind=kLoop, calls=%fused_computation.16 | loop fusion | flops 1155072 | bytes 1867776 | tf_op jit(solution)/shard_map/reduce_sum | solution.py:48
  19.5 0.1 bitcast_reduce_fusion
  19.6 0.1 reshape.108
  19.7 37.0 %all-gather = f32[128,1,192]{2,1,0:T(1,128)S(1)} all-gather(f32[1,1,192]{2,1,0:T(1,128)S(1)} %reshape.108), channel_id=1, replica_groups=mesh['shard'=16,'tensor'=8] {'shard','tensor'}, dimensions={0}, use_global_device_ids=true | all-gather | bytes 99072 | tf_op jit(solution)/shard_map/all_gather | solution.py:60
  56.6 0.2 reduce_sum.47
  56.8 1.2 %scatter_custom_fusion = f32[384]{0:T(512)S(1)} fusion(s32[192]{0:T(256)S(1)} %compare_select_fusion, f32[192]{0:T(256)S(1)} %reduce_sum.47, f32[]{:T(128)} %constant.20.clone.1), kind=kCustom, calls=%fused_computation.34 | custom fusion | bytes 1540 | tf_op jit(solution)/shard_map/scatter | solution.py:66
  58.0 0.2 dynamic-slice_reduce_fusion
  58.2 0.0 all-to-all-done
  58.2 1.1 %copy.53 = bf16[3,128,4,128]{3,2,1,0:T(4,128)(2,1)S(1)} copy(bf16[3,128,4,128]{3,2,0,1:T(4,128)(2,1)} %all-to-all-done) | data formatting | bytes 786432 | tf_op jit(solution)/shard_map/all_to_all | solution.py:56
  59.3 1.6 %fusion = f32[3,128,512]{1,2,0:T(8,128)S(1)} fusion(bf16[3,512,128]{2,1,0:T(8,128)(2,1)S(1)} %bitcast.49, f32[1,3,512,512]{3,2,1,0:T(8,128)S(1)} %copy-done), kind=kOutput, calls=%fused_computation.3 | convolution fusion | flops 1207959552 | bytes 4325376 | tf_op jit(solution)/shard_map/cij,cjb->cib/dot_general | solution.py:82
  60.9 1.8 %multiply_reduce_fusion = (f32[3]{0:T(128)S(1)}, f32[3,512,128]{2,1,0:T(8,128)S(1)}) fusion(f32[3,128,512]{1,2,0:T(8,128)S(1)} %fusion, f32[1,3,128,128]{3,2,1,0:T(8,128)} %param.17), kind=kOutput, calls=%fused_computation.9 | convolution fusion | flops 302383104 | bytes 1769484 | tf_op jit(solution)/shard_map/cib,cbd->cid/dot_general | solution.py:85
  62.8 0.1 broadcast_multiply_fusion
  62.9 1.0 %copy.56 = f32[3,128,4,128]{3,2,0,1:T(4,128)} copy(f32[3,128,4,128]{3,2,1,0:T(4,128)S(1)} %bitcast.52) | data formatting | bytes 1572864 | tf_op jit(solution)/shard_map/reshape | solution.py:89
  63.9 5.6 %all-to-all-start.1 = ((f32[3,128,4,128]{3,2,0,1:T(4,128)}), f32[3,128,4,128]{3,2,0,1:T(4,128)}, u32[]{:S(2)}, u32[]{:S(2)}) async-start(f32[3,128,4,128]{3,2,0,1:T(4,128)} %copy.56), calls=%async_computation.1 | async-start | bytes 1572864 | tf_op jit(solution)/shard_map/all_to_all | solution.py:90
  69.6 1.4 %add_divide_fusion = (f32[6336]{0:T(1024)}, f32[6336]{0:T(1024)}, f32[6336]{0:T(1024)}) fusion(f32[6336]{0:T(1024)} %param.19, f32[6336]{0:T(1024)} %param.21, f32[6336]{0:T(1024)} %param.20), kind=kLoop, calls=%fused_computation.28 | loop fusion | flops 57024 | bytes 152064 | tf_op jit(solution)/shard_map/div | solution.py:15
  71.0 0.1 broadcast_in_dim.31
  71.1 1.9 %fusion.3 = f32[1,3,128,128]{3,2,1,0:T(8,128)} fusion(f32[1,3,128,128]{3,2,1,0:T(8,128)} %param.15, bf16[3,512,128]{2,1,0:T(8,128)(2,1)S(1)} %bitcast.50), kind=kOutput, calls=%fused_computation.8 | convolution fusion | flops 50380800 | bytes 786432 | tf_op jit(solution)/shard_map/cib,cid->cbd/dot_general | solution.py:78
  73.0 4.1 %bitcast_add_fusion = f32[1,3,512,512]{3,2,1,0:T(8,128)} fusion(f32[1,3,512,512]{3,2,1,0:T(8,128)} %param.14, bf16[3,512,128]{2,1,0:T(8,128)(2,1)S(1)} %bitcast.51), kind=kOutput, calls=%fused_computation.2 | convolution fusion | flops 202113024 | bytes 6684672 | tf_op jit(solution)/shard_map/cib,cjb->cij/dot_general | solution.py:72
  77.1 8.4 %all-to-all-done.1 = f32[3,128,4,128]{3,2,0,1:T(4,128)} async-done(((f32[3,128,4,128]{3,2,0,1:T(4,128)}), f32[3,128,4,128]{3,2,0,1:T(4,128)}, u32[]{:S(2)}, u32[]{:S(2)}) %all-to-all-start.1) | async-done | bytes 786464 | tf_op jit(solution)/shard_map/all_to_all | solution.py:90
  85.5 2.2 %copy.57 = f32[3,128,4,128]{3,2,1,0:T(4,128)} copy(f32[3,128,4,128]{3,2,0,1:T(4,128)} %all-to-all-done.1) | data formatting | bytes 1572864 | tf_op jit(solution)/shard_map/all_to_all | solution.py:90
  87.7 2.0 %gather_fusion = f32[192,4,128]{2,1,0:T(4,128)S(1)} fusion(f32[384,4,128]{2,1,0:T(4,128)} %bitcast.53, s32[1024]{0:T(1024)S(1)} %pad_clamp_fusion), kind=kCustom, calls=%fused_computation | custom fusion | bytes 787200 | tf_op jit(solution)/shard_map/jit(_take)/gather | solution.py:92
  89.8 0.8 select_bitcast_fusion
  90.6 1.1 %reshape.89 = f32[4,4,6144]{2,0,1:T(4,128)S(1)} reshape(f32[4,4,48,128]{3,2,0,1:T(8,128)} %select_bitcast_fusion) | data formatting | bytes 786432 | tf_op jit(solution)/shard_map/reshape | solution.py:95
  91.7 1.0 %copy.60 = f32[4,4,6144]{2,1,0:T(4,128)} copy(f32[4,4,6144]{2,0,1:T(4,128)S(1)} %reshape.89) | data formatting | bytes 786432
  (7 shorter events, 0.1 us)
Async XLA Ops:
  0.6 58.7 %copy-start = (f32[1,3,512,512]{3,2,1,0:T(8,128)S(1)}, f32[1,3,512,512]{3,2,1,0:T(8,128)}, u32[]{:S(2)}) copy-start(f32[1,3,512,512]{3,2,1,0:T(8,128)} %param.16) | copy-start | bytes 9437188
  0.6 16.3 %copy-start.1 = (bf16[4,4,6144]{2,1,0:T(4,128)(2,1)S(1)}, bf16[4,4,6144]{2,1,0:T(4,128)(2,1)}, u32[]{:S(2)}) copy-start(bf16[4,4,6144]{2,1,0:T(4,128)(2,1)} %param.11) | copy-start | bytes 589828
  5.1 53.1 %all-to-all-start = ((bf16[3,128,4,128]{3,2,0,1:T(4,128)(2,1)}), bf16[3,128,4,128]{3,2,0,1:T(4,128)(2,1)}, u32[]{:S(2)}, u32[]{:S(2)}) async-start(bf16[3,128,4,128]{3,2,0,1:T(4,128)(2,1)} %copy.52), calls=%async_computation | async-start | bytes 786432 | tf_op jit(solution)/shard_map/all_to_all | solution.py:56
  63.9 21.6 %all-to-all-start.1 = ((f32[3,128,4,128]{3,2,0,1:T(4,128)}), f32[3,128,4,128]{3,2,0,1:T(4,128)}, u32[]{:S(2)}, u32[]{:S(2)}) async-start(f32[3,128,4,128]{3,2,0,1:T(4,128)} %copy.56), calls=%async_computation.1 | async-start | bytes 1572864 | tf_op jit(solution)/shard_map/all_to_all | solution.py:90

commit v5 on v2

--- a/solution.py
+++ b/solution.py
@@ -1,14 +1,9 @@
-import functools
-
 import jax
 import jax.numpy as jnp
 from jax import lax
-from jax.experimental import pallas as pl
-from jax.experimental.pallas import tpu as pltpu
 from jax.sharding import PartitionSpec as P
 
 BLOCK = 128
-MESH = pl.DeviceIdType.MESH
 
 
 PRECISE = lax.Precision.HIGHEST
@@ -20,58 +15,8 @@
     return (mean_new, square_new, mean_new / (jnp.sqrt(square_new) + 1e-08))
 
 
-def _a2a_kernel(n, width, x_ref, y_ref, send_sem, recv_sem):
-    me = lax.axis_index("shard") * width + lax.axis_index("tensor")
-
-    def where(d):
-        return (lax.div(d, width), lax.rem(d, width))
-
-    barrier = pltpu.get_barrier_semaphore()
-
-    def greet(j, c):
-        pl.semaphore_signal(
-            barrier, inc=1, device_id=where(lax.rem(me + j, n)), device_id_type=MESH
-        )
-        return c
-
-    lax.fori_loop(1, n, greet, 0)
-    pl.semaphore_wait(barrier, n - 1)
-
-    def send(j, c):
-        d = lax.rem(me + j, n)
-        pltpu.make_async_remote_copy(
-            src_ref=x_ref.at[pl.ds(d, 1)],
-            dst_ref=y_ref.at[pl.ds(me, 1)],
-            send_sem=send_sem,
-            recv_sem=recv_sem,
-            device_id=where(d),
-            device_id_type=MESH,
-        ).start()
-        return c
-
-    lax.fori_loop(1, n, send, 0)
-    y_ref[pl.ds(me, 1)] = x_ref[pl.ds(me, 1)]
-    every = pltpu.make_async_remote_copy(
-        src_ref=x_ref.at[pl.ds(0, n - 1)],
-        dst_ref=y_ref.at[pl.ds(0, n - 1)],
-        send_sem=send_sem,
-        recv_sem=recv_sem,
-        device_id=where(lax.rem(me + 1, n)),
-        device_id_type=MESH,
-    )
-    every.wait_send()
-    every.wait_recv()
-
-
-def exchange(x, n, width, cid):
-    return pl.pallas_call(
-        functools.partial(_a2a_kernel, n, width),
-        out_shape=jax.ShapeDtypeStruct(x.shape, x.dtype),
-        in_specs=[pl.BlockSpec(memory_space=pltpu.VMEM)],
-        out_specs=pl.BlockSpec(memory_space=pltpu.VMEM),
-        scratch_shapes=[pltpu.SemaphoreType.DMA, pltpu.SemaphoreType.DMA],
-        compiler_params=pltpu.CompilerParams(collective_id=cid, has_side_effects=True),
-    )(x)
+def exchange(x):
+    return lax.all_to_all(x, ("shard", "tensor"), split_axis=0, concat_axis=0, tiled=True)
 
 
 def per_device(
@@ -90,7 +35,6 @@
     layer_count, row_count, col_count = gradients.shape
     block_count = col_count // BLOCK
     devices = lax.axis_size(("shard", "tensor"))
-    width = lax.axis_size("tensor")
     slot_count = stat_left.shape[1]
     total_blocks = owners.shape[0]
     positions = jnp.arange(total_blocks, dtype=jnp.int32)
@@ -130,7 +74,7 @@
     outgoing = jnp.concatenate(
         [outgoing.reshape(devices, slot_count * row_count, BLOCK), extra], axis=1
     )
-    incoming = exchange(outgoing, devices, width, 0)
+    incoming = exchange(outgoing)
     block_grads = (
         incoming[:, : slot_count * row_count]
         .reshape(devices, slot_count, row_count, BLOCK)
@@ -167,7 +111,7 @@
         .transpose(1, 0, 2, 3)
         .reshape(devices, slot_count * row_count, BLOCK)
     )
-    returned = exchange(shaped, devices, width, 1)
+    returned = exchange(shaped)
     returned = returned.reshape(devices * slot_count, row_count, BLOCK)
     own_rows = jnp.take(returned, target, axis=0).reshape(
         layer_count, block_count, row_count, BLOCK

time: 76 us -> 74.5 us (0.980)
  Pallas kernels: 42.5 us -> 0 us
  blocking collectives: 0 us -> 24.8 us
  waiting for transfers between devices: 0 us -> 11.3 us
  starting transfers between devices: 0 us -> 5.68 us
  other arithmetic: 10.8 us -> 8.62 us
  matrix products: 8.01 us -> 8.89 us
    pallas_call x2 -> x0, Pallas kernels: 42.5 us -> none  [exchange(): pl.pallas_call(functools.partial(_a2a_kernel, n, width), out_shape=jax.Sh...]
    all_to_all x0 -> x1, blocking collectives: none -> 24.8 us  [exchange(): lax.all_to_all(x, ('shard', 'tensor'), split_axis=0, concat_axis=0, tiled...]
    all_to_all x0 -> x1, waiting for transfers between devices: none -> 11.3 us  [exchange(): lax.all_to_all(x, ('shard', 'tensor'), split_axis=0, concat_axis=0, tiled...]
    all_to_all x0 -> x1, starting transfers between devices: none -> 5.68 us  [exchange(): lax.all_to_all(x, ('shard', 'tensor'), split_axis=0, concat_axis=0, tiled...]
    reshape x1 -> x0, other arithmetic: 2.01 us -> none  [per_device(): own_rows.transpose(0, 2, 1, 3).reshape(layer_count, row_count, col_count)]
    reshape x0 -> x1, local copies, waits for them, and re-layouts: none -> 1.13 us  [per_device(): own_rows.transpose(0, 2, 1, 3).reshape(layer_count, row_count, col_count)]
    slice x1, local copies, waits for them, and re-layouts: 1.18 us -> 0.1 us  [per_device(): incoming[:, :slot_count * row_count]]
    reduce_sum x1, other arithmetic: 1.22 us -> 0.17 us  [per_device(): jnp.sum(incoming[:, tail, :slot_count].astype(jnp.float32) + incoming[:,...]
  transfers between devices with their start and end apart: 0 -> 1, of which waited for: 0 -> 1; matrix products, arithmetic and copies ran while one was open for 0% -> 10% of each run, Pallas kernels for 0% -> 0%
where the time goes in v5:
time: 74.5 us; the launch traced here: 74 us
  blocking collectives  24.8 us (33%)
  local copies, waits for them, and re-layouts  13.9 us (19%)
  waiting for transfers between devices  11.3 us (15%)
  matrix products  8.89 us (12%)
  other arithmetic  8.62 us (12%)
  starting transfers between devices  5.68 us (8%)
  between operations  0.79 us (1%)
    all_to_all x1, blocking collectives, exchange(): lax.all_to_all(x, ('shard', 'tensor'), split_axis=0, concat_axis=0, tiled...  24.8 us
    all_to_all x1, waiting for transfers between devices, exchange(): lax.all_to_all(x, ('shard', 'tensor'), split_axis=0, concat_axis=0, tiled...  11.3 us
    all_to_all x1, starting transfers between devices, exchange(): lax.all_to_all(x, ('shard', 'tensor'), split_axis=0, concat_axis=0, tiled...  5.68 us
    dot_general x1, matrix products, per_device(): jnp.einsum('cib,cjb->cij', block_grads, block_grads, preferred_element_ty...  4.13 us
    reduce_sum x2, other arithmetic, per_device(): jnp.sum(jnp.square(direction).reshape(layer_count, row_count, block_count...  2.72 us
    reshape x1, local copies, waits for them, and re-layouts, per_device(): returned = returned.reshape(devices * slot_count, row_count, BLOCK)  2.39 us
    gather x2, local copies, waits for them, and re-layouts, per_device(): jnp.take(returned, target, axis=0)  2.05 us
    dot_general x1, matrix products, per_device(): jnp.einsum('cib,cid->cbd', block_grads, block_grads, preferred_element_ty...  1.92 us
  transfers between devices with their start and end apart: 1, of which 1 were waited for; matrix products, arithmetic and copies ran while one was open for 10% of the time, Pallas kernels for 0%

profile of v5, /device:TPU:1, one launch (start us, length us, event | category | flops | bytes accessed | tf_op | source)
XLA Modules:
  0.0 74.0 jit_solution(11933397825763471661)
XLA Ops:
  0.6 1.0 %convert_reduce_fusion = s32[192]{0:T(256)S(1)} fusion(s32[192]{0:T(256)} %param.18), kind=kLoop, calls=%fused_computation.22 | loop fusion | flops 184128 | bytes 1536 | tf_op jit(solution)/shard_map/reduce_sum | solution.py:42
  1.7 0.7 compare_and_fusion
  2.5 1.1 %reshape.93 = bf16[4,4,48,128]{3,2,1,0:T(8,128)(2,1)S(1)} reshape(bf16[4,4,6144]{2,1,0:T(4,128)(2,1)} %param.11) | data formatting | bytes 393216 | tf_op jit(solution)/shard_map/reshape | solution.py:70
  3.5 2.6 %multiply_reduce_fusion.1 = (f32[4,6144]{1,0:T(4,128)S(1)}, f32[4,4,6144]{2,1,0:T(4,128)}, f32[4,4,6144]{2,1,0:T(4,128)}) fusion(bf16[4,4,6144]{2,1,0:T(4,128)(2,1)} %param.11, f32[4,4,6144]{2,1,0:T(4,128)} %param.13, f32[4,4,6144]{2,1,0:T(4,128)} %param.12), kind=kLoop, calls=%fused_computation.17 | loop fusion | flops 1155072 | bytes 1867776 | tf_op jit(solution)/shard_map/reduce_sum | solution.py:52
  6.1 0.1 bitcast_reduce_fusion
  6.3 1.2 %scatter_custom_fusion = f32[384]{0:T(512)S(1)} fusion(s32[192]{0:T(256)S(1)} %compare_select_fusion, f32[192]{0:T(256)S(1)} %reshape.115, f32[]{:T(128)} %constant.17.clone.1), kind=kCustom, calls=%fused_computation.41 | custom fusion | bytes 1540 | tf_op jit(solution)/shard_map/scatter | solution.py:58
  7.5 0.2 reshape.96
  7.8 0.7 copy.75
  8.5 0.7 copy.74
  9.1 0.4 fusion.2
  9.5 0.3 copy.73
  9.9 0.9 %reshape.94 = bf16[128,12,128]{2,1,0:T(8,128)(2,1)} reshape(bf16[384,4,128]{2,1,0:T(4,128)(2,1)S(1)} %copy.73) | data formatting | bytes 786432 | tf_op jit(solution)/shard_map/reshape | solution.py:75
  10.8 1.6 %maximum_maximum_fusion = bf16[128,16,128]{2,1,0:T(8,128)(2,1)S(1)} fusion(bf16[128,1,128]{2,1,0:T(2,128)(2,1)} %copy.75, bf16[128,1,128]{2,1,0:T(2,128)(2,1)} %copy.74, bf16[128,12,128]{2,1,0:T(8,128)(2,1)} %reshape.94, bf16[16]{0:T(256)(128)(2,1)S(1)} %pad.12.clone), kind=kLoop, calls=%fused_computation.11 | loop fusion | flops 2097152 | bytes 983072 | tf_op jit(solution)/shard_map/concatenate | solution.py:74
  12.4 24.8 %all_to_all.10 = bf16[128,16,128]{2,1,0:T(8,128)(2,1)S(1)} all-to-all(bf16[128,16,128]{2,1,0:T(8,128)(2,1)S(1)} %maximum_maximum_fusion), channel_id=1, replica_groups=mesh['shard'=16,'tensor'=8] {'shard','tensor'}, dimensions={0} | all-to-all | bytes 1048576 | tf_op jit(solution)/shard_map/all_to_all | solution.py:19
  37.3 0.1 copy.76
  37.4 0.3 copy.77
  37.7 1.6 %fusion = f32[3,128,512]{1,2,0:T(8,128)S(1)} fusion(bf16[3,512,128]{2,1,0:T(8,128)(2,1)S(1)} %bitcast.57, f32[1,3,512,512]{3,2,1,0:T(8,128)S(1)} %copy-done), kind=kOutput, calls=%fused_computation.3 | convolution fusion | flops 1207959552 | bytes 4325376 | tf_op jit(solution)/shard_map/cij,cjb->cib/dot_general | solution.py:102
  39.3 0.9 %multiply_reduce_fusion = (f32[3]{0:T(128)S(1)}, f32[3,512,128]{2,1,0:T(8,128)S(1)}) fusion(f32[3,128,512]{1,2,0:T(8,128)S(1)} %fusion, f32[1,3,128,128]{3,2,1,0:T(8,128)S(1)} %copy-done.1), kind=kOutput, calls=%fused_computation.9 | convolution fusion | flops 302383104 | bytes 1769484 | tf_op jit(solution)/shard_map/cib,cbd->cid/dot_general | solution.py:105
  40.2 0.2 fusion.13
  40.4 0.1 broadcast_multiply_fusion
  40.6 1.5 %copy.81 = f32[128,12,128]{2,1,0:T(8,128)} copy(f32[128,12,128]{2,0,1:T(8,128)S(1)} %bitcast.60) | data formatting | bytes 1572864 | tf_op jit(solution)/shard_map/reshape | solution.py:112
  42.1 5.7 %all-to-all-start.1 = ((f32[128,12,128]{2,1,0:T(8,128)}), f32[128,12,128]{2,1,0:T(8,128)}, u32[]{:S(2)}, u32[]{:S(2)}) async-start(f32[128,12,128]{2,1,0:T(8,128)} %copy.81), calls=%async_computation.1 | async-start | bytes 2097152 | tf_op jit(solution)/shard_map/all_to_all | solution.py:19
  47.8 1.4 %add_divide_fusion = (f32[6336]{0:T(1024)}, f32[6336]{0:T(1024)}, f32[6336]{0:T(1024)}) fusion(f32[6336]{0:T(1024)} %param.19, f32[6336]{0:T(1024)} %param.21, f32[6336]{0:T(1024)} %param.20), kind=kLoop, calls=%fused_computation.36 | loop fusion | flops 57024 | bytes 152064 | tf_op jit(solution)/shard_map/div | solution.py:15
  49.2 0.1 broadcast_in_dim.31
  49.3 1.9 %fusion.3 = f32[1,3,128,128]{3,2,1,0:T(8,128)} fusion(f32[1,3,128,128]{3,2,1,0:T(8,128)} %param.15, bf16[3,512,128]{2,1,0:T(8,128)(2,1)S(1)} %bitcast.58), kind=kOutput, calls=%fused_computation.8 | convolution fusion | flops 50380800 | bytes 786432 | tf_op jit(solution)/shard_map/cib,cid->cbd/dot_general | solution.py:98
  51.2 4.1 %bitcast_add_fusion = f32[1,3,512,512]{3,2,1,0:T(8,128)} fusion(f32[1,3,512,512]{3,2,1,0:T(8,128)} %param.14, bf16[3,512,128]{2,1,0:T(8,128)(2,1)S(1)} %bitcast.59), kind=kOutput, calls=%fused_computation.2 | convolution fusion | flops 202113024 | bytes 6684672 | tf_op jit(solution)/shard_map/cib,cjb->cij/dot_general | solution.py:92
  55.3 11.3 %all-to-all-done.1 = f32[128,12,128]{2,1,0:T(8,128)} async-done(((f32[128,12,128]{2,1,0:T(8,128)}), f32[128,12,128]{2,1,0:T(8,128)}, u32[]{:S(2)}, u32[]{:S(2)}) %all-to-all-start.1) | async-done | bytes 786464 | tf_op jit(solution)/shard_map/all_to_all | solution.py:19
  66.6 2.4 %reshape.101 = f32[384,4,128]{2,1,0:T(4,128)} reshape(f32[128,12,128]{2,1,0:T(8,128)} %all-to-all-done.1) | data formatting | bytes 1572864 | tf_op jit(solution)/shard_map/reshape | solution.py:115
  69.0 2.0 %gather_fusion = f32[192,4,128]{2,1,0:T(4,128)S(1)} fusion(f32[384,4,128]{2,1,0:T(4,128)} %reshape.101, s32[1024]{0:T(1024)S(1)} %pad_clamp_fusion), kind=kCustom, calls=%fused_computation | custom fusion | bytes 787200 | tf_op jit(solution)/shard_map/jit(_take)/gather | solution.py:116
  71.0 0.8 %select_bitcast_fusion = f32[4,4,48,128]{3,2,0,1:T(8,128)} fusion(f32[4,48,4,128]{3,1,0,2:T(8,128)S(1)} %bitcast.64, pred[4,48]{1,0:T(4,128)(4,1)S(1)} %broadcast_in_dim.31), kind=kLoop, calls=%fused_computation.15 | loop fusion | flops 98304 | bytes 786624 | tf_op jit(solution)/shard_map/transpose | solution.py:119
  71.9 1.1 %reshape.102 = f32[4,4,6144]{2,0,1:T(4,128)S(1)} reshape(f32[4,4,48,128]{3,2,0,1:T(8,128)} %select_bitcast_fusion) | data formatting | bytes 786432 | tf_op jit(solution)/shard_map/reshape | solution.py:119
  73.0 1.0 %copy.84 = f32[4,4,6144]{2,1,0:T(4,128)} copy(f32[4,4,6144]{2,0,1:T(4,128)S(1)} %reshape.102) | data formatting | bytes 786432
  (15 shorter events, 0.4 us)
Async XLA Ops:
  0.6 37.0 %copy-start = (f32[1,3,512,512]{3,2,1,0:T(8,128)S(1)}, f32[1,3,512,512]{3,2,1,0:T(8,128)}, u32[]{:S(2)}) copy-start(f32[1,3,512,512]{3,2,1,0:T(8,128)} %param.16) | copy-start | bytes 9437188
  37.3 2.0 %copy-start.1 = (f32[1,3,128,128]{3,2,1,0:T(8,128)S(1)}, f32[1,3,128,128]{3,2,1,0:T(8,128)}, u32[]{:S(2)}) copy-start(f32[1,3,128,128]{3,2,1,0:T(8,128)} %param.17) | copy-start | bytes 589828
  42.1 24.5 %all-to-all-start.1 = ((f32[128,12,128]{2,1,0:T(8,128)}), f32[128,12,128]{2,1,0:T(8,128)}, u32[]{:S(2)}, u32[]{:S(2)}) async-start(f32[128,12,128]{2,1,0:T(8,128)} %copy.81), calls=%async_computation.1 | async-start | bytes 2097152 | tf_op jit(solution)/shard_map/all_to_all | solution.py:19

commit v6 on v5

--- a/solution.py
+++ b/solution.py
@@ -106,17 +106,12 @@
     precond_sums = jnp.sum(jnp.square(precond), axis=(1, 2))
     graft_ratio = jnp.sqrt(adam_sums / (precond_sums + 1e-06))
     scaled = precond * graft_ratio[:, None, None]
-    shaped = (
-        scaled.reshape(slot_count, devices, row_count, BLOCK)
-        .transpose(1, 0, 2, 3)
-        .reshape(devices, slot_count * row_count, BLOCK)
-    )
-    returned = exchange(shaped)
-    returned = returned.reshape(devices * slot_count, row_count, BLOCK)
-    own_rows = jnp.take(returned, target, axis=0).reshape(
-        layer_count, block_count, row_count, BLOCK
-    )
-    updates = own_rows.transpose(0, 2, 1, 3).reshape(layer_count, row_count, col_count)
+    shaped = scaled.reshape(slot_count, devices, row_count, BLOCK).transpose(1, 0, 2, 3)
+    returned = exchange(shaped).reshape(devices * slot_count, row_count, BLOCK)
+    rows = jnp.arange(row_count, dtype=jnp.int32)
+    updates = returned[
+        target.reshape(layer_count, 1, block_count), rows[None, :, None]
+    ].reshape(layer_count, row_count, col_count)
     small_mean_out, small_square_out, small_update = adam_moments(
         small_grad, small_mean, small_square
     )

time: 74.5 us -> 75.4 us (1.012)
  blocking collectives: 24.8 us -> 0 us
  starting transfers between devices: 5.68 us -> 17.6 us
  waiting for transfers between devices: 11.3 us -> 21.7 us
  local copies, waits for them, and re-layouts: 13.9 us -> 15.3 us
  other arithmetic: 8.62 us -> 9.63 us
  matrix products: 8.89 us -> 9.85 us
    all_to_all x1 -> x0, blocking collectives: 24.8 us -> none  [exchange(): lax.all_to_all(x, ('shard', 'tensor'), split_axis=0, concat_axis=0, tiled...]
    all_to_all x1 -> x2, starting transfers between devices: 5.68 us -> 17.6 us  [exchange(): lax.all_to_all(x, ('shard', 'tensor'), split_axis=0, concat_axis=0, tiled...]
    all_to_all x1 -> x2, waiting for transfers between devices: 11.3 us -> 21.7 us  [exchange(): lax.all_to_all(x, ('shard', 'tensor'), split_axis=0, concat_axis=0, tiled...]
    gather x2 -> x1, local copies, waits for them, and re-layouts: 2.05 us -> 6.55 us  [per_device(): returned[target.reshape(layer_count, 1, block_count), rows[None, :, None]]]
    reshape x3 -> x1, local copies, waits for them, and re-layouts: 5.03 us -> 0.9 us  [per_device(): updates = returned[target.reshape(layer_count, 1, block_count), rows[None...]
    reduce_sum x1, other arithmetic: 0.17 us -> 1.22 us  [per_device(): jnp.sum(incoming[:, tail, :slot_count].astype(jnp.float32) + incoming[:,...]
    slice x1, local copies, waits for them, and re-layouts: 0.1 us -> 1.14 us  [per_device(): incoming[:, :slot_count * row_count]]
    unnamed x5 -> x2, local copies, waits for them, and re-layouts: 1.01 us -> 0.01 us
  transfers between devices with their start and end apart: 1 -> 2, of which waited for: 1 -> 2; matrix products, arithmetic and copies ran while one was open for 10% -> 10% of each run, Pallas kernels for 0% -> 0%
where the time goes in v6:
time: 75.4 us; the launch traced here: 74.8 us
  waiting for transfers between devices  21.7 us (29%)
  starting transfers between devices  17.6 us (23%)
  local copies, waits for them, and re-layouts  15.3 us (20%)
  matrix products  9.85 us (13%)
  other arithmetic  9.63 us (13%)
  between operations  0.78 us (1%)
    all_to_all x2, waiting for transfers between devices, exchange(): lax.all_to_all(x, ('shard', 'tensor'), split_axis=0, concat_axis=0, tiled...  21.7 us
    all_to_all x2, starting transfers between devices, exchange(): lax.all_to_all(x, ('shard', 'tensor'), split_axis=0, concat_axis=0, tiled...  17.6 us
    gather x1, local copies, waits for them, and re-layouts, per_device(): returned[target.reshape(layer_count, 1, block_count), rows[None, :, None]]  6.55 us
    dot_general x1, matrix products, per_device(): jnp.einsum('cib,cjb->cij', block_grads, block_grads, preferred_element_ty...  4.13 us
    reduce_sum x2, other arithmetic, per_device(): jnp.sum(jnp.square(direction).reshape(layer_count, row_count, block_count...  2.72 us
    concatenate x1, other arithmetic, per_device(): jnp.concatenate([outgoing.reshape(devices, slot_count * row_count, BLOCK)...  2.4 us
    dot_general x1, matrix products, per_device(): jnp.einsum('cib,cid->cbd', block_grads, block_grads, preferred_element_ty...  1.91 us
    dot_general x1, matrix products, per_device(): jnp.einsum('cib,cbd->cid', left_applied, root_right[0], precision=PRECISE)  1.82 us
  transfers between devices with their start and end apart: 2, of which 2 were waited for; matrix products, arithmetic and copies ran while one was open for 10% of the time, Pallas kernels for 0%

profile of v6, /device:TPU:1, one launch (start us, length us, event | category | flops | bytes accessed | tf_op | source)
XLA Modules:
  0.0 74.8 jit_solution(11084455393923748951)
XLA Ops:
  0.6 1.0 %convert_reduce_fusion = s32[192]{0:T(256)S(1)} fusion(s32[192]{0:T(256)} %param.18), kind=kLoop, calls=%fused_computation.22 | loop fusion | flops 184128 | bytes 1536 | tf_op jit(solution)/shard_map/reduce_sum | solution.py:42
  1.7 0.7 compare_select_fusion.1
  2.4 1.1 %reshape.103 = bf16[4,4,48,128]{3,2,1,0:T(8,128)(2,1)S(1)} reshape(bf16[4,4,6144]{2,1,0:T(4,128)(2,1)} %param.11) | data formatting | bytes 393216 | tf_op jit(solution)/shard_map/reshape | solution.py:70
  3.4 2.6 %multiply_reduce_fusion.1 = (f32[4,6144]{1,0:T(4,128)S(1)}, f32[4,4,6144]{2,1,0:T(4,128)}, f32[4,4,6144]{2,1,0:T(4,128)}) fusion(bf16[4,4,6144]{2,1,0:T(4,128)(2,1)} %param.11, f32[4,4,6144]{2,1,0:T(4,128)} %param.13, f32[4,4,6144]{2,1,0:T(4,128)} %param.12), kind=kLoop, calls=%fused_computation.17 | loop fusion | flops 1155072 | bytes 1867776 | tf_op jit(solution)/shard_map/reduce_sum | solution.py:52
  6.0 0.1 bitcast_reduce_fusion
  6.1 0.1 reshape.122
  6.2 1.2 %scatter_custom_fusion = f32[384]{0:T(512)S(1)} fusion(s32[192]{0:T(256)S(1)} %get-tuple-element.16, f32[192]{0:T(256)S(1)} %reshape.122, f32[]{:T(128)} %constant.13.clone.1), kind=kCustom, calls=%fused_computation.43 | custom fusion | bytes 1540 | tf_op jit(solution)/shard_map/scatter | solution.py:58
  7.4 0.2 reshape.106
  7.7 0.7 copy.64
  8.4 0.7 copy.63
  9.1 0.1 eq.48
  9.1 0.4 fusion.2
  9.5 0.3 copy.62
  9.9 0.9 %reshape.104 = bf16[128,12,128]{2,1,0:T(8,128)(2,1)} reshape(bf16[384,4,128]{2,1,0:T(4,128)(2,1)S(1)} %copy.62) | data formatting | bytes 786432 | tf_op jit(solution)/shard_map/reshape | solution.py:75
  10.7 0.1 pad.12.clone
  10.8 2.4 %maximum_maximum_fusion = bf16[128,16,128]{2,1,0:T(8,128)(2,1)} fusion(bf16[128,1,128]{2,1,0:T(2,128)(2,1)} %copy.64, bf16[128,1,128]{2,1,0:T(2,128)(2,1)} %copy.63, bf16[128,12,128]{2,1,0:T(8,128)(2,1)} %reshape.104, bf16[16]{0:T(256)(128)(2,1)S(1)} %pad.12.clone), kind=kLoop, calls=%fused_computation.12 | loop fusion | flops 2097152 | bytes 983072 | tf_op jit(solution)/shard_map/concatenate | solution.py:74
  13.2 11.9 %all-to-all-start = ((bf16[128,16,128]{2,1,0:T(8,128)(2,1)}), bf16[128,16,128]{2,1,0:T(8,128)(2,1)}, u32[]{:S(2)}, u32[]{:S(2)}) async-start(bf16[128,16,128]{2,1,0:T(8,128)(2,1)} %maximum_maximum_fusion), calls=%async_computation | async-start | bytes 1048576 | tf_op jit(solution)/shard_map/all_to_all | solution.py:19
  25.3 13.1 %all-to-all-done = bf16[128,16,128]{2,1,0:T(8,128)(2,1)} async-done(((bf16[128,16,128]{2,1,0:T(8,128)(2,1)}), bf16[128,16,128]{2,1,0:T(8,128)(2,1)}, u32[]{:S(2)}, u32[]{:S(2)}) %all-to-all-start) | async-done | bytes 524320 | tf_op jit(solution)/shard_map/all_to_all | solution.py:19
  38.4 1.1 %copy.65 = bf16[128,12,128]{2,0,1:T(8,128)(2,1)S(1)} copy(bf16[128,12,128]{2,1,0:T(8,128)(2,1)} %bitcast.52) | data formatting | bytes 786432 | tf_op jit(solution)/shard_map/slice | solution.py:79
  39.5 0.3 copy.66
  39.8 1.6 %fusion = f32[3,128,512]{1,2,0:T(8,128)S(1)} fusion(bf16[3,512,128]{2,1,0:T(8,128)(2,1)S(1)} %bitcast.53, f32[1,3,512,512]{3,2,1,0:T(8,128)S(1)} %copy-done), kind=kOutput, calls=%fused_computation.3 | convolution fusion | flops 1207959552 | bytes 4325376 | tf_op jit(solution)/shard_map/cij,cjb->cib/dot_general | solution.py:102
  41.4 1.8 %multiply_reduce_fusion = (f32[3]{0:T(128)S(1)}, f32[3,512,128]{2,1,0:T(8,128)S(1)}) fusion(f32[3,128,512]{1,2,0:T(8,128)S(1)} %fusion, f32[1,3,128,128]{3,2,1,0:T(8,128)} %param.17), kind=kOutput, calls=%fused_computation.10 | convolution fusion | flops 302383104 | bytes 1769484 | tf_op jit(solution)/shard_map/cib,cbd->cid/dot_general | solution.py:105
  43.2 1.2 %fusion.13 = f32[3]{0:T(128)S(1)} fusion(bf16[128,16,128]{2,1,0:T(8,128)(2,1)} %all-to-all-done), kind=kLoop, calls=%fused_computation.31 | loop fusion | flops 1533 | bytes 1548 | tf_op jit(solution)/shard_map/reduce_sum | solution.py:85
  44.5 0.1 broadcast_multiply_fusion
  44.6 1.0 %copy.78 = f32[3,128,4,128]{3,2,0,1:T(4,128)} copy(f32[3,128,4,128]{3,2,1,0:T(4,128)S(1)} %bitcast.57) | data formatting | bytes 1572864 | tf_op jit(solution)/shard_map/reshape | solution.py:109
  45.7 5.6 %all-to-all-start.1 = ((f32[128,3,4,128]{3,2,1,0:T(4,128)}), f32[128,3,4,128]{3,2,1,0:T(4,128)}, u32[]{:S(2)}, u32[]{:S(2)}) async-start(f32[128,3,4,128]{3,2,1,0:T(4,128)} %bitcast.56), calls=%async_computation.1 | async-start | bytes 1572864 | tf_op jit(solution)/shard_map/all_to_all | solution.py:19
  51.3 1.4 %add_divide_fusion = (f32[6336]{0:T(1024)}, f32[6336]{0:T(1024)}, f32[6336]{0:T(1024)}) fusion(f32[6336]{0:T(1024)} %param.19, f32[6336]{0:T(1024)} %param.21, f32[6336]{0:T(1024)} %param.20), kind=kLoop, calls=%fused_computation.36 | loop fusion | flops 57024 | bytes 152064 | tf_op jit(solution)/shard_map/div | solution.py:15
  52.7 1.9 %fusion.3 = f32[1,3,128,128]{3,2,1,0:T(8,128)} fusion(f32[1,3,128,128]{3,2,1,0:T(8,128)} %param.15, bf16[3,512,128]{2,1,0:T(8,128)(2,1)S(1)} %bitcast.54), kind=kOutput, calls=%fused_computation.8 | convolution fusion | flops 50380800 | bytes 786432 | tf_op jit(solution)/shard_map/cib,cid->cbd/dot_general | solution.py:98
  54.6 4.1 %bitcast_add_fusion = f32[1,3,512,512]{3,2,1,0:T(8,128)} fusion(f32[1,3,512,512]{3,2,1,0:T(8,128)} %param.14, bf16[3,512,128]{2,1,0:T(8,128)(2,1)S(1)} %bitcast.55), kind=kOutput, calls=%fused_computation.2 | convolution fusion | flops 202113024 | bytes 6684672 | tf_op jit(solution)/shard_map/cib,cjb->cij/dot_general | solution.py:92
  58.8 8.6 %all-to-all-done.1 = f32[128,3,4,128]{3,2,1,0:T(4,128)} async-done(((f32[128,3,4,128]{3,2,1,0:T(4,128)}), f32[128,3,4,128]{3,2,1,0:T(4,128)}, u32[]{:S(2)}, u32[]{:S(2)}) %all-to-all-start.1) | async-done | bytes 786464 | tf_op jit(solution)/shard_map/all_to_all | solution.py:19
  67.4 6.5 %gather_fusion = f32[768,128]{1,0:T(8,128)S(1)} fusion(f32[384,4,128]{2,1,0:T(4,128)} %bitcast.13, s32[768]{0:T(1024)S(1)} %reshape.112), kind=kCustom, calls=%fused_computation | custom fusion | bytes 792576 | tf_op jit(solution)/shard_map/gather | solution.py:112
  73.9 0.9 %reshape.111 = f32[4,4,6144]{2,1,0:T(4,128)} reshape(f32[768,128]{1,0:T(8,128)S(1)} %gather_fusion) | data formatting | bytes 786432 | tf_op jit(solution)/shard_map/reshape | solution.py:114
  (9 shorter events, 0.1 us)
Async XLA Ops:
  0.6 39.2 %copy-start = (f32[1,3,512,512]{3,2,1,0:T(8,128)S(1)}, f32[1,3,512,512]{3,2,1,0:T(8,128)}, u32[]{:S(2)}) copy-start(f32[1,3,512,512]{3,2,1,0:T(8,128)} %param.16) | copy-start | bytes 9437188
  13.2 25.1 %all-to-all-start = ((bf16[128,16,128]{2,1,0:T(8,128)(2,1)}), bf16[128,16,128]{2,1,0:T(8,128)(2,1)}, u32[]{:S(2)}, u32[]{:S(2)}) async-start(bf16[128,16,128]{2,1,0:T(8,128)(2,1)} %maximum_maximum_fusion), calls=%async_computation | async-start | bytes 1048576 | tf_op jit(solution)/shard_map/all_to_all | solution.py:19
  45.7 21.7 %all-to-all-start.1 = ((f32[128,3,4,128]{3,2,1,0:T(4,128)}), f32[128,3,4,128]{3,2,1,0:T(4,128)}, u32[]{:S(2)}, u32[]{:S(2)}) async-start(f32[128,3,4,128]{3,2,1,0:T(4,128)} %bitcast.56), calls=%async_computation.1 | async-start | bytes 1572864 | tf_op jit(solution)/shard_map/all_to_all | solution.py:19

commit v7 on v1

--- a/solution.py
+++ b/solution.py
@@ -37,9 +37,10 @@
     earlier = (owners[:, None] == owners[None, :]) & (positions[None, :] < positions[:, None])
     slot_index = jnp.sum(earlier.astype(jnp.int32), axis=1)
     target = slot_index * devices + owners
+    sent_to = owners * slot_count + slot_index
     places = jnp.arange(slot_count * devices, dtype=jnp.int32)
     picker = (
-        (places[:, None] == target[None, :])
+        (places[:, None] == sent_to[None, :])
         .astype(jnp.bfloat16)
         .reshape(slot_count * devices, layer_count, block_count)
     )
@@ -48,31 +49,38 @@
     adam_part = jnp.sum(
         jnp.square(direction).reshape(layer_count, row_count, block_count, BLOCK), axis=(1, 3)
     )
-    part_by_place = jnp.zeros((slot_count * devices,), jnp.float32).at[target].set(
-        adam_part.reshape(total_blocks)
-    )
-    part_hi = part_by_place.astype(jnp.bfloat16)
-    part_lo = (part_by_place - part_hi.astype(jnp.float32)).astype(jnp.bfloat16)
+    part_hi = adam_part.astype(jnp.bfloat16)
+    part_lo = (adam_part - part_hi.astype(jnp.float32)).astype(jnp.bfloat16)
     lane = jnp.arange(BLOCK, dtype=jnp.int32)
     extra = jnp.where(
-        lane[None, :] == 0,
-        part_hi[:, None],
-        jnp.where(lane[None, :] == 1, part_lo[:, None], jnp.zeros((), jnp.bfloat16)),
-    )[:, None, :]
-    pieces = gradients.reshape(layer_count, row_count, block_count, BLOCK)
+        lane == 0,
+        part_hi[:, :, None],
+        jnp.where(lane == 1, part_lo[:, :, None], jnp.zeros((), jnp.bfloat16)),
+    )[:, None]
+    pieces = jnp.concatenate(
+        [gradients.reshape(layer_count, row_count, block_count, BLOCK), extra], axis=1
+    )
     outgoing = jnp.einsum(
         "qln,lrnb->qrb", picker, pieces, preferred_element_type=jnp.float32
     ).astype(jnp.bfloat16)
-    outgoing = jnp.concatenate([outgoing, extra], axis=1)
-    outgoing = outgoing.reshape(slot_count, devices, row_count + 1, BLOCK)
+    chunk = slot_count * (row_count + 1)
+    chunk_rows = -(-chunk // 16) * 16
+    outgoing = jnp.pad(
+        outgoing.reshape(devices, chunk, BLOCK), ((0, 0), (0, chunk_rows - chunk), (0, 0))
+    )
     incoming = lax.all_to_all(
-        outgoing, ("shard", "tensor"), split_axis=1, concat_axis=1, tiled=True
+        outgoing, ("shard", "tensor"), split_axis=0, concat_axis=0, tiled=True
     )
-    block_grads = incoming[:, :, :row_count, :].reshape(slot_count, devices * row_count, BLOCK)
+    incoming = incoming[:, :chunk].reshape(devices, slot_count, row_count + 1, BLOCK)
+    block_grads = (
+        incoming[:, :, :row_count]
+        .transpose(1, 0, 2, 3)
+        .reshape(slot_count, devices * row_count, BLOCK)
+    )
     adam_sums = jnp.sum(
         incoming[:, :, row_count, 0].astype(jnp.float32)
         + incoming[:, :, row_count, 1].astype(jnp.float32),
-        axis=1,
+        axis=0,
     )
     left_out = (
         stat_left

time: 69.4 us -> 72.2 us (1.040)
  blocking collectives: 26.2 us -> 0 us
  waiting for transfers between devices: 8.53 us -> 22.5 us
  starting transfers between devices: 5.7 us -> 17.6 us
  local copies, waits for them, and re-layouts: 10.9 us -> 15.5 us
  other arithmetic: 7.96 us -> 6.3 us
    all_to_all x1 -> x0, blocking collectives: 26.2 us -> none  [per_device(): lax.all_to_all(outgoing, ('shard', 'tensor'), split_axis=1, concat_axis=1...]
    all_to_all x0 -> x1, waiting for transfers between devices: none -> 12.5 us  [per_device(): lax.all_to_all(outgoing, ('shard', 'tensor'), split_axis=0, concat_axis=0...]
    all_to_all x0 -> x1, starting transfers between devices: none -> 11.9 us  [per_device(): lax.all_to_all(outgoing, ('shard', 'tensor'), split_axis=0, concat_axis=0...]
    reshape x2, local copies, waits for them, and re-layouts: 1.14 us -> 3.22 us  [the longest x1 2.01 us: per_device(): outgoing.reshape(devices, chunk, BLOCK)]
    pad x0 -> x1, local copies, waits for them, and re-layouts: none -> 1.93 us  [per_device(): jnp.pad(outgoing.reshape(devices, chunk, BLOCK), ((0, 0), (0, chunk_rows...]
    all_to_all x1, waiting for transfers between devices: 8.53 us -> 9.93 us  [per_device(): lax.all_to_all(shaped, ('shard', 'tensor'), split_axis=1, concat_axis=1,...]
    convert_element_type x0 -> x1, local copies, waits for them, and re-layouts: none -> 1.24 us  [per_device(): outgoing = jnp.einsum('qln,lrnb->qrb', picker, pieces, preferred_element_...]
    scatter x1 -> x0, local copies, waits for them, and re-layouts: 1.21 us -> none  [per_device(): jnp.zeros((slot_count * devices,), jnp.float32).at[target]]
  transfers between devices with their start and end apart: 1 -> 2, of which waited for: 1 -> 2; matrix products, arithmetic and copies ran while one was open for 11% -> 9% of each run, Pallas kernels for 0% -> 0%
where the time goes in v7:
time: 72.2 us; the launch traced here: 71.6 us
  waiting for transfers between devices  22.5 us (31%)
  starting transfers between devices  17.6 us (24%)
  local copies, waits for them, and re-layouts  15.5 us (21%)
  matrix products  8.96 us (12%)
  other arithmetic  6.3 us (9%)
  between operations  0.86 us (1%)
    all_to_all x1, waiting for transfers between devices, per_device(): lax.all_to_all(outgoing, ('shard', 'tensor'), split_axis=0, concat_axis=0...  12.5 us
    all_to_all x1, starting transfers between devices, per_device(): lax.all_to_all(outgoing, ('shard', 'tensor'), split_axis=0, concat_axis=0...  11.9 us
    all_to_all x1, waiting for transfers between devices, per_device(): lax.all_to_all(shaped, ('shard', 'tensor'), split_axis=1, concat_axis=1,...  9.93 us
    all_to_all x1, starting transfers between devices, per_device(): lax.all_to_all(shaped, ('shard', 'tensor'), split_axis=1, concat_axis=1,...  5.61 us
    dot_general x1, matrix products, per_device(): jnp.einsum('cib,cjb->cij', block_grads, block_grads, preferred_element_ty...  4.12 us
    reduce_sum x2, other arithmetic, per_device(): jnp.sum(jnp.square(direction).reshape(layer_count, row_count, block_count...  2.72 us
    all_to_all x1, local copies, waits for them, and re-layouts, per_device(): lax.all_to_all(shaped, ('shard', 'tensor'), split_axis=1, concat_axis=1,...  2.16 us
    gather x2, local copies, waits for them, and re-layouts, per_device(): jnp.take(returned, target, axis=0)  2.05 us
  transfers between devices with their start and end apart: 2, of which 2 were waited for; matrix products, arithmetic and copies ran while one was open for 9% of the time, Pallas kernels for 0%

profile of v7, /device:TPU:1, one launch (start us, length us, event | category | flops | bytes accessed | tf_op | source)
XLA Modules:
  0.0 71.6 jit_solution(6328696924386219746)
XLA Ops:
  0.6 0.0 copy-start
  0.7 1.2 %reshape.102 = bf16[4,4,48,128]{3,2,1,0:T(8,128)(2,1)S(1)} reshape(bf16[4,4,6144]{2,1,0:T(4,128)(2,1)} %param.11) | data formatting | bytes 393216 | tf_op jit(solution)/shard_map/reshape | solution.py:61
  1.9 2.6 %multiply_reduce_fusion.1 = (f32[4,6144]{1,0:T(4,128)S(1)}, f32[4,4,6144]{2,1,0:T(4,128)}, f32[4,4,6144]{2,1,0:T(4,128)}) fusion(bf16[4,4,6144]{2,1,0:T(4,128)(2,1)} %param.11, f32[4,4,6144]{2,1,0:T(4,128)} %param.13, f32[4,4,6144]{2,1,0:T(4,128)} %param.12), kind=kLoop, calls=%fused_computation.16 | loop fusion | flops 1155072 | bytes 1867776 | tf_op jit(solution)/shard_map/reduce_sum | solution.py:49
  4.5 0.1 bitcast_reduce_fusion
  4.6 0.9 %convert_reduce_fusion = s32[192]{0:T(256)S(1)} fusion(s32[192]{0:T(256)} %param.18), kind=kLoop, calls=%fused_computation.25 | loop fusion | flops 184128 | bytes 1536 | tf_op jit(solution)/shard_map/reduce_sum | solution.py:38
  5.6 0.7 multiply_add_fusion.1
  6.3 0.1 eq.45
  6.4 0.1 select_select_fusion
  6.5 0.5 fusion.2
  6.9 1.2 %copy.58 = bf16[384,5,128]{2,1,0:T(8,128)(2,1)} copy(bf16[384,5,128]{2,0,1:T(8,128)(2,1)S(1)} %fusion.2) | data formatting | bytes 983040 | tf_op jit(solution)/shard_map/convert_element_type | solution.py:65
  8.2 2.0 %reshape.85 = bf16[128,15,128]{2,1,0:T(8,128)(2,1)} reshape(bf16[384,5,128]{2,1,0:T(8,128)(2,1)} %copy.58) | data formatting | bytes 983040 | tf_op jit(solution)/shard_map/reshape | solution.py:69
  10.2 1.9 %pad.4 = bf16[128,16,128]{2,1,0:T(8,128)(2,1)} pad(bf16[128,15,128]{2,1,0:T(8,128)(2,1)} %reshape.85, bf16[]{:T(256)} %constant.10.clone.1), padding=0_0x0_1x0_0 | pad | bytes 1015810 | tf_op jit(solution)/shard_map/jit(_pad)/pad | solution.py:68
  12.1 11.9 %all-to-all-start = ((bf16[128,16,128]{2,1,0:T(8,128)(2,1)}), bf16[128,16,128]{2,1,0:T(8,128)(2,1)}, u32[]{:S(2)}, u32[]{:S(2)}) async-start(bf16[128,16,128]{2,1,0:T(8,128)(2,1)} %pad.4), calls=%async_computation | async-start | bytes 1048576 | tf_op jit(solution)/shard_map/all_to_all | solution.py:71
  24.1 0.6 add_divide_fusion
  24.7 12.5 %all-to-all-done = bf16[128,16,128]{2,1,0:T(8,128)(2,1)} async-done(((bf16[128,16,128]{2,1,0:T(8,128)(2,1)}), bf16[128,16,128]{2,1,0:T(8,128)(2,1)}, u32[]{:S(2)}, u32[]{:S(2)}) %all-to-all-start) | async-done | bytes 524320 | tf_op jit(solution)/shard_map/all_to_all | solution.py:71
  37.3 1.2 %copy.59 = bf16[128,15,128]{2,0,1:T(8,128)(2,1)S(1)} copy(bf16[128,15,128]{2,1,0:T(8,128)(2,1)} %bitcast.44) | data formatting | bytes 983040 | tf_op jit(solution)/shard_map/slice | solution.py:74
  38.5 0.2 add_reduce_fusion
  38.7 0.3 copy.60
  39.0 1.6 %fusion = f32[3,128,512]{1,2,0:T(8,128)S(1)} fusion(bf16[3,512,128]{2,1,0:T(8,128)(2,1)S(1)} %bitcast.45, f32[1,3,512,512]{3,2,1,0:T(8,128)S(1)} %copy-done), kind=kOutput, calls=%fused_computation.2 | convolution fusion | flops 1207959552 | bytes 4325376 | tf_op jit(solution)/shard_map/cij,cjb->cib/dot_general | solution.py:97
  40.6 0.9 %multiply_reduce_fusion = (f32[3]{0:T(128)S(1)}, f32[3,512,128]{2,1,0:T(8,128)S(1)}) fusion(f32[3,128,512]{1,2,0:T(8,128)S(1)} %fusion, f32[1,3,128,128]{3,2,1,0:T(8,128)S(1)} %copy-done.1), kind=kOutput, calls=%fused_computation.8 | convolution fusion | flops 302383104 | bytes 1769484 | tf_op jit(solution)/shard_map/cib,cbd->cid/dot_general | solution.py:100
  41.5 0.1 broadcast_multiply_fusion
  41.7 1.0 %copy.63 = f32[3,128,4,128]{3,2,0,1:T(4,128)} copy(f32[3,128,4,128]{3,2,1,0:T(4,128)S(1)} %bitcast.48) | data formatting | bytes 1572864 | tf_op jit(solution)/shard_map/reshape | solution.py:104
  42.7 5.6 %all-to-all-start.1 = ((f32[3,128,4,128]{3,2,0,1:T(4,128)}), f32[3,128,4,128]{3,2,0,1:T(4,128)}, u32[]{:S(2)}, u32[]{:S(2)}) async-start(f32[3,128,4,128]{3,2,0,1:T(4,128)} %copy.63), calls=%async_computation.1 | async-start | bytes 1572864 | tf_op jit(solution)/shard_map/all_to_all | solution.py:105
  48.3 0.1 broadcast_in_dim.58
  48.4 1.9 %fusion.3 = f32[1,3,128,128]{3,2,1,0:T(8,128)} fusion(f32[1,3,128,128]{3,2,1,0:T(8,128)} %param.15, bf16[3,512,128]{2,1,0:T(8,128)(2,1)S(1)} %bitcast.46), kind=kOutput, calls=%fused_computation.7 | convolution fusion | flops 50380800 | bytes 786432 | tf_op jit(solution)/shard_map/cib,cid->cbd/dot_general | solution.py:93
  50.4 4.1 %bitcast_add_fusion = f32[1,3,512,512]{3,2,1,0:T(8,128)} fusion(f32[1,3,512,512]{3,2,1,0:T(8,128)} %param.14, bf16[3,512,128]{2,1,0:T(8,128)(2,1)S(1)} %bitcast.47), kind=kOutput, calls=%fused_computation.1 | convolution fusion | flops 202113024 | bytes 6684672 | tf_op jit(solution)/shard_map/cib,cjb->cij/dot_general | solution.py:87
  54.5 9.9 %all-to-all-done.1 = f32[3,128,4,128]{3,2,0,1:T(4,128)} async-done(((f32[3,128,4,128]{3,2,0,1:T(4,128)}), f32[3,128,4,128]{3,2,0,1:T(4,128)}, u32[]{:S(2)}, u32[]{:S(2)}) %all-to-all-start.1) | async-done | bytes 786464 | tf_op jit(solution)/shard_map/all_to_all | solution.py:105
  64.4 2.2 %copy.64 = f32[3,128,4,128]{3,2,1,0:T(4,128)} copy(f32[3,128,4,128]{3,2,0,1:T(4,128)} %all-to-all-done.1) | data formatting | bytes 1572864 | tf_op jit(solution)/shard_map/all_to_all | solution.py:105
  66.6 2.0 %gather_fusion = f32[192,4,128]{2,1,0:T(4,128)S(1)} fusion(f32[384,4,128]{2,1,0:T(4,128)} %bitcast.51, s32[1024]{0:T(1024)S(1)} %pad_clamp_fusion), kind=kCustom, calls=%fused_computation | custom fusion | bytes 787200 | tf_op jit(solution)/shard_map/jit(_take)/gather | solution.py:107
  68.6 0.8 %select_bitcast_fusion = f32[4,4,48,128]{3,2,0,1:T(8,128)} fusion(f32[4,48,4,128]{3,1,0,2:T(8,128)S(1)} %bitcast.52, pred[4,48]{1,0:T(4,128)(4,1)S(1)} %broadcast_in_dim.58), kind=kLoop, calls=%fused_computation.14 | loop fusion | flops 98304 | bytes 786624 | tf_op jit(solution)/shard_map/transpose | solution.py:110
  69.5 1.1 %reshape.90 = f32[4,4,6144]{2,0,1:T(4,128)S(1)} reshape(f32[4,4,48,128]{3,2,0,1:T(8,128)} %select_bitcast_fusion) | data formatting | bytes 786432 | tf_op jit(solution)/shard_map/reshape | solution.py:110
  70.6 1.0 %copy.67 = f32[4,4,6144]{2,1,0:T(4,128)} copy(f32[4,4,6144]{2,0,1:T(4,128)S(1)} %reshape.90) | data formatting | bytes 786432
  (18 shorter events, 0.1 us)
Async XLA Ops:
  0.6 38.4 %copy-start = (f32[1,3,512,512]{3,2,1,0:T(8,128)S(1)}, f32[1,3,512,512]{3,2,1,0:T(8,128)}, u32[]{:S(2)}) copy-start(f32[1,3,512,512]{3,2,1,0:T(8,128)} %param.16) | copy-start | bytes 9437188
  4.5 19.6 %copy-start.2 = (f32[6336]{0:T(1024)S(1)}, f32[6336]{0:T(1024)}, u32[]{:S(2)}) copy-start(f32[6336]{0:T(1024)} %param.19) | copy-start | bytes 76036
  4.5 19.6 %copy-start.3 = (f32[6336]{0:T(1024)S(1)}, f32[6336]{0:T(1024)}, u32[]{:S(2)}) copy-start(f32[6336]{0:T(1024)} %param.21) | copy-start | bytes 76036
  4.5 19.6 %copy-start.4 = (f32[6336]{0:T(1024)S(1)}, f32[6336]{0:T(1024)}, u32[]{:S(2)}) copy-start(f32[6336]{0:T(1024)} %param.20) | copy-start | bytes 76036
  12.1 25.1 %all-to-all-start = ((bf16[128,16,128]{2,1,0:T(8,128)(2,1)}), bf16[128,16,128]{2,1,0:T(8,128)(2,1)}, u32[]{:S(2)}, u32[]{:S(2)}) async-start(bf16[128,16,128]{2,1,0:T(8,128)(2,1)} %pad.4), calls=%async_computation | async-start | bytes 1048576 | tf_op jit(solution)/shard_map/all_to_all | solution.py:71
  38.5 2.1 %copy-start.1 = (f32[1,3,128,128]{3,2,1,0:T(8,128)S(1)}, f32[1,3,128,128]{3,2,1,0:T(8,128)}, u32[]{:S(2)}) copy-start(f32[1,3,128,128]{3,2,1,0:T(8,128)} %param.17) | copy-start | bytes 589828
  40.6 7.7 %copy-start.5 = (s32[192]{0:T(256)S(1)}, s32[192]{0:T(256)}, u32[]{:S(2)}) copy-start(s32[192]{0:T(256)} %param.18) | copy-start | bytes 2308
  42.7 21.7 %all-to-all-start.1 = ((f32[3,128,4,128]{3,2,0,1:T(4,128)}), f32[3,128,4,128]{3,2,0,1:T(4,128)}, u32[]{:S(2)}, u32[]{:S(2)}) async-start(f32[3,128,4,128]{3,2,0,1:T(4,128)} %copy.63), calls=%async_computation.1 | async-start | bytes 1572864 | tf_op jit(solution)/shard_map/all_to_all | solution.py:105

commit v8 on v1

--- a/solution.py
+++ b/solution.py
@@ -95,11 +95,15 @@
     scaled = precond * graft_ratio[:, None, None]
     shaped = scaled.reshape(slot_count, devices, row_count, BLOCK)
     returned = lax.all_to_all(shaped, ("shard", "tensor"), split_axis=1, concat_axis=1, tiled=True)
-    returned = returned.reshape(slot_count * devices, row_count, BLOCK)
-    own_rows = jnp.take(returned, target, axis=0).reshape(
-        layer_count, block_count, row_count, BLOCK
+    placer = (
+        (target[:, None] == places[None, :])
+        .astype(jnp.float32)
+        .reshape(layer_count, block_count, slot_count, devices)
     )
-    updates = own_rows.transpose(0, 2, 1, 3).reshape(layer_count, row_count, col_count)
+    updates = jnp.einsum(
+        "lnqd,qdrb->lrnb", placer, returned, precision=PRECISE,
+        preferred_element_type=jnp.float32,
+    ).reshape(layer_count, row_count, col_count)
     small_mean_out, small_square_out, small_update = adam_moments(
         small_grad, small_mean, small_square
     )

time: 69.4 us -> 70.4 us (1.014)
  matrix products: 8.9 us -> 12.3 us
  local copies, waits for them, and re-layouts: 10.9 us -> 8.45 us
    dot_general x0 -> x1, matrix products: none -> 2.44 us  [per_device(): jnp.einsum('lnqd,qdrb->lrnb', placer, returned, precision=PRECISE, prefer...]
    all_to_all x1 -> x0, local copies, waits for them, and re-layouts: 2.17 us -> none  [per_device(): lax.all_to_all(shaped, ('shard', 'tensor'), split_axis=1, concat_axis=1,...]
    gather x2 -> x0, local copies, waits for them, and re-layouts: 2.05 us -> none  [per_device(): jnp.take(returned, target, axis=0)]
    dot_general x1, matrix products: 0.39 us -> 1.32 us  [per_device(): jnp.einsum('qln,lrnb->qrb', picker, pieces, preferred_element_type=jnp.fl...]
    transpose x1 -> x0, other arithmetic: 0.84 us -> none  [per_device(): own_rows.transpose(0, 2, 1, 3).reshape(layer_count, row_count, col_count)]
    select_n x1, other arithmetic: 0.34 us -> 1.11 us  [per_device(): jnp.where(lane[None, :] == 0, part_hi[:, None], jnp.where(lane[None, :] =...]
where the time goes in v8:
time: 70.4 us; the launch traced here: 69.8 us
  blocking collectives  26.2 us (37%)
  matrix products  12.3 us (17%)
  waiting for transfers between devices  8.62 us (12%)
  local copies, waits for them, and re-layouts  8.45 us (12%)
  other arithmetic  7.89 us (11%)
  starting transfers between devices  5.7 us (8%)
  between operations  0.77 us (1%)
    all_to_all x1, blocking collectives, per_device(): lax.all_to_all(outgoing, ('shard', 'tensor'), split_axis=1, concat_axis=1...  26.2 us
    all_to_all x1, waiting for transfers between devices, per_device(): lax.all_to_all(shaped, ('shard', 'tensor'), split_axis=1, concat_axis=1,...  8.62 us
    all_to_all x1, starting transfers between devices, per_device(): lax.all_to_all(shaped, ('shard', 'tensor'), split_axis=1, concat_axis=1,...  5.7 us
    dot_general x1, matrix products, per_device(): jnp.einsum('cib,cjb->cij', block_grads, block_grads, preferred_element_ty...  4.13 us
    reduce_sum x2, other arithmetic, per_device(): jnp.sum(jnp.square(direction).reshape(layer_count, row_count, block_count...  2.71 us
    dot_general x1, matrix products, per_device(): jnp.einsum('lnqd,qdrb->lrnb', placer, returned, precision=PRECISE, prefer...  2.44 us
    dot_general x1, matrix products, per_device(): jnp.einsum('cib,cid->cbd', block_grads, block_grads, preferred_element_ty...  1.92 us
    reshape x1, local copies, waits for them, and re-layouts, per_device(): pieces = gradients.reshape(layer_count, row_count, block_count, BLOCK)  1.73 us
  transfers between devices with their start and end apart: 1, of which 1 were waited for; matrix products, arithmetic and copies ran while one was open for 11% of the time, Pallas kernels for 0%

profile of v8, /device:TPU:1, one launch (start us, length us, event | category | flops | bytes accessed | tf_op | source)
XLA Modules:
  0.0 69.8 jit_solution(1928782829444000011)
XLA Ops:
  0.6 0.0 copy-start
  0.7 1.0 %convert_reduce_fusion = s32[192]{0:T(256)S(1)} fusion(s32[192]{0:T(256)} %param.18), kind=kLoop, calls=%fused_computation.25 | loop fusion | flops 184128 | bytes 1536 | tf_op jit(solution)/shard_map/reduce_sum | solution.py:38
  1.7 0.7 compare_select_fusion
  2.4 1.7 %reshape.136 = bf16[4,4,48,128]{3,2,1,0:T(8,128)(2,1)} reshape(bf16[4,4,6144]{2,1,0:T(4,128)(2,1)} %param.11) | data formatting | bytes 393216 | tf_op jit(solution)/shard_map/reshape | solution.py:62
  4.1 2.6 %multiply_reduce_fusion.1 = (f32[4,6144]{1,0:T(4,128)S(1)}, f32[4,4,6144]{2,1,0:T(4,128)}, f32[4,4,6144]{2,1,0:T(4,128)}) fusion(bf16[4,4,6144]{2,1,0:T(4,128)(2,1)} %param.11, f32[4,4,6144]{2,1,0:T(4,128)} %param.13, f32[4,4,6144]{2,1,0:T(4,128)} %param.12), kind=kLoop, calls=%fused_computation.17 | loop fusion | flops 1155072 | bytes 1867776 | tf_op jit(solution)/shard_map/reduce_sum | solution.py:48
  6.7 0.1 bitcast_reduce_fusion
  6.8 0.1 reshape.145
  6.9 1.2 %scatter_custom_fusion = f32[384]{0:T(512)S(1)} fusion(s32[192]{0:T(256)S(1)} %get-tuple-element.62, f32[192]{0:T(256)S(1)} %reshape.145, f32[]{:T(128)} %constant.14.clone.1), kind=kCustom, calls=%fused_computation.41 | custom fusion | bytes 1540 | tf_op jit(solution)/shard_map/scatter | solution.py:51
  8.1 0.7 %copy.67 = bf16[3,128]{0,1:T(8,128)(2,1)} copy(bf16[3,128]{1,0:T(4,128)(2,1)S(1)} %get-tuple-element.65) | data formatting | bytes 1536 | tf_op jit(solution)/shard_map/jit(_where)/broadcast_in_dim | solution.py:60
  8.9 0.7 %copy.66 = bf16[3,128]{0,1:T(8,128)(2,1)} copy(bf16[3,128]{1,0:T(4,128)(2,1)S(1)} %get-tuple-element.64) | data formatting | bytes 1536 | tf_op jit(solution)/shard_map/jit(_where)/broadcast_in_dim | solution.py:57
  9.6 0.1 eq.90
  9.7 1.3 %fusion.2 = bf16[384,4,128]{2,0,1:T(8,128)(2,1)S(1)} fusion(bf16[4,4,48,128]{3,2,1,0:T(8,128)(2,1)} %reshape.136, s32[4,48]{1,0:T(4,128)S(1)} %eq.90), kind=kOutput, calls=%fused_computation.5 | convolution fusion | flops 75767808 | bytes 590592 | tf_op jit(solution)/shard_map/qln,lrnb->qrb/dot_general | solution.py:63
  11.0 0.3 copy.68
  11.4 1.1 %select_select_fusion = bf16[3,128,1,128]{3,0,2,1:T(4,128)(2,1)S(1)} fusion(pred[128]{0:T(512)(128)(4,1)S(1)} %get-tuple-element.68, pred[128]{0:T(512)(128)(4,1)S(1)} %get-tuple-element.69, bf16[3,128]{0,1:T(8,128)(2,1)} %copy.67, bf16[3,128]{0,1:T(8,128)(2,1)} %copy.66), kind=kLoop, calls=%fused_computation.31 | loop fusion | flops 98304 | bytes 100096 | tf_op jit(solution)/shard_map/jit(_where)/select_n | solution.py:57
  12.5 0.4 pad_maximum_fusion
  12.9 26.2 %all_to_all.10 = bf16[3,128,5,128]{3,0,2,1:T(4,128)(2,1)S(1)} all-to-all(bf16[3,128,5,128]{3,0,2,1:T(4,128)(2,1)S(1)} %pad_maximum_fusion), channel_id=1, replica_groups=mesh['shard'=16,'tensor'=8] {'shard','tensor'}, dimensions={1} | all-to-all | bytes 983040 | tf_op jit(solution)/shard_map/all_to_all | solution.py:68
  39.1 0.2 slice.12
  39.3 0.2 copy.69
  39.5 0.0 copy-done
  39.5 1.6 %fusion = f32[3,128,512]{1,2,0:T(8,128)S(1)} fusion(bf16[3,512,128]{2,1,0:T(8,128)(2,1)S(1)} %bitcast.57, f32[1,3,512,512]{3,2,1,0:T(8,128)S(1)} %copy-done), kind=kOutput, calls=%fused_computation.2 | convolution fusion | flops 1207959552 | bytes 4325376 | tf_op jit(solution)/shard_map/cij,cjb->cib/dot_general | solution.py:89
  41.0 0.9 %multiply_reduce_fusion = (f32[3]{0:T(128)S(1)}, f32[3,512,128]{2,1,0:T(8,128)S(1)}) fusion(f32[3,128,512]{1,2,0:T(8,128)S(1)} %fusion, f32[1,3,128,128]{3,2,1,0:T(8,128)S(1)} %copy-done.1), kind=kOutput, calls=%fused_computation.10 | convolution fusion | flops 302383104 | bytes 1769484 | tf_op jit(solution)/shard_map/cib,cbd->cid/dot_general | solution.py:92
  41.9 0.3 add_reduce_fusion
  42.3 0.1 broadcast_multiply_fusion
  42.4 1.0 %copy.72 = f32[3,128,4,128]{3,2,0,1:T(4,128)} copy(f32[3,128,4,128]{3,2,1,0:T(4,128)S(1)} %bitcast.60) | data formatting | bytes 1572864 | tf_op jit(solution)/shard_map/reshape | solution.py:96
  43.5 5.7 %all-to-all-start.1 = ((f32[3,128,4,128]{3,2,0,1:T(4,128)}), f32[3,128,4,128]{3,2,0,1:T(4,128)}, u32[]{:S(2)}, u32[]{:S(2)}) async-start(f32[3,128,4,128]{3,2,0,1:T(4,128)} %copy.72), calls=%async_computation.1 | async-start | bytes 1572864 | tf_op jit(solution)/shard_map/all_to_all | solution.py:97
  49.2 1.4 %add_divide_fusion = (f32[6336]{0:T(1024)}, f32[6336]{0:T(1024)}, f32[6336]{0:T(1024)}) fusion(f32[6336]{0:T(1024)} %param.19, f32[6336]{0:T(1024)} %param.21, f32[6336]{0:T(1024)} %param.20), kind=kLoop, calls=%fused_computation.35 | loop fusion | flops 57024 | bytes 152064 | tf_op jit(solution)/shard_map/div | solution.py:15
  50.6 1.9 %fusion.3 = f32[1,3,128,128]{3,2,1,0:T(8,128)} fusion(f32[1,3,128,128]{3,2,1,0:T(8,128)} %param.15, bf16[3,512,128]{2,1,0:T(8,128)(2,1)S(1)} %bitcast.58), kind=kOutput, calls=%fused_computation.8 | convolution fusion | flops 50380800 | bytes 786432 | tf_op jit(solution)/shard_map/cib,cid->cbd/dot_general | solution.py:85
  52.5 4.1 %bitcast_add_fusion = f32[1,3,512,512]{3,2,1,0:T(8,128)} fusion(f32[1,3,512,512]{3,2,1,0:T(8,128)} %param.14, bf16[3,512,128]{2,1,0:T(8,128)(2,1)S(1)} %bitcast.59), kind=kOutput, calls=%fused_computation.1 | convolution fusion | flops 202113024 | bytes 6684672 | tf_op jit(solution)/shard_map/cib,cjb->cij/dot_general | solution.py:79
  56.6 8.6 %all-to-all-done.1 = f32[3,128,4,128]{3,2,0,1:T(4,128)} async-done(((f32[3,128,4,128]{3,2,0,1:T(4,128)}), f32[3,128,4,128]{3,2,0,1:T(4,128)}, u32[]{:S(2)}, u32[]{:S(2)}) %all-to-all-start.1) | async-done | bytes 786464 | tf_op jit(solution)/shard_map/all_to_all | solution.py:97
  65.3 2.4 %convolution_bitcast_fusion.1 = f32[4,4,48,128]{3,2,0,1:T(8,128)} fusion(f32[3,128,4,128,1]{3,2,0,1,4:T(4,128)} %bitcast.11, s32[3,128]{1,0:T(4,128)S(1)} %multiply_add_fusion.1, s32[4,48]{1,0:T(4,128)S(1)} %eq.90), kind=kOutput, calls=%fused_computation.6 | convolution fusion | flops 453058560 | bytes 1181952 | tf_op jit(solution)/shard_map/lnqd,qdrb->lrnb/dot_general | solution.py:103
  67.7 1.1 %reshape.140 = f32[4,4,6144]{2,0,1:T(4,128)S(1)} reshape(f32[4,4,48,128]{3,2,0,1:T(8,128)} %convolution_bitcast_fusion.1) | data formatting | bytes 786432 | tf_op jit(solution)/shard_map/reshape | solution.py:106
  68.8 1.0 %copy.75 = f32[4,4,6144]{2,1,0:T(4,128)} copy(f32[4,4,6144]{2,0,1:T(4,128)S(1)} %reshape.140) | data formatting | bytes 786432
  (6 shorter events, 0.0 us)
Async XLA Ops:
  0.6 38.8 %copy-start = (f32[1,3,512,512]{3,2,1,0:T(8,128)S(1)}, f32[1,3,512,512]{3,2,1,0:T(8,128)}, u32[]{:S(2)}) copy-start(f32[1,3,512,512]{3,2,1,0:T(8,128)} %param.16) | copy-start | bytes 9437188
  39.1 2.0 %copy-start.1 = (f32[1,3,128,128]{3,2,1,0:T(8,128)S(1)}, f32[1,3,128,128]{3,2,1,0:T(8,128)}, u32[]{:S(2)}) copy-start(f32[1,3,128,128]{3,2,1,0:T(8,128)} %param.17) | copy-start | bytes 589828
  43.5 21.8 %all-to-all-start.1 = ((f32[3,128,4,128]{3,2,0,1:T(4,128)}), f32[3,128,4,128]{3,2,0,1:T(4,128)}, u32[]{:S(2)}, u32[]{:S(2)}) async-start(f32[3,128,4,128]{3,2,0,1:T(4,128)} %copy.72), calls=%async_computation.1 | async-start | bytes 1572864 | tf_op jit(solution)/shard_map/all_to_all | solution.py:97

commit v9 on v8

--- a/solution.py
+++ b/solution.py
@@ -95,11 +95,12 @@
     scaled = precond * graft_ratio[:, None, None]
     shaped = scaled.reshape(slot_count, devices, row_count, BLOCK)
     returned = lax.all_to_all(shaped, ("shard", "tensor"), split_axis=1, concat_axis=1, tiled=True)
+    slot_ids = jnp.arange(slot_count, dtype=jnp.int32)
+    device_ids = jnp.arange(devices, dtype=jnp.int32)
     placer = (
-        (target[:, None] == places[None, :])
-        .astype(jnp.float32)
-        .reshape(layer_count, block_count, slot_count, devices)
-    )
+        (slot_index[:, None, None] == slot_ids[None, :, None])
+        & (owners[:, None, None] == device_ids[None, None, :])
+    ).astype(jnp.float32).reshape(layer_count, block_count, slot_count, devices)
     updates = jnp.einsum(
         "lnqd,qdrb->lrnb", placer, returned, precision=PRECISE,
         preferred_element_type=jnp.float32,

time: 70.4 us -> 69.9 us (level)
  blocking collectives: 26.2 us -> 0 us
  waiting for transfers between devices: 8.62 us -> 23.1 us
  starting transfers between devices: 5.7 us -> 17.6 us
  matrix products: 12.3 us -> 11.3 us
  other arithmetic: 7.89 us -> 8.84 us
    all_to_all x1 -> x0, blocking collectives: 26.2 us -> none  [per_device(): lax.all_to_all(outgoing, ('shard', 'tensor'), split_axis=1, concat_axis=1...]
    all_to_all x0 -> x1, waiting for transfers between devices: none -> 13 us  [per_device(): lax.all_to_all(outgoing, ('shard', 'tensor'), split_axis=1, concat_axis=1...]
    all_to_all x0 -> x1, starting transfers between devices: none -> 11.9 us  [per_device(): lax.all_to_all(outgoing, ('shard', 'tensor'), split_axis=1, concat_axis=1...]
    all_to_all x1, waiting for transfers between devices: 8.62 us -> 10 us  [per_device(): lax.all_to_all(shaped, ('shard', 'tensor'), split_axis=1, concat_axis=1,...]
    slice x2, local copies, waits for them, and re-layouts: 0.35 us -> 1.43 us  [per_device(): incoming[:, :, :row_count, :]]
    reduce_sum x1, other arithmetic: 0.32 us -> 1.3 us  [per_device(): jnp.sum(incoming[:, :, row_count, 0].astype(jnp.float32) + incoming[:, :,...]
    dot_general x1, matrix products: 1.32 us -> 0.4 us  [per_device(): jnp.einsum('qln,lrnb->qrb', picker, pieces, preferred_element_type=jnp.fl...]
    concatenate x1, other arithmetic: 0.44 us -> 1.28 us  [per_device(): outgoing = jnp.concatenate([outgoing, extra], axis=1)]
  transfers between devices with their start and end apart: 1 -> 2, of which waited for: 1 -> 2; matrix products, arithmetic and copies ran while one was open for 11% -> 11% of each run, Pallas kernels for 0% -> 0%
where the time goes in v9:
time: 69.9 us; the launch traced here: 69.5 us
  waiting for transfers between devices  23.1 us (33%)
  starting transfers between devices  17.6 us (25%)
  matrix products  11.3 us (16%)
  other arithmetic  8.84 us (13%)
  local copies, waits for them, and re-layouts  7.84 us (11%)
  between operations  0.82 us (1%)
    all_to_all x1, waiting for transfers between devices, per_device(): lax.all_to_all(outgoing, ('shard', 'tensor'), split_axis=1, concat_axis=1...  13 us
    all_to_all x1, starting transfers between devices, per_device(): lax.all_to_all(outgoing, ('shard', 'tensor'), split_axis=1, concat_axis=1...  11.9 us
    all_to_all x1, waiting for transfers between devices, per_device(): lax.all_to_all(shaped, ('shard', 'tensor'), split_axis=1, concat_axis=1,...  10 us
    all_to_all x1, starting transfers between devices, per_device(): lax.all_to_all(shaped, ('shard', 'tensor'), split_axis=1, concat_axis=1,...  5.7 us
    dot_general x1, matrix products, per_device(): jnp.einsum('cib,cjb->cij', block_grads, block_grads, preferred_element_ty...  4.13 us
    reduce_sum x2, other arithmetic, per_device(): jnp.sum(jnp.square(direction).reshape(layer_count, row_count, block_count...  2.72 us
    dot_general x1, matrix products, per_device(): jnp.einsum('lnqd,qdrb->lrnb', placer, returned, precision=PRECISE, prefer...  2.43 us
    dot_general x1, matrix products, per_device(): jnp.einsum('cib,cid->cbd', block_grads, block_grads, preferred_element_ty...  1.92 us
  transfers between devices with their start and end apart: 2, of which 2 were waited for; matrix products, arithmetic and copies ran while one was open for 11% of the time, Pallas kernels for 0%

profile of v9, /device:TPU:1, one launch (start us, length us, event | category | flops | bytes accessed | tf_op | source)
XLA Modules:
  0.0 69.5 jit_solution(640867559436003097)
XLA Ops:
  0.7 1.0 %convert_reduce_fusion = s32[192]{0:T(256)S(1)} fusion(s32[192]{0:T(256)} %param.18), kind=kLoop, calls=%fused_computation.25 | loop fusion | flops 184128 | bytes 1536 | tf_op jit(solution)/shard_map/reduce_sum | solution.py:38
  1.7 0.7 compare_select_fusion
  2.4 1.1 %reshape.173 = bf16[4,4,48,128]{3,2,1,0:T(8,128)(2,1)S(1)} reshape(bf16[4,4,6144]{2,1,0:T(4,128)(2,1)} %param.11) | data formatting | bytes 393216 | tf_op jit(solution)/shard_map/reshape | solution.py:62
  3.5 2.6 %multiply_reduce_fusion.1 = (f32[4,6144]{1,0:T(4,128)S(1)}, f32[4,4,6144]{2,1,0:T(4,128)}, f32[4,4,6144]{2,1,0:T(4,128)}) fusion(bf16[4,4,6144]{2,1,0:T(4,128)(2,1)} %param.11, f32[4,4,6144]{2,1,0:T(4,128)} %param.13, f32[4,4,6144]{2,1,0:T(4,128)} %param.12), kind=kLoop, calls=%fused_computation.17 | loop fusion | flops 1155072 | bytes 1867776 | tf_op jit(solution)/shard_map/reduce_sum | solution.py:48
  6.1 0.1 bitcast_reduce_fusion
  6.3 1.2 %scatter_custom_fusion = f32[384]{0:T(512)S(1)} fusion(s32[192]{0:T(256)S(1)} %get-tuple-element.62, f32[192]{0:T(256)S(1)} %reshape.182, f32[]{:T(128)} %constant.14.clone.1), kind=kCustom, calls=%fused_computation.42 | custom fusion | bytes 1540 | tf_op jit(solution)/shard_map/scatter | solution.py:51
  7.5 0.1 copy.67
  7.7 0.1 copy.66
  7.9 0.4 fusion.2
  8.3 0.3 copy.68
  8.6 0.3 select_select_fusion
  9.0 1.3 %pad_maximum_fusion = bf16[3,128,5,128]{3,0,2,1:T(4,128)(2,1)} fusion(bf16[3,128,1,128]{3,0,2,1:T(4,128)(2,1)S(1)} %select_select_fusion, bf16[3,128,4,128]{3,0,2,1:T(4,128)(2,1)S(1)} %copy.68), kind=kLoop, calls=%fused_computation.11 | loop fusion | flops 245760 | bytes 983040 | tf_op jit(solution)/shard_map/concatenate | solution.py:66
  10.2 11.9 %all-to-all-start = ((bf16[3,128,5,128]{3,0,2,1:T(4,128)(2,1)}), bf16[3,128,5,128]{3,0,2,1:T(4,128)(2,1)}, u32[]{:S(2)}, u32[]{:S(2)}) async-start(bf16[3,128,5,128]{3,0,2,1:T(4,128)(2,1)} %pad_maximum_fusion), calls=%async_computation | async-start | bytes 1310720 | tf_op jit(solution)/shard_map/all_to_all | solution.py:68
  22.2 0.1 eq.122
  22.2 0.1 eq.118
  22.3 0.7 %iota_compare_fusion.2 = pred[4,48,128]{2,1,0:T(8,128)(4,1)} fusion(s32[4,48]{1,0:T(4,128)S(1)} %eq.122), kind=kLoop, calls=%fused_computation.33 | loop fusion | flops 24576 | bytes 25344 | tf_op jit(solution)/shard_map/eq | solution.py:102
  23.0 0.6 add_divide_fusion
  23.7 13.0 %all-to-all-done = bf16[3,128,5,128]{3,0,2,1:T(4,128)(2,1)} async-done(((bf16[3,128,5,128]{3,0,2,1:T(4,128)(2,1)}), bf16[3,128,5,128]{3,0,2,1:T(4,128)(2,1)}, u32[]{:S(2)}, u32[]{:S(2)}) %all-to-all-start) | async-done | bytes 491552 | tf_op jit(solution)/shard_map/all_to_all | solution.py:68
  36.7 1.3 %slice.12 = bf16[3,128,4,128]{3,0,2,1:T(4,128)(2,1)S(1)} slice(bf16[3,128,5,128]{3,0,2,1:T(4,128)(2,1)} %all-to-all-done), slice={[0:3], [0:128], [0:4], [0:128]} | slice | bytes 786432 | tf_op jit(solution)/shard_map/slice | solution.py:71
  38.0 0.2 copy.69
  38.2 1.6 %fusion = f32[3,128,512]{1,2,0:T(8,128)S(1)} fusion(bf16[3,512,128]{2,1,0:T(8,128)(2,1)S(1)} %bitcast.57, f32[1,3,512,512]{3,2,1,0:T(8,128)S(1)} %copy-done), kind=kOutput, calls=%fused_computation.2 | convolution fusion | flops 1207959552 | bytes 4325376 | tf_op jit(solution)/shard_map/cij,cjb->cib/dot_general | solution.py:89
  39.8 0.9 %multiply_reduce_fusion = (f32[3]{0:T(128)S(1)}, f32[3,512,128]{2,1,0:T(8,128)S(1)}) fusion(f32[3,128,512]{1,2,0:T(8,128)S(1)} %fusion, f32[1,3,128,128]{3,2,1,0:T(8,128)S(1)} %copy-done.1), kind=kOutput, calls=%fused_computation.10 | convolution fusion | flops 302383104 | bytes 1769484 | tf_op jit(solution)/shard_map/cib,cbd->cid/dot_general | solution.py:92
  40.6 1.3 %add_reduce_fusion = f32[3]{0:T(128)S(1)} fusion(bf16[3,128,5,128]{3,0,2,1:T(4,128)(2,1)} %all-to-all-done), kind=kLoop, calls=%fused_computation.22 | loop fusion | flops 1533 | bytes 1548 | tf_op jit(solution)/shard_map/reduce_sum | solution.py:72
  42.0 0.1 broadcast_multiply_fusion
  42.1 1.0 %copy.72 = f32[3,128,4,128]{3,2,0,1:T(4,128)} copy(f32[3,128,4,128]{3,2,1,0:T(4,128)S(1)} %bitcast.60) | data formatting | bytes 1572864 | tf_op jit(solution)/shard_map/reshape | solution.py:96
  43.1 5.7 %all-to-all-start.1 = ((f32[3,128,4,128]{3,2,0,1:T(4,128)}), f32[3,128,4,128]{3,2,0,1:T(4,128)}, u32[]{:S(2)}, u32[]{:S(2)}) async-start(f32[3,128,4,128]{3,2,0,1:T(4,128)} %copy.72), calls=%async_computation.1 | async-start | bytes 1572864 | tf_op jit(solution)/shard_map/all_to_all | solution.py:97
  48.9 1.9 %fusion.3 = f32[1,3,128,128]{3,2,1,0:T(8,128)} fusion(f32[1,3,128,128]{3,2,1,0:T(8,128)} %param.15, bf16[3,512,128]{2,1,0:T(8,128)(2,1)S(1)} %bitcast.58), kind=kOutput, calls=%fused_computation.8 | convolution fusion | flops 50380800 | bytes 786432 | tf_op jit(solution)/shard_map/cib,cid->cbd/dot_general | solution.py:85
  50.8 4.1 %bitcast_add_fusion = f32[1,3,512,512]{3,2,1,0:T(8,128)} fusion(f32[1,3,512,512]{3,2,1,0:T(8,128)} %param.14, bf16[3,512,128]{2,1,0:T(8,128)(2,1)S(1)} %bitcast.59), kind=kOutput, calls=%fused_computation.1 | convolution fusion | flops 202113024 | bytes 6684672 | tf_op jit(solution)/shard_map/cib,cjb->cij/dot_general | solution.py:79
  54.9 10.0 %all-to-all-done.1 = f32[3,128,4,128]{3,2,0,1:T(4,128)} async-done(((f32[3,128,4,128]{3,2,0,1:T(4,128)}), f32[3,128,4,128]{3,2,0,1:T(4,128)}, u32[]{:S(2)}, u32[]{:S(2)}) %all-to-all-start.1) | async-done | bytes 786464 | tf_op jit(solution)/shard_map/all_to_all | solution.py:97
  64.9 2.4 %convolution_bitcast_fusion.1 = f32[4,4,48,128]{3,2,0,1:T(8,128)} fusion(f32[3,128,4,128,1]{3,2,0,1,4:T(4,128)} %bitcast.11, pred[4,48,128]{2,1,0:T(8,128)(4,1)} %iota_compare_fusion.2, pred[4,48,3]{1,2,0:T(4,128)(4,1)S(1)} %iota_compare_fusion.3), kind=kOutput, calls=%fused_computation.6 | convolution fusion | flops 453058560 | bytes 1204800 | tf_op jit(solution)/shard_map/lnqd,qdrb->lrnb/dot_general | solution.py:104
  67.4 1.1 %reshape.177 = f32[4,4,6144]{2,0,1:T(4,128)S(1)} reshape(f32[4,4,48,128]{3,2,0,1:T(8,128)} %convolution_bitcast_fusion.1) | data formatting | bytes 786432 | tf_op jit(solution)/shard_map/reshape | solution.py:107
  68.5 1.0 %copy.75 = f32[4,4,6144]{2,1,0:T(4,128)} copy(f32[4,4,6144]{2,0,1:T(4,128)S(1)} %reshape.177) | data formatting | bytes 786432
  (18 shorter events, 0.2 us)
Async XLA Ops:
  0.6 37.5 %copy-start = (f32[1,3,512,512]{3,2,1,0:T(8,128)S(1)}, f32[1,3,512,512]{3,2,1,0:T(8,128)}, u32[]{:S(2)}) copy-start(f32[1,3,512,512]{3,2,1,0:T(8,128)} %param.16) | copy-start | bytes 9437188
  3.4 18.7 %copy-start.5 = (s32[192]{0:T(256)S(1)}, s32[192]{0:T(256)}, u32[]{:S(2)}) copy-start(s32[192]{0:T(256)} %param.18) | copy-start | bytes 2308
  3.4 19.6 %copy-start.2 = (f32[6336]{0:T(1024)S(1)}, f32[6336]{0:T(1024)}, u32[]{:S(2)}) copy-start(f32[6336]{0:T(1024)} %param.19) | copy-start | bytes 76036
  3.5 19.6 %copy-start.3 = (f32[6336]{0:T(1024)S(1)}, f32[6336]{0:T(1024)}, u32[]{:S(2)}) copy-start(f32[6336]{0:T(1024)} %param.21) | copy-start | bytes 76036
  3.5 19.6 %copy-start.4 = (f32[6336]{0:T(1024)S(1)}, f32[6336]{0:T(1024)}, u32[]{:S(2)}) copy-start(f32[6336]{0:T(1024)} %param.20) | copy-start | bytes 76036
  10.2 26.5 %all-to-all-start = ((bf16[3,128,5,128]{3,0,2,1:T(4,128)(2,1)}), bf16[3,128,5,128]{3,0,2,1:T(4,128)(2,1)}, u32[]{:S(2)}, u32[]{:S(2)}) async-start(bf16[3,128,5,128]{3,0,2,1:T(4,128)(2,1)} %pad_maximum_fusion), calls=%async_computation | async-start | bytes 1310720 | tf_op jit(solution)/shard_map/all_to_all | solution.py:68
  36.7 3.0 %copy-start.1 = (f32[1,3,128,128]{3,2,1,0:T(8,128)S(1)}, f32[1,3,128,128]{3,2,1,0:T(8,128)}, u32[]{:S(2)}) copy-start(f32[1,3,128,128]{3,2,1,0:T(8,128)} %param.17) | copy-start | bytes 589828
  43.1 21.8 %all-to-all-start.1 = ((f32[3,128,4,128]{3,2,0,1:T(4,128)}), f32[3,128,4,128]{3,2,0,1:T(4,128)}, u32[]{:S(2)}, u32[]{:S(2)}) async-start(f32[3,128,4,128]{3,2,0,1:T(4,128)} %copy.72), calls=%async_computation.1 | async-start | bytes 1572864 | tf_op jit(solution)/shard_map/all_to_all | solution.py:97

commit v10 on v9

--- a/solution.py
+++ b/solution.py
@@ -48,11 +48,14 @@
     adam_part = jnp.sum(
         jnp.square(direction).reshape(layer_count, row_count, block_count, BLOCK), axis=(1, 3)
     )
-    part_by_place = jnp.zeros((slot_count * devices,), jnp.float32).at[target].set(
-        adam_part.reshape(total_blocks)
-    )
-    part_hi = part_by_place.astype(jnp.bfloat16)
-    part_lo = (part_by_place - part_hi.astype(jnp.float32)).astype(jnp.bfloat16)
+    block_hi = adam_part.astype(jnp.bfloat16)
+    block_lo = (adam_part - block_hi.astype(jnp.float32)).astype(jnp.bfloat16)
+    halves = jnp.einsum(
+        "qln,lnk->qk", picker, jnp.stack([block_hi, block_lo], axis=-1),
+        preferred_element_type=jnp.float32,
+    ).astype(jnp.bfloat16)
+    part_hi = halves[:, 0]
+    part_lo = halves[:, 1]
     lane = jnp.arange(BLOCK, dtype=jnp.int32)
     extra = jnp.where(
         lane[None, :] == 0,

time: 69.9 us -> 69 us (0.987)
  local copies, waits for them, and re-layouts: 7.84 us -> 6.59 us
    scatter x1 -> x0, local copies, waits for them, and re-layouts: 1.21 us -> none  [per_device(): jnp.zeros((slot_count * devices,), jnp.float32).at[target]]
where the time goes in v10:
time: 69 us; the launch traced here: 68.6 us
  waiting for transfers between devices  23.1 us (33%)
  starting transfers between devices  17.6 us (26%)
  matrix products  11.6 us (17%)
  other arithmetic  8.9 us (13%)
  local copies, waits for them, and re-layouts  6.59 us (10%)
  between operations  0.83 us (1%)
    all_to_all x1, waiting for transfers between devices, per_device(): lax.all_to_all(outgoing, ('shard', 'tensor'), split_axis=1, concat_axis=1...  13 us
    all_to_all x1, starting transfers between devices, per_device(): lax.all_to_all(outgoing, ('shard', 'tensor'), split_axis=1, concat_axis=1...  11.9 us
    all_to_all x1, waiting for transfers between devices, per_device(): lax.all_to_all(shaped, ('shard', 'tensor'), split_axis=1, concat_axis=1,...  10 us
    all_to_all x1, starting transfers between devices, per_device(): lax.all_to_all(shaped, ('shard', 'tensor'), split_axis=1, concat_axis=1,...  5.7 us
    dot_general x1, matrix products, per_device(): jnp.einsum('cib,cjb->cij', block_grads, block_grads, preferred_element_ty...  4.12 us
    reduce_sum x2, other arithmetic, per_device(): jnp.sum(jnp.square(direction).reshape(layer_count, row_count, block_count...  2.87 us
    dot_general x1, matrix products, per_device(): jnp.einsum('lnqd,qdrb->lrnb', placer, returned, precision=PRECISE, prefer...  2.43 us
    dot_general x1, matrix products, per_device(): jnp.einsum('cib,cid->cbd', block_grads, block_grads, preferred_element_ty...  1.91 us
  transfers between devices with their start and end apart: 2, of which 2 were waited for; matrix products, arithmetic and copies ran while one was open for 11% of the time, Pallas kernels for 0%

profile of v10, /device:TPU:1, one launch (start us, length us, event | category | flops | bytes accessed | tf_op | source)
XLA Modules:
  0.0 68.6 jit_solution(826643669218418375)
XLA Ops:
  0.7 2.8 %multiply_reduce_fusion.1 = (f32[4,6144]{1,0:T(4,128)S(1)}, f32[4,4,6144]{2,1,0:T(4,128)}, f32[4,4,6144]{2,1,0:T(4,128)}) fusion(bf16[4,4,6144]{2,1,0:T(4,128)(2,1)} %param.11, f32[4,4,6144]{2,1,0:T(4,128)} %param.13, f32[4,4,6144]{2,1,0:T(4,128)} %param.12), kind=kLoop, calls=%fused_computation.18 | loop fusion | flops 1155072 | bytes 1867776 | tf_op jit(solution)/shard_map/reduce_sum | solution.py:48
  3.5 0.1 bitcast_reduce_fusion
  3.6 1.1 %reshape.189 = bf16[4,4,48,128]{3,2,1,0:T(8,128)(2,1)S(1)} reshape(bf16[4,4,6144]{2,1,0:T(4,128)(2,1)} %param.11) | data formatting | bytes 393216 | tf_op jit(solution)/shard_map/reshape | solution.py:65
  4.7 0.9 %convert_reduce_fusion = s32[192]{0:T(256)S(1)} fusion(s32[192]{0:T(256)} %param.18), kind=kLoop, calls=%fused_computation.27 | loop fusion | flops 184128 | bytes 1536 | tf_op jit(solution)/shard_map/reduce_sum | solution.py:38
  5.6 0.7 %multiply_add_fusion.1 = s32[192]{0:T(256)S(1)} fusion(s32[192]{0:T(256)} %param.18, s32[192]{0:T(256)S(1)} %convert_reduce_fusion), kind=kLoop, calls=%fused_computation.48 | loop fusion | flops 384 | bytes 2304 | tf_op jit(solution)/shard_map/add | solution.py:39
  6.3 0.1 eq.116
  6.4 0.2 fusion.4
  6.6 0.1 copy.58
  6.8 0.1 copy.57
  6.9 0.4 fusion.2
  7.3 0.3 copy.59
  7.7 0.3 select_select_fusion
  8.0 1.3 %pad_maximum_fusion = bf16[3,128,5,128]{3,0,2,1:T(4,128)(2,1)} fusion(bf16[3,128,1,128]{3,0,2,1:T(4,128)(2,1)S(1)} %select_select_fusion, bf16[3,128,4,128]{3,0,2,1:T(4,128)(2,1)S(1)} %copy.59), kind=kLoop, calls=%fused_computation.12 | loop fusion | flops 245760 | bytes 983040 | tf_op jit(solution)/shard_map/concatenate | solution.py:69
  9.3 11.9 %all-to-all-start = ((bf16[3,128,5,128]{3,0,2,1:T(4,128)(2,1)}), bf16[3,128,5,128]{3,0,2,1:T(4,128)(2,1)}, u32[]{:S(2)}, u32[]{:S(2)}) async-start(bf16[3,128,5,128]{3,0,2,1:T(4,128)(2,1)} %pad_maximum_fusion), calls=%async_computation | async-start | bytes 1310720 | tf_op jit(solution)/shard_map/all_to_all | solution.py:71
  21.2 0.1 eq.131
  21.4 0.7 %iota_compare_fusion.4 = pred[4,48,128]{2,1,0:T(8,128)(4,1)} fusion(s32[4,48]{1,0:T(4,128)S(1)} %eq.131), kind=kLoop, calls=%fused_computation.36 | loop fusion | flops 24576 | bytes 25344 | tf_op jit(solution)/shard_map/eq | solution.py:105
  22.1 0.6 add_divide_fusion
  22.7 13.0 %all-to-all-done = bf16[3,128,5,128]{3,0,2,1:T(4,128)(2,1)} async-done(((bf16[3,128,5,128]{3,0,2,1:T(4,128)(2,1)}), bf16[3,128,5,128]{3,0,2,1:T(4,128)(2,1)}, u32[]{:S(2)}, u32[]{:S(2)}) %all-to-all-start) | async-done | bytes 491552 | tf_op jit(solution)/shard_map/all_to_all | solution.py:71
  35.7 1.3 %slice.22 = bf16[3,128,4,128]{3,0,2,1:T(4,128)(2,1)S(1)} slice(bf16[3,128,5,128]{3,0,2,1:T(4,128)(2,1)} %all-to-all-done), slice={[0:3], [0:128], [0:4], [0:128]} | slice | bytes 786432 | tf_op jit(solution)/shard_map/slice | solution.py:74
  37.0 0.2 copy.60
  37.2 1.6 %fusion = f32[3,128,512]{1,2,0:T(8,128)S(1)} fusion(bf16[3,512,128]{2,1,0:T(8,128)(2,1)S(1)} %bitcast.60, f32[1,3,512,512]{3,2,1,0:T(8,128)S(1)} %copy-done), kind=kOutput, calls=%fused_computation.1 | convolution fusion | flops 1207959552 | bytes 4325376 | tf_op jit(solution)/shard_map/cij,cjb->cib/dot_general | solution.py:92
  38.8 0.9 %multiply_reduce_fusion = (f32[3]{0:T(128)S(1)}, f32[3,512,128]{2,1,0:T(8,128)S(1)}) fusion(f32[3,128,512]{1,2,0:T(8,128)S(1)} %fusion, f32[1,3,128,128]{3,2,1,0:T(8,128)S(1)} %copy-done.1), kind=kOutput, calls=%fused_computation.11 | convolution fusion | flops 302383104 | bytes 1769484 | tf_op jit(solution)/shard_map/cib,cbd->cid/dot_general | solution.py:95
  39.7 1.3 %add_reduce_fusion = f32[3]{0:T(128)S(1)} fusion(bf16[3,128,5,128]{3,0,2,1:T(4,128)(2,1)} %all-to-all-done), kind=kLoop, calls=%fused_computation.24 | loop fusion | flops 1533 | bytes 1548 | tf_op jit(solution)/shard_map/reduce_sum | solution.py:75
  41.0 0.1 broadcast_multiply_fusion
  41.1 1.0 %copy.63 = f32[3,128,4,128]{3,2,0,1:T(4,128)} copy(f32[3,128,4,128]{3,2,1,0:T(4,128)S(1)} %bitcast.63) | data formatting | bytes 1572864 | tf_op jit(solution)/shard_map/reshape | solution.py:99
  42.2 5.7 %all-to-all-start.1 = ((f32[3,128,4,128]{3,2,0,1:T(4,128)}), f32[3,128,4,128]{3,2,0,1:T(4,128)}, u32[]{:S(2)}, u32[]{:S(2)}) async-start(f32[3,128,4,128]{3,2,0,1:T(4,128)} %copy.63), calls=%async_computation.1 | async-start | bytes 1572864 | tf_op jit(solution)/shard_map/all_to_all | solution.py:100
  47.9 1.9 %fusion.3 = f32[1,3,128,128]{3,2,1,0:T(8,128)} fusion(f32[1,3,128,128]{3,2,1,0:T(8,128)} %param.15, bf16[3,512,128]{2,1,0:T(8,128)(2,1)S(1)} %bitcast.61), kind=kOutput, calls=%fused_computation.7 | convolution fusion | flops 50380800 | bytes 786432 | tf_op jit(solution)/shard_map/cib,cid->cbd/dot_general | solution.py:88
  49.8 4.1 %bitcast_add_fusion = f32[1,3,512,512]{3,2,1,0:T(8,128)} fusion(f32[1,3,512,512]{3,2,1,0:T(8,128)} %param.14, bf16[3,512,128]{2,1,0:T(8,128)(2,1)S(1)} %bitcast.62), kind=kOutput, calls=%fused_computation | convolution fusion | flops 202113024 | bytes 6684672 | tf_op jit(solution)/shard_map/cib,cjb->cij/dot_general | solution.py:82
  53.9 10.0 %all-to-all-done.1 = f32[3,128,4,128]{3,2,0,1:T(4,128)} async-done(((f32[3,128,4,128]{3,2,0,1:T(4,128)}), f32[3,128,4,128]{3,2,0,1:T(4,128)}, u32[]{:S(2)}, u32[]{:S(2)}) %all-to-all-start.1) | async-done | bytes 786464 | tf_op jit(solution)/shard_map/all_to_all | solution.py:100
  64.0 2.4 %convolution_bitcast_fusion.1 = f32[4,4,48,128]{3,2,0,1:T(8,128)} fusion(f32[3,128,4,128,1]{3,2,0,1,4:T(4,128)} %bitcast.11, pred[4,48,128]{2,1,0:T(8,128)(4,1)} %iota_compare_fusion.4, pred[4,48,3]{1,2,0:T(4,128)(4,1)S(1)} %iota_compare_fusion.5), kind=kOutput, calls=%fused_computation.5 | convolution fusion | flops 453058560 | bytes 1204800 | tf_op jit(solution)/shard_map/lnqd,qdrb->lrnb/dot_general | solution.py:107
  66.4 1.1 %reshape.192 = f32[4,4,6144]{2,0,1:T(4,128)S(1)} reshape(f32[4,4,48,128]{3,2,0,1:T(8,128)} %convolution_bitcast_fusion.1) | data formatting | bytes 786432 | tf_op jit(solution)/shard_map/reshape | solution.py:110
  67.5 1.0 %copy.66 = f32[4,4,6144]{2,1,0:T(4,128)} copy(f32[4,4,6144]{2,0,1:T(4,128)S(1)} %reshape.192) | data formatting | bytes 786432
  (19 shorter events, 0.2 us)
Async XLA Ops:
  0.6 36.6 %copy-start = (f32[1,3,512,512]{3,2,1,0:T(8,128)S(1)}, f32[1,3,512,512]{3,2,1,0:T(8,128)}, u32[]{:S(2)}) copy-start(f32[1,3,512,512]{3,2,1,0:T(8,128)} %param.16) | copy-start | bytes 9437188
  3.4 17.8 %copy-start.5 = (s32[192]{0:T(256)S(1)}, s32[192]{0:T(256)}, u32[]{:S(2)}) copy-start(s32[192]{0:T(256)} %param.18) | copy-start | bytes 2308
  3.4 18.6 %copy-start.2 = (f32[6336]{0:T(1024)S(1)}, f32[6336]{0:T(1024)}, u32[]{:S(2)}) copy-start(f32[6336]{0:T(1024)} %param.19) | copy-start | bytes 76036
  3.5 18.6 %copy-start.3 = (f32[6336]{0:T(1024)S(1)}, f32[6336]{0:T(1024)}, u32[]{:S(2)}) copy-start(f32[6336]{0:T(1024)} %param.21) | copy-start | bytes 76036
  3.5 18.6 %copy-start.4 = (f32[6336]{0:T(1024)S(1)}, f32[6336]{0:T(1024)}, u32[]{:S(2)}) copy-start(f32[6336]{0:T(1024)} %param.20) | copy-start | bytes 76036
  9.3 26.5 %all-to-all-start = ((bf16[3,128,5,128]{3,0,2,1:T(4,128)(2,1)}), bf16[3,128,5,128]{3,0,2,1:T(4,128)(2,1)}, u32[]{:S(2)}, u32[]{:S(2)}) async-start(bf16[3,128,5,128]{3,0,2,1:T(4,128)(2,1)} %pad_maximum_fusion), calls=%async_computation | async-start | bytes 1310720 | tf_op jit(solution)/shard_map/all_to_all | solution.py:71
  35.7 3.0 %copy-start.1 = (f32[1,3,128,128]{3,2,1,0:T(8,128)S(1)}, f32[1,3,128,128]{3,2,1,0:T(8,128)}, u32[]{:S(2)}) copy-start(f32[1,3,128,128]{3,2,1,0:T(8,128)} %param.17) | copy-start | bytes 589828
  42.2 21.8 %all-to-all-start.1 = ((f32[3,128,4,128]{3,2,0,1:T(4,128)}), f32[3,128,4,128]{3,2,0,1:T(4,128)}, u32[]{:S(2)}, u32[]{:S(2)}) async-start(f32[3,128,4,128]{3,2,0,1:T(4,128)} %copy.63), calls=%async_computation.1 | async-start | bytes 1572864 | tf_op jit(solution)/shard_map/all_to_all | solution.py:100

commit v11 on v10

--- a/solution.py
+++ b/solution.py
@@ -104,10 +104,14 @@
         (slot_index[:, None, None] == slot_ids[None, :, None])
         & (owners[:, None, None] == device_ids[None, None, :])
     ).astype(jnp.float32).reshape(layer_count, block_count, slot_count, devices)
-    updates = jnp.einsum(
-        "lnqd,qdrb->lrnb", placer, returned, precision=PRECISE,
-        preferred_element_type=jnp.float32,
-    ).reshape(layer_count, row_count, col_count)
+    updates = (
+        jnp.einsum(
+            "lnqd,qdrb->lnrb", placer, returned, precision=PRECISE,
+            preferred_element_type=jnp.float32,
+        )
+        .transpose(0, 2, 1, 3)
+        .reshape(layer_count, row_count, col_count)
+    )
     small_mean_out, small_square_out, small_update = adam_moments(
         small_grad, small_mean, small_square
     )

time: 69 us -> 67 us (0.971)
  local copies, waits for them, and re-layouts: 6.59 us -> 5.35 us
  matrix products: 11.6 us -> 10.8 us
    unnamed x13 -> x12, local copies, waits for them, and re-layouts: 1.04 us -> 0.04 us
    dot_general x1, matrix products: 2.43 us -> 1.7 us  [per_device(): jnp.einsum('lnqd,qdrb->lnrb', placer, returned, precision=PRECISE, prefer...]
where the time goes in v11:
time: 67 us; the launch traced here: 66.6 us
  waiting for transfers between devices  23.1 us (34%)
  starting transfers between devices  17.6 us (26%)
  matrix products  10.8 us (16%)
  other arithmetic  8.91 us (13%)
  local copies, waits for them, and re-layouts  5.35 us (8%)
  between operations  0.83 us (1%)
    all_to_all x1, waiting for transfers between devices, per_device(): lax.all_to_all(outgoing, ('shard', 'tensor'), split_axis=1, concat_axis=1...  13 us
    all_to_all x1, starting transfers between devices, per_device(): lax.all_to_all(outgoing, ('shard', 'tensor'), split_axis=1, concat_axis=1...  11.9 us
    all_to_all x1, waiting for transfers between devices, per_device(): lax.all_to_all(shaped, ('shard', 'tensor'), split_axis=1, concat_axis=1,...  10 us
    all_to_all x1, starting transfers between devices, per_device(): lax.all_to_all(shaped, ('shard', 'tensor'), split_axis=1, concat_axis=1,...  5.7 us
    dot_general x1, matrix products, per_device(): jnp.einsum('cib,cjb->cij', block_grads, block_grads, preferred_element_ty...  4.12 us
    reduce_sum x2, other arithmetic, per_device(): jnp.sum(jnp.square(direction).reshape(layer_count, row_count, block_count...  2.87 us
    dot_general x1, matrix products, per_device(): jnp.einsum('cib,cid->cbd', block_grads, block_grads, preferred_element_ty...  1.91 us
    dot_general x1, matrix products, per_device(): jnp.einsum('lnqd,qdrb->lnrb', placer, returned, precision=PRECISE, prefer...  1.7 us
  transfers between devices with their start and end apart: 2, of which 2 were waited for; matrix products, arithmetic and copies ran while one was open for 11% of the time, Pallas kernels for 0%

profile of v11, /device:TPU:1, one launch (start us, length us, event | category | flops | bytes accessed | tf_op | source)
XLA Modules:
  0.0 66.6 jit_solution(13016880150318675785)
XLA Ops:
  0.7 2.8 %multiply_reduce_fusion.1 = (f32[4,6144]{1,0:T(4,128)S(1)}, f32[4,4,6144]{2,1,0:T(4,128)}, f32[4,4,6144]{2,1,0:T(4,128)}) fusion(bf16[4,4,6144]{2,1,0:T(4,128)(2,1)} %param.11, f32[4,4,6144]{2,1,0:T(4,128)} %param.13, f32[4,4,6144]{2,1,0:T(4,128)} %param.12), kind=kLoop, calls=%fused_computation.19 | loop fusion | flops 1155072 | bytes 1867776 | tf_op jit(solution)/shard_map/reduce_sum | solution.py:48
  3.5 0.1 bitcast_reduce_fusion
  3.6 1.1 %reshape.189 = bf16[4,4,48,128]{3,2,1,0:T(8,128)(2,1)S(1)} reshape(bf16[4,4,6144]{2,1,0:T(4,128)(2,1)} %param.11) | data formatting | bytes 393216 | tf_op jit(solution)/shard_map/reshape | solution.py:65
  4.7 0.9 %convert_reduce_fusion = s32[192]{0:T(256)S(1)} fusion(s32[192]{0:T(256)} %param.18), kind=kLoop, calls=%fused_computation.28 | loop fusion | flops 184128 | bytes 1536 | tf_op jit(solution)/shard_map/reduce_sum | solution.py:38
  5.6 0.7 %multiply_add_fusion.1 = s32[192]{0:T(256)S(1)} fusion(s32[192]{0:T(256)} %param.18, s32[192]{0:T(256)S(1)} %convert_reduce_fusion), kind=kLoop, calls=%fused_computation.49 | loop fusion | flops 384 | bytes 2304 | tf_op jit(solution)/shard_map/add | solution.py:39
  6.3 0.1 eq.124
  6.4 0.2 fusion.4
  6.6 0.1 copy.54
  6.8 0.1 copy.53
  6.9 0.4 fusion.2
  7.3 0.3 copy.55
  7.7 0.3 select_select_fusion
  8.0 1.3 %pad_maximum_fusion = bf16[3,128,5,128]{3,0,2,1:T(4,128)(2,1)} fusion(bf16[3,128,1,128]{3,0,2,1:T(4,128)(2,1)S(1)} %select_select_fusion, bf16[3,128,4,128]{3,0,2,1:T(4,128)(2,1)S(1)} %copy.55), kind=kLoop, calls=%fused_computation.13 | loop fusion | flops 245760 | bytes 983040 | tf_op jit(solution)/shard_map/concatenate | solution.py:69
  9.3 11.9 %all-to-all-start = ((bf16[3,128,5,128]{3,0,2,1:T(4,128)(2,1)}), bf16[3,128,5,128]{3,0,2,1:T(4,128)(2,1)}, u32[]{:S(2)}, u32[]{:S(2)}) async-start(bf16[3,128,5,128]{3,0,2,1:T(4,128)(2,1)} %pad_maximum_fusion), calls=%async_computation | async-start | bytes 1310720 | tf_op jit(solution)/shard_map/all_to_all | solution.py:71
  21.2 0.1 eq.119
  21.3 0.1 eq.115
  21.4 0.7 %iota_compare_fusion.4 = pred[4,48,128]{2,1,0:T(8,128)(4,1)} fusion(s32[4,48]{1,0:T(4,128)S(1)} %eq.119), kind=kLoop, calls=%fused_computation.37 | loop fusion | flops 24576 | bytes 25344 | tf_op jit(solution)/shard_map/eq | solution.py:105
  22.1 0.6 add_divide_fusion
  22.7 13.0 %all-to-all-done = bf16[3,128,5,128]{3,0,2,1:T(4,128)(2,1)} async-done(((bf16[3,128,5,128]{3,0,2,1:T(4,128)(2,1)}), bf16[3,128,5,128]{3,0,2,1:T(4,128)(2,1)}, u32[]{:S(2)}, u32[]{:S(2)}) %all-to-all-start) | async-done | bytes 491552 | tf_op jit(solution)/shard_map/all_to_all | solution.py:71
  35.7 1.3 %slice.22 = bf16[3,128,4,128]{3,0,2,1:T(4,128)(2,1)S(1)} slice(bf16[3,128,5,128]{3,0,2,1:T(4,128)(2,1)} %all-to-all-done), slice={[0:3], [0:128], [0:4], [0:128]} | slice | bytes 786432 | tf_op jit(solution)/shard_map/slice | solution.py:74
  37.0 0.2 copy.56
  37.2 1.6 %fusion = f32[3,128,512]{1,2,0:T(8,128)S(1)} fusion(bf16[3,512,128]{2,1,0:T(8,128)(2,1)S(1)} %bitcast.62, f32[1,3,512,512]{3,2,1,0:T(8,128)S(1)} %copy-done), kind=kOutput, calls=%fused_computation.1 | convolution fusion | flops 1207959552 | bytes 4325376 | tf_op jit(solution)/shard_map/cij,cjb->cib/dot_general | solution.py:92
  38.8 0.9 %multiply_reduce_fusion = (f32[3]{0:T(128)S(1)}, f32[3,512,128]{2,1,0:T(8,128)S(1)}) fusion(f32[3,128,512]{1,2,0:T(8,128)S(1)} %fusion, f32[1,3,128,128]{3,2,1,0:T(8,128)S(1)} %copy-done.1), kind=kOutput, calls=%fused_computation.12 | convolution fusion | flops 302383104 | bytes 1769484 | tf_op jit(solution)/shard_map/cib,cbd->cid/dot_general | solution.py:95
  39.7 1.3 %add_reduce_fusion = f32[3]{0:T(128)S(1)} fusion(bf16[3,128,5,128]{3,0,2,1:T(4,128)(2,1)} %all-to-all-done), kind=kLoop, calls=%fused_computation.25 | loop fusion | flops 1533 | bytes 1548 | tf_op jit(solution)/shard_map/reduce_sum | solution.py:75
  41.0 0.1 broadcast_multiply_fusion
  41.1 1.0 %copy.59 = f32[3,128,4,128]{3,2,0,1:T(4,128)} copy(f32[3,128,4,128]{3,2,1,0:T(4,128)S(1)} %bitcast.65) | data formatting | bytes 1572864 | tf_op jit(solution)/shard_map/reshape | solution.py:99
  42.2 5.7 %all-to-all-start.1 = ((f32[3,128,4,128]{3,2,0,1:T(4,128)}), f32[3,128,4,128]{3,2,0,1:T(4,128)}, u32[]{:S(2)}, u32[]{:S(2)}) async-start(f32[3,128,4,128]{3,2,0,1:T(4,128)} %copy.59), calls=%async_computation.1 | async-start | bytes 1572864 | tf_op jit(solution)/shard_map/all_to_all | solution.py:100
  47.9 1.9 %fusion.3 = f32[1,3,128,128]{3,2,1,0:T(8,128)} fusion(f32[1,3,128,128]{3,2,1,0:T(8,128)} %param.15, bf16[3,512,128]{2,1,0:T(8,128)(2,1)S(1)} %bitcast.63), kind=kOutput, calls=%fused_computation.7 | convolution fusion | flops 50380800 | bytes 786432 | tf_op jit(solution)/shard_map/cib,cid->cbd/dot_general | solution.py:88
  49.8 4.1 %bitcast_add_fusion = f32[1,3,512,512]{3,2,1,0:T(8,128)} fusion(f32[1,3,512,512]{3,2,1,0:T(8,128)} %param.14, bf16[3,512,128]{2,1,0:T(8,128)(2,1)S(1)} %bitcast.64), kind=kOutput, calls=%fused_computation | convolution fusion | flops 202113024 | bytes 6684672 | tf_op jit(solution)/shard_map/cib,cjb->cij/dot_general | solution.py:82
  53.9 10.0 %all-to-all-done.1 = f32[3,128,4,128]{3,2,0,1:T(4,128)} async-done(((f32[3,128,4,128]{3,2,0,1:T(4,128)}), f32[3,128,4,128]{3,2,0,1:T(4,128)}, u32[]{:S(2)}, u32[]{:S(2)}) %all-to-all-start.1) | async-done | bytes 786464 | tf_op jit(solution)/shard_map/all_to_all | solution.py:100
  64.0 1.7 %convolution_bitcast_fusion.1 = f32[4,4,48,128]{3,2,1,0:T(8,128)S(1)} fusion(f32[3,128,4,128]{3,2,0,1:T(4,128)} %all-to-all-done.1, pred[4,48,128]{2,1,0:T(8,128)(4,1)} %iota_compare_fusion.4, pred[4,48,3]{1,2,0:T(4,128)(4,1)S(1)} %iota_compare_fusion.5), kind=kOutput, calls=%fused_computation.5 | convolution fusion | flops 453058560 | bytes 1204800 | tf_op jit(solution)/shard_map/lnqd,qdrb->lnrb/dot_general | solution.py:108
  65.7 0.9 %reshape.192 = f32[4,4,6144]{2,1,0:T(4,128)} reshape(f32[4,4,48,128]{3,2,1,0:T(8,128)S(1)} %convolution_bitcast_fusion.1) | data formatting | bytes 786432 | tf_op jit(solution)/shard_map/reshape | solution.py:113
  (18 shorter events, 0.1 us)
Async XLA Ops:
  0.6 36.6 %copy-start = (f32[1,3,512,512]{3,2,1,0:T(8,128)S(1)}, f32[1,3,512,512]{3,2,1,0:T(8,128)}, u32[]{:S(2)}) copy-start(f32[1,3,512,512]{3,2,1,0:T(8,128)} %param.16) | copy-start | bytes 9437188
  3.4 17.8 %copy-start.5 = (s32[192]{0:T(256)S(1)}, s32[192]{0:T(256)}, u32[]{:S(2)}) copy-start(s32[192]{0:T(256)} %param.18) | copy-start | bytes 2308
  3.4 18.6 %copy-start.2 = (f32[6336]{0:T(1024)S(1)}, f32[6336]{0:T(1024)}, u32[]{:S(2)}) copy-start(f32[6336]{0:T(1024)} %param.19) | copy-start | bytes 76036
  3.5 18.6 %copy-start.3 = (f32[6336]{0:T(1024)S(1)}, f32[6336]{0:T(1024)}, u32[]{:S(2)}) copy-start(f32[6336]{0:T(1024)} %param.21) | copy-start | bytes 76036
  3.5 18.6 %copy-start.4 = (f32[6336]{0:T(1024)S(1)}, f32[6336]{0:T(1024)}, u32[]{:S(2)}) copy-start(f32[6336]{0:T(1024)} %param.20) | copy-start | bytes 76036
  9.3 26.5 %all-to-all-start = ((bf16[3,128,5,128]{3,0,2,1:T(4,128)(2,1)}), bf16[3,128,5,128]{3,0,2,1:T(4,128)(2,1)}, u32[]{:S(2)}, u32[]{:S(2)}) async-start(bf16[3,128,5,128]{3,0,2,1:T(4,128)(2,1)} %pad_maximum_fusion), calls=%async_computation | async-start | bytes 1310720 | tf_op jit(solution)/shard_map/all_to_all | solution.py:71
  35.7 3.0 %copy-start.1 = (f32[1,3,128,128]{3,2,1,0:T(8,128)S(1)}, f32[1,3,128,128]{3,2,1,0:T(8,128)}, u32[]{:S(2)}) copy-start(f32[1,3,128,128]{3,2,1,0:T(8,128)} %param.17) | copy-start | bytes 589828
  42.2 21.8 %all-to-all-start.1 = ((f32[3,128,4,128]{3,2,0,1:T(4,128)}), f32[3,128,4,128]{3,2,0,1:T(4,128)}, u32[]{:S(2)}, u32[]{:S(2)}) async-start(f32[3,128,4,128]{3,2,0,1:T(4,128)} %copy.59), calls=%async_computation.1 | async-start | bytes 1572864 | tf_op jit(solution)/shard_map/all_to_all | solution.py:100

commit v12 on v11

--- a/solution.py
+++ b/solution.py
@@ -54,28 +54,23 @@
         "qln,lnk->qk", picker, jnp.stack([block_hi, block_lo], axis=-1),
         preferred_element_type=jnp.float32,
     ).astype(jnp.bfloat16)
-    part_hi = halves[:, 0]
-    part_lo = halves[:, 1]
-    lane = jnp.arange(BLOCK, dtype=jnp.int32)
-    extra = jnp.where(
-        lane[None, :] == 0,
-        part_hi[:, None],
-        jnp.where(lane[None, :] == 1, part_lo[:, None], jnp.zeros((), jnp.bfloat16)),
-    )[:, None, :]
+    part_slot = jnp.pad(
+        halves.reshape(slot_count, devices, 2).transpose(1, 2, 0),
+        ((0, 0), (0, row_count - 2), (0, BLOCK - slot_count)),
+    )[None]
     pieces = gradients.reshape(layer_count, row_count, block_count, BLOCK)
     outgoing = jnp.einsum(
         "qln,lrnb->qrb", picker, pieces, preferred_element_type=jnp.float32
     ).astype(jnp.bfloat16)
-    outgoing = jnp.concatenate([outgoing, extra], axis=1)
-    outgoing = outgoing.reshape(slot_count, devices, row_count + 1, BLOCK)
+    outgoing = jnp.concatenate(
+        [outgoing.reshape(slot_count, devices, row_count, BLOCK), part_slot], axis=0
+    )
     incoming = lax.all_to_all(
         outgoing, ("shard", "tensor"), split_axis=1, concat_axis=1, tiled=True
     )
-    block_grads = incoming[:, :, :row_count, :].reshape(slot_count, devices * row_count, BLOCK)
+    block_grads = incoming[:slot_count].reshape(slot_count, devices * row_count, BLOCK)
     adam_sums = jnp.sum(
-        incoming[:, :, row_count, 0].astype(jnp.float32)
-        + incoming[:, :, row_count, 1].astype(jnp.float32),
-        axis=1,
+        incoming[slot_count, :, 0:2, 0:slot_count].astype(jnp.float32), axis=(0, 1)
     )
     left_out = (
         stat_left

time: 67 us -> 67.5 us (level)
  matrix products: 10.8 us -> 12.7 us
  waiting for transfers between devices: 23.1 us -> 21.7 us
    all_to_all x1, waiting for transfers between devices: 13 us -> 11.7 us  [per_device(): lax.all_to_all(outgoing, ('shard', 'tensor'), split_axis=1, concat_axis=1...]
    dot_general x1, matrix products: 0.4 us -> 1.33 us  [per_device(): jnp.einsum('qln,lrnb->qrb', picker, pieces, preferred_element_type=jnp.fl...]
    dot_general x1, matrix products: 0.89 us -> 1.82 us  [per_device(): jnp.einsum('cib,cbd->cid', left_applied, root_right[0], precision=PRECISE)]
    reshape x1, local copies, waits for them, and re-layouts: 1.05 us -> 1.73 us  [per_device(): pieces = gradients.reshape(layer_count, row_count, block_count, BLOCK)]
    slice x3 -> x1, local copies, waits for them, and re-layouts: 1.46 us -> 1.21 us  [per_device(): incoming[:slot_count].reshape(slot_count, devices * row_count, BLOCK)]
where the time goes in v12:
time: 67.5 us; the launch traced here: 67 us
  waiting for transfers between devices  21.7 us (32%)
  starting transfers between devices  17.6 us (26%)
  matrix products  12.7 us (19%)
  other arithmetic  8.56 us (13%)
  local copies, waits for them, and re-layouts  5.72 us (8%)
  between operations  0.8 us (1%)
    all_to_all x1, starting transfers between devices, per_device(): lax.all_to_all(outgoing, ('shard', 'tensor'), split_axis=1, concat_axis=1...  11.9 us
    all_to_all x1, waiting for transfers between devices, per_device(): lax.all_to_all(outgoing, ('shard', 'tensor'), split_axis=1, concat_axis=1...  11.7 us
    all_to_all x1, waiting for transfers between devices, per_device(): lax.all_to_all(shaped, ('shard', 'tensor'), split_axis=1, concat_axis=1,...  10 us
    all_to_all x1, starting transfers between devices, per_device(): lax.all_to_all(shaped, ('shard', 'tensor'), split_axis=1, concat_axis=1,...  5.62 us
    dot_general x1, matrix products, per_device(): jnp.einsum('cib,cjb->cij', block_grads, block_grads, preferred_element_ty...  4.12 us
    reduce_sum x2, other arithmetic, per_device(): jnp.sum(jnp.square(direction).reshape(layer_count, row_count, block_count...  2.86 us
    dot_general x1, matrix products, per_device(): jnp.einsum('cib,cid->cbd', block_grads, block_grads, preferred_element_ty...  1.92 us
    dot_general x1, matrix products, per_device(): jnp.einsum('cib,cbd->cid', left_applied, root_right[0], precision=PRECISE)  1.82 us
  transfers between devices with their start and end apart: 2, of which 2 were waited for; matrix products, arithmetic and copies ran while one was open for 11% of the time, Pallas kernels for 0%

profile of v12, /device:TPU:1, one launch (start us, length us, event | category | flops | bytes accessed | tf_op | source)
XLA Modules:
  0.0 67.0 jit_solution(13415297973758269726)
XLA Ops:
  0.6 0.0 copy-start
  0.6 2.8 %multiply_reduce_fusion.1 = (f32[4,6144]{1,0:T(4,128)S(1)}, f32[4,4,6144]{2,1,0:T(4,128)}, f32[4,4,6144]{2,1,0:T(4,128)}) fusion(bf16[4,4,6144]{2,1,0:T(4,128)(2,1)} %param.11, f32[4,4,6144]{2,1,0:T(4,128)} %param.13, f32[4,4,6144]{2,1,0:T(4,128)} %param.12), kind=kLoop, calls=%fused_computation.19 | loop fusion | flops 1155072 | bytes 1867776 | tf_op jit(solution)/shard_map/reduce_sum | solution.py:48
  3.4 0.0 copy-start.4
  3.4 0.1 bitcast_reduce_fusion
  3.6 1.7 %reshape.144 = bf16[4,4,48,128]{3,2,1,0:T(8,128)(2,1)} reshape(bf16[4,4,6144]{2,1,0:T(4,128)(2,1)} %param.11) | data formatting | bytes 393216 | tf_op jit(solution)/shard_map/reshape | solution.py:61
  5.3 0.9 %convert_reduce_fusion = s32[192]{0:T(256)S(1)} fusion(s32[192]{0:T(256)} %param.18), kind=kLoop, calls=%fused_computation.27 | loop fusion | flops 184128 | bytes 1536 | tf_op jit(solution)/shard_map/reduce_sum | solution.py:38
  6.2 0.7 %multiply_add_fusion.1 = s32[192]{0:T(256)S(1)} fusion(s32[192]{0:T(256)} %param.18, s32[192]{0:T(256)S(1)} %convert_reduce_fusion), kind=kLoop, calls=%fused_computation.48 | loop fusion | flops 384 | bytes 2304 | tf_op jit(solution)/shard_map/add | solution.py:39
  6.9 0.1 eq.102
  7.0 0.2 fusion.4
  7.3 0.2 copy.59
  7.5 0.0 copy-start.1
  7.5 1.3 %fusion.2 = bf16[384,4,128]{2,0,1:T(8,128)(2,1)S(1)} fusion(bf16[4,4,48,128]{3,2,1,0:T(8,128)(2,1)} %reshape.144, s32[4,48]{1,0:T(4,128)S(1)} %eq.102), kind=kOutput, calls=%fused_computation.4 | convolution fusion | flops 75767808 | bytes 590592 | tf_op jit(solution)/shard_map/qln,lrnb->qrb/dot_general | solution.py:62
  8.8 0.3 copy.58
  9.2 1.3 %pad_maximum_fusion = bf16[4,128,4,128]{3,0,2,1:T(4,128)(2,1)} fusion(bf16[1,128,4,128]{3,0,2,1:T(2,128)(2,1)S(1)} %copy.59, bf16[3,128,4,128]{3,0,2,1:T(4,128)(2,1)S(1)} %copy.58), kind=kLoop, calls=%fused_computation.14 | loop fusion | flops 1048576 | bytes 1048576 | tf_op jit(solution)/shard_map/concatenate | solution.py:65
  10.5 11.9 %all-to-all-start = ((bf16[4,128,4,128]{3,0,2,1:T(4,128)(2,1)}), bf16[4,128,4,128]{3,0,2,1:T(4,128)(2,1)}, u32[]{:S(2)}, u32[]{:S(2)}) async-start(bf16[4,128,4,128]{3,0,2,1:T(4,128)(2,1)} %pad_maximum_fusion), calls=%async_computation | async-start | bytes 1048576 | tf_op jit(solution)/shard_map/all_to_all | solution.py:68
  22.5 0.1 eq.97
  22.6 0.1 eq.93
  22.6 0.7 %iota_compare_fusion.4 = pred[4,48,128]{2,1,0:T(8,128)(4,1)} fusion(s32[4,48]{1,0:T(4,128)S(1)} %eq.97), kind=kLoop, calls=%fused_computation.38 | loop fusion | flops 24576 | bytes 25344 | tf_op jit(solution)/shard_map/eq | solution.py:100
  23.4 0.6 add_divide_fusion
  24.0 11.7 %all-to-all-done = bf16[4,128,4,128]{3,0,2,1:T(4,128)(2,1)} async-done(((bf16[4,128,4,128]{3,0,2,1:T(4,128)(2,1)}), bf16[4,128,4,128]{3,0,2,1:T(4,128)(2,1)}, u32[]{:S(2)}, u32[]{:S(2)}) %all-to-all-start) | async-done | bytes 524320 | tf_op jit(solution)/shard_map/all_to_all | solution.py:68
  35.7 1.2 %copy.60 = bf16[3,128,4,128]{3,2,1,0:T(4,128)(2,1)S(1)} copy(bf16[3,128,4,128]{3,0,2,1:T(4,128)(2,1)} %bitcast.65) | data formatting | bytes 786432 | tf_op jit(solution)/shard_map/slice | solution.py:71
  36.9 1.6 %fusion = f32[3,128,512]{1,2,0:T(8,128)S(1)} fusion(bf16[3,512,128]{2,1,0:T(8,128)(2,1)S(1)} %bitcast.66, f32[1,3,512,512]{3,2,1,0:T(8,128)S(1)} %copy-done), kind=kOutput, calls=%fused_computation.1 | convolution fusion | flops 1207959552 | bytes 4325376 | tf_op jit(solution)/shard_map/cij,cjb->cib/dot_general | solution.py:87
  38.5 1.8 %multiply_reduce_fusion = (f32[3]{0:T(128)S(1)}, f32[3,512,128]{2,1,0:T(8,128)S(1)}) fusion(f32[3,128,512]{1,2,0:T(8,128)S(1)} %fusion, f32[1,3,128,128]{3,2,1,0:T(8,128)} %param.17), kind=kOutput, calls=%fused_computation.12 | convolution fusion | flops 302383104 | bytes 1769484 | tf_op jit(solution)/shard_map/cib,cbd->cid/dot_general | solution.py:90
  40.3 1.2 %fusion.20 = f32[3]{0:T(128)S(1)} fusion(bf16[4,128,4,128]{3,0,2,1:T(4,128)(2,1)} %all-to-all-done), kind=kLoop, calls=%fused_computation.35 | loop fusion | flops 1533 | bytes 1548 | tf_op jit(solution)/shard_map/reduce_sum | solution.py:72
  41.5 0.1 broadcast_multiply_fusion
  41.7 1.0 %copy.63 = f32[3,128,4,128]{3,2,0,1:T(4,128)} copy(f32[3,128,4,128]{3,2,1,0:T(4,128)S(1)} %bitcast.69) | data formatting | bytes 1572864 | tf_op jit(solution)/shard_map/reshape | solution.py:94
  42.7 5.6 %all-to-all-start.1 = ((f32[3,128,4,128]{3,2,0,1:T(4,128)}), f32[3,128,4,128]{3,2,0,1:T(4,128)}, u32[]{:S(2)}, u32[]{:S(2)}) async-start(f32[3,128,4,128]{3,2,0,1:T(4,128)} %copy.63), calls=%async_computation.1 | async-start | bytes 1572864 | tf_op jit(solution)/shard_map/all_to_all | solution.py:95
  48.4 1.9 %fusion.3 = f32[1,3,128,128]{3,2,1,0:T(8,128)} fusion(f32[1,3,128,128]{3,2,1,0:T(8,128)} %param.15, bf16[3,512,128]{2,1,0:T(8,128)(2,1)S(1)} %bitcast.67), kind=kOutput, calls=%fused_computation.7 | convolution fusion | flops 50380800 | bytes 786432 | tf_op jit(solution)/shard_map/cib,cid->cbd/dot_general | solution.py:83
  50.3 4.1 %bitcast_add_fusion = f32[1,3,512,512]{3,2,1,0:T(8,128)} fusion(f32[1,3,512,512]{3,2,1,0:T(8,128)} %param.14, bf16[3,512,128]{2,1,0:T(8,128)(2,1)S(1)} %bitcast.68), kind=kOutput, calls=%fused_computation | convolution fusion | flops 202113024 | bytes 6684672 | tf_op jit(solution)/shard_map/cib,cjb->cij/dot_general | solution.py:77
  54.4 10.0 %all-to-all-done.1 = f32[3,128,4,128]{3,2,0,1:T(4,128)} async-done(((f32[3,128,4,128]{3,2,0,1:T(4,128)}), f32[3,128,4,128]{3,2,0,1:T(4,128)}, u32[]{:S(2)}, u32[]{:S(2)}) %all-to-all-start.1) | async-done | bytes 786464 | tf_op jit(solution)/shard_map/all_to_all | solution.py:95
  64.4 1.7 %convolution_bitcast_fusion.1 = f32[4,4,48,128]{3,2,1,0:T(8,128)S(1)} fusion(f32[3,128,4,128]{3,2,0,1:T(4,128)} %all-to-all-done.1, pred[4,48,128]{2,1,0:T(8,128)(4,1)} %iota_compare_fusion.4, pred[4,48,3]{1,2,0:T(4,128)(4,1)S(1)} %iota_compare_fusion.5), kind=kOutput, calls=%fused_computation.5 | convolution fusion | flops 453058560 | bytes 1204800 | tf_op jit(solution)/shard_map/lnqd,qdrb->lnrb/dot_general | solution.py:103
  66.1 0.9 %reshape.149 = f32[4,4,6144]{2,1,0:T(4,128)} reshape(f32[4,4,48,128]{3,2,1,0:T(8,128)S(1)} %convolution_bitcast_fusion.1) | data formatting | bytes 786432 | tf_op jit(solution)/shard_map/reshape | solution.py:108
  (13 shorter events, 0.1 us)
Async XLA Ops:
  0.6 36.2 %copy-start = (f32[1,3,512,512]{3,2,1,0:T(8,128)S(1)}, f32[1,3,512,512]{3,2,1,0:T(8,128)}, u32[]{:S(2)}) copy-start(f32[1,3,512,512]{3,2,1,0:T(8,128)} %param.16) | copy-start | bytes 9437188
  3.4 19.0 %copy-start.4 = (s32[192]{0:T(256)S(1)}, s32[192]{0:T(256)}, u32[]{:S(2)}) copy-start(s32[192]{0:T(256)} %param.18) | copy-start | bytes 2308
  7.5 15.9 %copy-start.1 = (f32[6336]{0:T(1024)S(1)}, f32[6336]{0:T(1024)}, u32[]{:S(2)}) copy-start(f32[6336]{0:T(1024)} %param.19) | copy-start | bytes 76036
  7.5 15.9 %copy-start.2 = (f32[6336]{0:T(1024)S(1)}, f32[6336]{0:T(1024)}, u32[]{:S(2)}) copy-start(f32[6336]{0:T(1024)} %param.21) | copy-start | bytes 76036
  7.5 15.9 %copy-start.3 = (f32[6336]{0:T(1024)S(1)}, f32[6336]{0:T(1024)}, u32[]{:S(2)}) copy-start(f32[6336]{0:T(1024)} %param.20) | copy-start | bytes 76036
  10.5 25.2 %all-to-all-start = ((bf16[4,128,4,128]{3,0,2,1:T(4,128)(2,1)}), bf16[4,128,4,128]{3,0,2,1:T(4,128)(2,1)}, u32[]{:S(2)}, u32[]{:S(2)}) async-start(bf16[4,128,4,128]{3,0,2,1:T(4,128)(2,1)} %pad_maximum_fusion), calls=%async_computation | async-start | bytes 1048576 | tf_op jit(solution)/shard_map/all_to_all | solution.py:68
  42.7 21.7 %all-to-all-start.1 = ((f32[3,128,4,128]{3,2,0,1:T(4,128)}), f32[3,128,4,128]{3,2,0,1:T(4,128)}, u32[]{:S(2)}, u32[]{:S(2)}) async-start(f32[3,128,4,128]{3,2,0,1:T(4,128)} %copy.63), calls=%async_computation.1 | async-start | bytes 1572864 | tf_op jit(solution)/shard_map/all_to_all | solution.py:95

commit v13 on v11

--- a/solution.py
+++ b/solution.py
@@ -44,7 +44,10 @@
         .reshape(slot_count * devices, layer_count, block_count)
     )
     grad_wide = gradients.astype(jnp.float32)
-    mean_out, square_out, direction = adam_moments(grad_wide, adam_mean, adam_square)
+    _, _, direction = adam_moments(grad_wide, adam_mean, adam_square)
+    mean_out, square_out, _ = adam_moments(
+        *lax.optimization_barrier((grad_wide, adam_mean, adam_square))
+    )
     adam_part = jnp.sum(
         jnp.square(direction).reshape(layer_count, row_count, block_count, BLOCK), axis=(1, 3)
     )

time: 67 us -> 70.3 us (1.049)
  other arithmetic: 8.91 us -> 12.5 us
  waiting for transfers between devices: 23.1 us -> 20.7 us
  local copies, waits for them, and re-layouts: 5.35 us -> 6.55 us
    all_to_all x1, waiting for transfers between devices: 13 us -> 10.7 us  [per_device(): lax.all_to_all(outgoing, ('shard', 'tensor'), split_axis=1, concat_axis=1...]
    add x0 -> x1, other arithmetic: none -> 2.3 us  [adam_moments(): square_new = 0.95 * square_old + 0.05 * grad_wide * grad_wide]
    select_n x1, other arithmetic: 0.34 us -> 1.15 us  [per_device(): jnp.where(lane[None, :] == 0, part_hi[:, None], jnp.where(lane[None, :] =...]
  transfers between devices with their start and end apart: 2 -> 2, of which waited for: 2 -> 2; matrix products, arithmetic and copies ran while one was open for 11% -> 14% of each run, Pallas kernels for 0% -> 0%
where the time goes in v13:
time: 70.3 us; the launch traced here: 69.7 us
  waiting for transfers between devices  20.7 us (29%)
  starting transfers between devices  17.6 us (25%)
  other arithmetic  12.5 us (18%)
  matrix products  11.5 us (16%)
  local copies, waits for them, and re-layouts  6.55 us (9%)
  between operations  0.83 us (1%)
    all_to_all x1, starting transfers between devices, per_device(): lax.all_to_all(outgoing, ('shard', 'tensor'), split_axis=1, concat_axis=1...  11.9 us
    all_to_all x1, waiting for transfers between devices, per_device(): lax.all_to_all(outgoing, ('shard', 'tensor'), split_axis=1, concat_axis=1...  10.7 us
    all_to_all x1, waiting for transfers between devices, per_device(): lax.all_to_all(shaped, ('shard', 'tensor'), split_axis=1, concat_axis=1,...  10 us
    all_to_all x1, starting transfers between devices, per_device(): lax.all_to_all(shaped, ('shard', 'tensor'), split_axis=1, concat_axis=1,...  5.7 us
    dot_general x1, matrix products, per_device(): jnp.einsum('cib,cjb->cij', block_grads, block_grads, preferred_element_ty...  4.13 us
    add x1, other arithmetic, adam_moments(): square_new = 0.95 * square_old + 0.05 * grad_wide * grad_wide  2.3 us
    reduce_sum x2, other arithmetic, per_device(): jnp.sum(jnp.square(direction).reshape(layer_count, row_count, block_count...  2.26 us
    dot_general x1, matrix products, per_device(): jnp.einsum('cib,cid->cbd', block_grads, block_grads, preferred_element_ty...  1.92 us
  transfers between devices with their start and end apart: 2, of which 2 were waited for; matrix products, arithmetic and copies ran while one was open for 14% of the time, Pallas kernels for 0%

profile of v13, /device:TPU:1, one launch (start us, length us, event | category | flops | bytes accessed | tf_op | source)
XLA Modules:
  0.0 69.7 jit_solution(8816606330855621230)
XLA Ops:
  0.6 0.5 iota_compare_fusion.6
  1.2 2.2 %multiply_reduce_fusion.1 = f32[4,6144]{1,0:T(4,128)S(1)} fusion(f32[4,4,6144]{2,1,0:T(4,128)} %param.13, f32[4,4,6144]{2,1,0:T(4,128)} %param.12, bf16[4,4,6144]{2,1,0:T(4,128)(2,1)} %param.11), kind=kLoop, calls=%fused_computation.23 | loop fusion | flops 1155072 | bytes 1081344 | tf_op jit(solution)/shard_map/reduce_sum | solution.py:51
  3.3 0.1 bitcast_reduce_fusion
  3.5 0.6 convert_element_type.60
  4.0 1.1 %reshape.189 = bf16[4,4,48,128]{3,2,1,0:T(8,128)(2,1)S(1)} reshape(bf16[4,4,6144]{2,1,0:T(4,128)(2,1)} %param.11) | data formatting | bytes 393216 | tf_op jit(solution)/shard_map/reshape | solution.py:68
  5.1 0.9 %convert_reduce_fusion = s32[192]{0:T(256)S(1)} fusion(s32[192]{0:T(256)} %param.18), kind=kLoop, calls=%fused_computation.32 | loop fusion | flops 184128 | bytes 1536 | tf_op jit(solution)/shard_map/reduce_sum | solution.py:38
  6.0 0.7 multiply_add_fusion.2
  6.8 0.9 %fusion.4 = bf16[384,2]{0,1:T(2,128)(2,1)S(1)} fusion(s32[4,48]{1,0:T(4,128)S(1)} %eq.124, bf16[4,48,1]{1,2,0:T(2,128)(2,1)S(1)} %subtract_convert_fusion, bf16[4,48,1]{1,2,0:T(2,128)(2,1)} %convert_element_type.60), kind=kOutput, calls=%fused_computation.9 | convolution fusion | flops 370944 | bytes 3072 | tf_op jit(solution)/shard_map/qln,lnk->qk/dot_general | solution.py:56
  7.7 0.7 %copy.54 = bf16[3,128]{0,1:T(8,128)(2,1)} copy(bf16[3,128]{1,0:T(4,128)(2,1)S(1)} %bitcast.71) | data formatting | bytes 1536 | tf_op jit(solution)/shard_map/jit(_where)/broadcast_in_dim | solution.py:66
  8.5 0.7 %copy.53 = bf16[3,128]{0,1:T(8,128)(2,1)} copy(bf16[3,128]{1,0:T(4,128)(2,1)S(1)} %bitcast.70) | data formatting | bytes 1536 | tf_op jit(solution)/shard_map/jit(_where)/broadcast_in_dim | solution.py:63
  9.2 0.4 fusion.2
  9.7 0.3 copy.55
  10.0 1.1 %select_select_fusion = bf16[3,128,1,128]{3,0,2,1:T(4,128)(2,1)S(1)} fusion(pred[128]{0:T(512)(128)(4,1)} %get-tuple-element.23, pred[128]{0:T(512)(128)(4,1)} %get-tuple-element.24, bf16[3,128]{0,1:T(8,128)(2,1)} %copy.54, bf16[3,128]{0,1:T(8,128)(2,1)} %copy.53), kind=kLoop, calls=%fused_computation.39 | loop fusion | flops 98304 | bytes 100096 | tf_op jit(solution)/shard_map/jit(_where)/select_n | solution.py:63
  11.2 1.3 %pad_maximum_fusion = bf16[3,128,5,128]{3,0,2,1:T(4,128)(2,1)} fusion(bf16[3,128,1,128]{3,0,2,1:T(4,128)(2,1)S(1)} %select_select_fusion, bf16[3,128,4,128]{3,0,2,1:T(4,128)(2,1)S(1)} %copy.55), kind=kLoop, calls=%fused_computation.13 | loop fusion | flops 245760 | bytes 983040 | tf_op jit(solution)/shard_map/concatenate | solution.py:72
  12.4 11.9 %all-to-all-start = ((bf16[3,128,5,128]{3,0,2,1:T(4,128)(2,1)}), bf16[3,128,5,128]{3,0,2,1:T(4,128)(2,1)}, u32[]{:S(2)}, u32[]{:S(2)}) async-start(bf16[3,128,5,128]{3,0,2,1:T(4,128)(2,1)} %pad_maximum_fusion), calls=%async_computation | async-start | bytes 1310720 | tf_op jit(solution)/shard_map/all_to_all | solution.py:74
  24.4 2.3 %fusion.11 = (f32[4,4,6144]{2,1,0:T(4,128)}, f32[4,4,6144]{2,1,0:T(4,128)}) fusion(f32[4,4,6144]{2,1,0:T(4,128)S(1)} %convert_element_type.59, f32[4,4,6144]{2,1,0:T(4,128)} %param.13, f32[4,4,6144]{2,1,0:T(4,128)} %param.12), kind=kLoop, calls=%fused_computation.20 | loop fusion | flops 688128 | bytes 1966080 | tf_op jit(solution)/shard_map/add | solution.py:14
  26.8 0.7 %iota_compare_fusion.4 = pred[4,48,128]{2,1,0:T(8,128)(4,1)} fusion(s32[4,48]{1,0:T(4,128)S(1)} %eq.119), kind=kLoop, calls=%fused_computation.41 | loop fusion | flops 24576 | bytes 25344 | tf_op jit(solution)/shard_map/eq | solution.py:108
  27.6 0.6 add_divide_fusion
  28.2 10.7 %all-to-all-done = bf16[3,128,5,128]{3,0,2,1:T(4,128)(2,1)} async-done(((bf16[3,128,5,128]{3,0,2,1:T(4,128)(2,1)}), bf16[3,128,5,128]{3,0,2,1:T(4,128)(2,1)}, u32[]{:S(2)}, u32[]{:S(2)}) %all-to-all-start) | async-done | bytes 491552 | tf_op jit(solution)/shard_map/all_to_all | solution.py:74
  38.9 1.3 %slice.22 = bf16[3,128,4,128]{3,0,2,1:T(4,128)(2,1)S(1)} slice(bf16[3,128,5,128]{3,0,2,1:T(4,128)(2,1)} %all-to-all-done), slice={[0:3], [0:128], [0:4], [0:128]} | slice | bytes 786432 | tf_op jit(solution)/shard_map/slice | solution.py:77
  40.2 0.2 copy.56
  40.4 1.6 %fusion = f32[3,128,512]{1,2,0:T(8,128)S(1)} fusion(bf16[3,512,128]{2,1,0:T(8,128)(2,1)S(1)} %bitcast.62, f32[1,3,512,512]{3,2,1,0:T(8,128)S(1)} %copy-done), kind=kOutput, calls=%fused_computation.1 | convolution fusion | flops 1207959552 | bytes 4325376 | tf_op jit(solution)/shard_map/cij,cjb->cib/dot_general | solution.py:95
  41.9 0.9 %multiply_reduce_fusion = (f32[3]{0:T(128)S(1)}, f32[3,512,128]{2,1,0:T(8,128)S(1)}) fusion(f32[3,128,512]{1,2,0:T(8,128)S(1)} %fusion, f32[1,3,128,128]{3,2,1,0:T(8,128)S(1)} %copy-done.2), kind=kOutput, calls=%fused_computation.12 | convolution fusion | flops 302383104 | bytes 1769484 | tf_op jit(solution)/shard_map/cib,cbd->cid/dot_general | solution.py:98
  42.8 1.3 %add_reduce_fusion = f32[3]{0:T(128)S(1)} fusion(bf16[3,128,5,128]{3,0,2,1:T(4,128)(2,1)} %all-to-all-done), kind=kLoop, calls=%fused_computation.29 | loop fusion | flops 1533 | bytes 1548 | tf_op jit(solution)/shard_map/reduce_sum | solution.py:78
  44.1 0.1 broadcast_multiply_fusion
  44.3 1.0 %copy.59 = f32[3,128,4,128]{3,2,0,1:T(4,128)} copy(f32[3,128,4,128]{3,2,1,0:T(4,128)S(1)} %bitcast.65) | data formatting | bytes 1572864 | tf_op jit(solution)/shard_map/reshape | solution.py:102
  45.3 5.7 %all-to-all-start.1 = ((f32[3,128,4,128]{3,2,0,1:T(4,128)}), f32[3,128,4,128]{3,2,0,1:T(4,128)}, u32[]{:S(2)}, u32[]{:S(2)}) async-start(f32[3,128,4,128]{3,2,0,1:T(4,128)} %copy.59), calls=%async_computation.1 | async-start | bytes 1572864 | tf_op jit(solution)/shard_map/all_to_all | solution.py:103
  51.1 1.9 %fusion.3 = f32[1,3,128,128]{3,2,1,0:T(8,128)} fusion(f32[1,3,128,128]{3,2,1,0:T(8,128)} %param.15, bf16[3,512,128]{2,1,0:T(8,128)(2,1)S(1)} %bitcast.63), kind=kOutput, calls=%fused_computation.7 | convolution fusion | flops 50380800 | bytes 786432 | tf_op jit(solution)/shard_map/cib,cid->cbd/dot_general | solution.py:91
  53.0 4.1 %bitcast_add_fusion = f32[1,3,512,512]{3,2,1,0:T(8,128)} fusion(f32[1,3,512,512]{3,2,1,0:T(8,128)} %param.14, bf16[3,512,128]{2,1,0:T(8,128)(2,1)S(1)} %bitcast.64), kind=kOutput, calls=%fused_computation | convolution fusion | flops 202113024 | bytes 6684672 | tf_op jit(solution)/shard_map/cib,cjb->cij/dot_general | solution.py:85
  57.1 10.0 %all-to-all-done.1 = f32[3,128,4,128]{3,2,0,1:T(4,128)} async-done(((f32[3,128,4,128]{3,2,0,1:T(4,128)}), f32[3,128,4,128]{3,2,0,1:T(4,128)}, u32[]{:S(2)}, u32[]{:S(2)}) %all-to-all-start.1) | async-done | bytes 786464 | tf_op jit(solution)/shard_map/all_to_all | solution.py:103
  67.1 1.7 %convolution_bitcast_fusion.1 = f32[4,4,48,128]{3,2,1,0:T(8,128)S(1)} fusion(f32[3,128,4,128]{3,2,0,1:T(4,128)} %all-to-all-done.1, pred[4,48,128]{2,1,0:T(8,128)(4,1)} %iota_compare_fusion.4, pred[4,48,3]{1,2,0:T(4,128)(4,1)S(1)} %iota_compare_fusion.5), kind=kOutput, calls=%fused_computation.5 | convolution fusion | flops 453058560 | bytes 1204800 | tf_op jit(solution)/shard_map/lnqd,qdrb->lnrb/dot_general | solution.py:111
  68.8 0.9 %reshape.192 = f32[4,4,6144]{2,1,0:T(4,128)} reshape(f32[4,4,48,128]{3,2,1,0:T(8,128)S(1)} %convolution_bitcast_fusion.1) | data formatting | bytes 786432 | tf_op jit(solution)/shard_map/reshape | solution.py:116
  (22 shorter events, 0.4 us)
Async XLA Ops:
  0.6 39.7 %copy-start = (f32[1,3,512,512]{3,2,1,0:T(8,128)S(1)}, f32[1,3,512,512]{3,2,1,0:T(8,128)}, u32[]{:S(2)}) copy-start(f32[1,3,512,512]{3,2,1,0:T(8,128)} %param.16) | copy-start | bytes 9437188
  1.2 23.2 %copy-start.1 = (bf16[4,4,6144]{2,1,0:T(4,128)(2,1)S(1)}, bf16[4,4,6144]{2,1,0:T(4,128)(2,1)}, u32[]{:S(2)}) copy-start(bf16[4,4,6144]{2,1,0:T(4,128)(2,1)} %param.11) | copy-start | bytes 589828
  9.6 17.1 %copy-start.6 = (s32[192]{0:T(256)S(1)}, s32[192]{0:T(256)}, u32[]{:S(2)}) copy-start(s32[192]{0:T(256)} %param.18) | copy-start | bytes 2308
  9.6 17.9 %copy-start.3 = (f32[6336]{0:T(1024)S(1)}, f32[6336]{0:T(1024)}, u32[]{:S(2)}) copy-start(f32[6336]{0:T(1024)} %param.19) | copy-start | bytes 76036
  9.6 17.9 %copy-start.4 = (f32[6336]{0:T(1024)S(1)}, f32[6336]{0:T(1024)}, u32[]{:S(2)}) copy-start(f32[6336]{0:T(1024)} %param.21) | copy-start | bytes 76036
  9.6 17.9 %copy-start.5 = (f32[6336]{0:T(1024)S(1)}, f32[6336]{0:T(1024)}, u32[]{:S(2)}) copy-start(f32[6336]{0:T(1024)} %param.20) | copy-start | bytes 76036
  12.4 26.5 %all-to-all-start = ((bf16[3,128,5,128]{3,0,2,1:T(4,128)(2,1)}), bf16[3,128,5,128]{3,0,2,1:T(4,128)(2,1)}, u32[]{:S(2)}, u32[]{:S(2)}) async-start(bf16[3,128,5,128]{3,0,2,1:T(4,128)(2,1)} %pad_maximum_fusion), calls=%async_computation | async-start | bytes 1310720 | tf_op jit(solution)/shard_map/all_to_all | solution.py:74
  38.9 3.0 %copy-start.2 = (f32[1,3,128,128]{3,2,1,0:T(8,128)S(1)}, f32[1,3,128,128]{3,2,1,0:T(8,128)}, u32[]{:S(2)}) copy-start(f32[1,3,128,128]{3,2,1,0:T(8,128)} %param.17) | copy-start | bytes 589828
  45.3 21.8 %all-to-all-start.1 = ((f32[3,128,4,128]{3,2,0,1:T(4,128)}), f32[3,128,4,128]{3,2,0,1:T(4,128)}, u32[]{:S(2)}, u32[]{:S(2)}) async-start(f32[3,128,4,128]{3,2,0,1:T(4,128)} %copy.59), calls=%async_computation.1 | async-start | bytes 1572864 | tf_op jit(solution)/shard_map/all_to_all | solution.py:103

commit v14 on v11

--- a/solution.py
+++ b/solution.py
@@ -7,6 +7,7 @@
 
 
 PRECISE = lax.Precision.HIGHEST
+NEAR = lax.Precision.HIGH
 
 
 def adam_moments(grad_wide, mean_old, square_old):
@@ -90,9 +91,9 @@
         ]
     )
     left_applied = jnp.einsum(
-        "cij,cjb->cib", root_left[0], block_grads.astype(jnp.float32), precision=PRECISE
+        "cij,cjb->cib", root_left[0], block_grads.astype(jnp.float32), precision=NEAR
     )
-    precond = jnp.einsum("cib,cbd->cid", left_applied, root_right[0], precision=PRECISE)
+    precond = jnp.einsum("cib,cbd->cid", left_applied, root_right[0], precision=NEAR)
     precond_sums = jnp.sum(jnp.square(precond), axis=(1, 2))
     graft_ratio = jnp.sqrt(adam_sums / (precond_sums + 1e-06))
     scaled = precond * graft_ratio[:, None, None]

time: 67 us -> 66.1 us (0.987)
  matrix products: 10.8 us -> 9.93 us
where the time goes in v14:
time: 66.1 us; the launch traced here: 65.7 us
  waiting for transfers between devices  23.1 us (35%)
  starting transfers between devices  17.6 us (27%)
  matrix products  9.93 us (15%)
  other arithmetic  8.91 us (13%)
  local copies, waits for them, and re-layouts  5.35 us (8%)
  between operations  0.83 us (1%)
    all_to_all x1, waiting for transfers between devices, per_device(): lax.all_to_all(outgoing, ('shard', 'tensor'), split_axis=1, concat_axis=1...  13 us
    all_to_all x1, starting transfers between devices, per_device(): lax.all_to_all(outgoing, ('shard', 'tensor'), split_axis=1, concat_axis=1...  11.9 us
    all_to_all x1, waiting for transfers between devices, per_device(): lax.all_to_all(shaped, ('shard', 'tensor'), split_axis=1, concat_axis=1,...  10 us
    all_to_all x1, starting transfers between devices, per_device(): lax.all_to_all(shaped, ('shard', 'tensor'), split_axis=1, concat_axis=1,...  5.7 us
    dot_general x1, matrix products, per_device(): jnp.einsum('cib,cjb->cij', block_grads, block_grads, preferred_element_ty...  4.12 us
    reduce_sum x2, other arithmetic, per_device(): jnp.sum(jnp.square(direction).reshape(layer_count, row_count, block_count...  2.87 us
    dot_general x1, matrix products, per_device(): jnp.einsum('cib,cid->cbd', block_grads, block_grads, preferred_element_ty...  1.91 us
    dot_general x1, matrix products, per_device(): jnp.einsum('lnqd,qdrb->lnrb', placer, returned, precision=PRECISE, prefer...  1.7 us
  transfers between devices with their start and end apart: 2, of which 2 were waited for; matrix products, arithmetic and copies ran while one was open for 11% of the time, Pallas kernels for 0%

profile of v14, /device:TPU:1, one launch (start us, length us, event | category | flops | bytes accessed | tf_op | source)
XLA Modules:
  0.0 65.7 jit_solution(8255429114305748935)
XLA Ops:
  0.7 2.8 %multiply_reduce_fusion.1 = (f32[4,6144]{1,0:T(4,128)S(1)}, f32[4,4,6144]{2,1,0:T(4,128)}, f32[4,4,6144]{2,1,0:T(4,128)}) fusion(bf16[4,4,6144]{2,1,0:T(4,128)(2,1)} %param.11, f32[4,4,6144]{2,1,0:T(4,128)} %param.13, f32[4,4,6144]{2,1,0:T(4,128)} %param.12), kind=kLoop, calls=%fused_computation.19 | loop fusion | flops 1155072 | bytes 1867776 | tf_op jit(solution)/shard_map/reduce_sum | solution.py:49
  3.5 0.1 bitcast_reduce_fusion
  3.6 1.1 %reshape.189 = bf16[4,4,48,128]{3,2,1,0:T(8,128)(2,1)S(1)} reshape(bf16[4,4,6144]{2,1,0:T(4,128)(2,1)} %param.11) | data formatting | bytes 393216 | tf_op jit(solution)/shard_map/reshape | solution.py:66
  4.7 0.9 %convert_reduce_fusion = s32[192]{0:T(256)S(1)} fusion(s32[192]{0:T(256)} %param.18), kind=kLoop, calls=%fused_computation.28 | loop fusion | flops 184128 | bytes 1536 | tf_op jit(solution)/shard_map/reduce_sum | solution.py:39
  5.6 0.7 %multiply_add_fusion.1 = s32[192]{0:T(256)S(1)} fusion(s32[192]{0:T(256)} %param.18, s32[192]{0:T(256)S(1)} %convert_reduce_fusion), kind=kLoop, calls=%fused_computation.49 | loop fusion | flops 384 | bytes 2304 | tf_op jit(solution)/shard_map/add | solution.py:40
  6.3 0.1 eq.124
  6.4 0.2 fusion.4
  6.6 0.1 copy.54
  6.8 0.1 copy.53
  6.9 0.4 fusion.2
  7.3 0.3 copy.55
  7.7 0.3 select_select_fusion
  8.0 1.3 %pad_maximum_fusion = bf16[3,128,5,128]{3,0,2,1:T(4,128)(2,1)} fusion(bf16[3,128,1,128]{3,0,2,1:T(4,128)(2,1)S(1)} %select_select_fusion, bf16[3,128,4,128]{3,0,2,1:T(4,128)(2,1)S(1)} %copy.55), kind=kLoop, calls=%fused_computation.13 | loop fusion | flops 245760 | bytes 983040 | tf_op jit(solution)/shard_map/concatenate | solution.py:70
  9.3 11.9 %all-to-all-start = ((bf16[3,128,5,128]{3,0,2,1:T(4,128)(2,1)}), bf16[3,128,5,128]{3,0,2,1:T(4,128)(2,1)}, u32[]{:S(2)}, u32[]{:S(2)}) async-start(bf16[3,128,5,128]{3,0,2,1:T(4,128)(2,1)} %pad_maximum_fusion), calls=%async_computation | async-start | bytes 1310720 | tf_op jit(solution)/shard_map/all_to_all | solution.py:72
  21.2 0.1 eq.119
  21.3 0.1 eq.115
  21.4 0.7 %iota_compare_fusion.4 = pred[4,48,128]{2,1,0:T(8,128)(4,1)} fusion(s32[4,48]{1,0:T(4,128)S(1)} %eq.119), kind=kLoop, calls=%fused_computation.37 | loop fusion | flops 24576 | bytes 25344 | tf_op jit(solution)/shard_map/eq | solution.py:106
  22.1 0.6 add_divide_fusion
  22.7 13.0 %all-to-all-done = bf16[3,128,5,128]{3,0,2,1:T(4,128)(2,1)} async-done(((bf16[3,128,5,128]{3,0,2,1:T(4,128)(2,1)}), bf16[3,128,5,128]{3,0,2,1:T(4,128)(2,1)}, u32[]{:S(2)}, u32[]{:S(2)}) %all-to-all-start) | async-done | bytes 491552 | tf_op jit(solution)/shard_map/all_to_all | solution.py:72
  35.7 1.3 %slice.22 = bf16[3,128,4,128]{3,0,2,1:T(4,128)(2,1)S(1)} slice(bf16[3,128,5,128]{3,0,2,1:T(4,128)(2,1)} %all-to-all-done), slice={[0:3], [0:128], [0:4], [0:128]} | slice | bytes 786432 | tf_op jit(solution)/shard_map/slice | solution.py:75
  37.0 0.2 copy.56
  37.2 1.0 %fusion = f32[3,128,512]{1,2,0:T(8,128)S(1)} fusion(bf16[3,512,128]{2,1,0:T(8,128)(2,1)S(1)} %bitcast.62, f32[1,3,512,512]{3,2,1,0:T(8,128)S(1)} %copy-done), kind=kOutput, calls=%fused_computation.1 | convolution fusion | flops 603979776 | bytes 4325376 | tf_op jit(solution)/shard_map/cij,cjb->cib/dot_general | solution.py:93
  38.2 0.6 multiply_reduce_fusion
  38.8 1.3 %add_reduce_fusion = f32[3]{0:T(128)S(1)} fusion(bf16[3,128,5,128]{3,0,2,1:T(4,128)(2,1)} %all-to-all-done), kind=kLoop, calls=%fused_computation.25 | loop fusion | flops 1533 | bytes 1548 | tf_op jit(solution)/shard_map/reduce_sum | solution.py:76
  40.1 0.1 broadcast_multiply_fusion
  40.2 1.0 %copy.59 = f32[3,128,4,128]{3,2,0,1:T(4,128)} copy(f32[3,128,4,128]{3,2,1,0:T(4,128)S(1)} %bitcast.65) | data formatting | bytes 1572864 | tf_op jit(solution)/shard_map/reshape | solution.py:100
  41.3 5.7 %all-to-all-start.1 = ((f32[3,128,4,128]{3,2,0,1:T(4,128)}), f32[3,128,4,128]{3,2,0,1:T(4,128)}, u32[]{:S(2)}, u32[]{:S(2)}) async-start(f32[3,128,4,128]{3,2,0,1:T(4,128)} %copy.59), calls=%async_computation.1 | async-start | bytes 1572864 | tf_op jit(solution)/shard_map/all_to_all | solution.py:101
  47.0 1.9 %fusion.3 = f32[1,3,128,128]{3,2,1,0:T(8,128)} fusion(f32[1,3,128,128]{3,2,1,0:T(8,128)} %param.15, bf16[3,512,128]{2,1,0:T(8,128)(2,1)S(1)} %bitcast.63), kind=kOutput, calls=%fused_computation.7 | convolution fusion | flops 50380800 | bytes 786432 | tf_op jit(solution)/shard_map/cib,cid->cbd/dot_general | solution.py:89
  48.9 4.1 %bitcast_add_fusion = f32[1,3,512,512]{3,2,1,0:T(8,128)} fusion(f32[1,3,512,512]{3,2,1,0:T(8,128)} %param.14, bf16[3,512,128]{2,1,0:T(8,128)(2,1)S(1)} %bitcast.64), kind=kOutput, calls=%fused_computation | convolution fusion | flops 202113024 | bytes 6684672 | tf_op jit(solution)/shard_map/cib,cjb->cij/dot_general | solution.py:83
  53.0 10.0 %all-to-all-done.1 = f32[3,128,4,128]{3,2,0,1:T(4,128)} async-done(((f32[3,128,4,128]{3,2,0,1:T(4,128)}), f32[3,128,4,128]{3,2,0,1:T(4,128)}, u32[]{:S(2)}, u32[]{:S(2)}) %all-to-all-start.1) | async-done | bytes 786464 | tf_op jit(solution)/shard_map/all_to_all | solution.py:101
  63.1 1.7 %convolution_bitcast_fusion.1 = f32[4,4,48,128]{3,2,1,0:T(8,128)S(1)} fusion(f32[3,128,4,128]{3,2,0,1:T(4,128)} %all-to-all-done.1, pred[4,48,128]{2,1,0:T(8,128)(4,1)} %iota_compare_fusion.4, pred[4,48,3]{1,2,0:T(4,128)(4,1)S(1)} %iota_compare_fusion.5), kind=kOutput, calls=%fused_computation.5 | convolution fusion | flops 453058560 | bytes 1204800 | tf_op jit(solution)/shard_map/lnqd,qdrb->lnrb/dot_general | solution.py:109
  64.8 0.9 %reshape.192 = f32[4,4,6144]{2,1,0:T(4,128)} reshape(f32[4,4,48,128]{3,2,1,0:T(8,128)S(1)} %convolution_bitcast_fusion.1) | data formatting | bytes 786432 | tf_op jit(solution)/shard_map/reshape | solution.py:114
  (18 shorter events, 0.1 us)
Async XLA Ops:
  0.6 36.6 %copy-start = (f32[1,3,512,512]{3,2,1,0:T(8,128)S(1)}, f32[1,3,512,512]{3,2,1,0:T(8,128)}, u32[]{:S(2)}) copy-start(f32[1,3,512,512]{3,2,1,0:T(8,128)} %param.16) | copy-start | bytes 9437188
  3.4 17.8 %copy-start.5 = (s32[192]{0:T(256)S(1)}, s32[192]{0:T(256)}, u32[]{:S(2)}) copy-start(s32[192]{0:T(256)} %param.18) | copy-start | bytes 2308
  3.4 18.6 %copy-start.2 = (f32[6336]{0:T(1024)S(1)}, f32[6336]{0:T(1024)}, u32[]{:S(2)}) copy-start(f32[6336]{0:T(1024)} %param.19) | copy-start | bytes 76036
  3.5 18.6 %copy-start.3 = (f32[6336]{0:T(1024)S(1)}, f32[6336]{0:T(1024)}, u32[]{:S(2)}) copy-start(f32[6336]{0:T(1024)} %param.21) | copy-start | bytes 76036
  3.5 18.6 %copy-start.4 = (f32[6336]{0:T(1024)S(1)}, f32[6336]{0:T(1024)}, u32[]{:S(2)}) copy-start(f32[6336]{0:T(1024)} %param.20) | copy-start | bytes 76036
  9.3 26.5 %all-to-all-start = ((bf16[3,128,5,128]{3,0,2,1:T(4,128)(2,1)}), bf16[3,128,5,128]{3,0,2,1:T(4,128)(2,1)}, u32[]{:S(2)}, u32[]{:S(2)}) async-start(bf16[3,128,5,128]{3,0,2,1:T(4,128)(2,1)} %pad_maximum_fusion), calls=%async_computation | async-start | bytes 1310720 | tf_op jit(solution)/shard_map/all_to_all | solution.py:72
  35.7 2.5 %copy-start.1 = (f32[1,3,128,128]{3,2,1,0:T(8,128)S(1)}, f32[1,3,128,128]{3,2,1,0:T(8,128)}, u32[]{:S(2)}) copy-start(f32[1,3,128,128]{3,2,1,0:T(8,128)} %param.17) | copy-start | bytes 589828
  41.3 21.8 %all-to-all-start.1 = ((f32[3,128,4,128]{3,2,0,1:T(4,128)}), f32[3,128,4,128]{3,2,0,1:T(4,128)}, u32[]{:S(2)}, u32[]{:S(2)}) async-start(f32[3,128,4,128]{3,2,0,1:T(4,128)} %copy.59), calls=%async_computation.1 | async-start | bytes 1572864 | tf_op jit(solution)/shard_map/all_to_all | solution.py:101

commit v15 on v14

--- a/solution.py
+++ b/solution.py
@@ -107,7 +107,7 @@
     ).astype(jnp.float32).reshape(layer_count, block_count, slot_count, devices)
     updates = (
         jnp.einsum(
-            "lnqd,qdrb->lnrb", placer, returned, precision=PRECISE,
+            "lnqd,qdrb->lnrb", placer, returned, precision=NEAR,
             preferred_element_type=jnp.float32,
         )
         .transpose(0, 2, 1, 3)

time: 66.1 us -> 66 us (level)
  transfers between devices with their start and end apart: 2 -> 2, of which waited for: 2 -> 2; matrix products, arithmetic and copies ran while one was open for 11% -> 12% of each run, Pallas kernels for 0% -> 0%
where the time goes in v15:
time: 66 us; the launch traced here: 65.6 us
  waiting for transfers between devices  23.1 us (35%)
  starting transfers between devices  17.6 us (27%)
  matrix products  9.8 us (15%)
  other arithmetic  8.91 us (14%)
  local copies, waits for them, and re-layouts  5.35 us (8%)
  between operations  0.83 us (1%)
    all_to_all x1, waiting for transfers between devices, per_device(): lax.all_to_all(outgoing, ('shard', 'tensor'), split_axis=1, concat_axis=1...  13 us
    all_to_all x1, starting transfers between devices, per_device(): lax.all_to_all(outgoing, ('shard', 'tensor'), split_axis=1, concat_axis=1...  11.9 us
    all_to_all x1, waiting for transfers between devices, per_device(): lax.all_to_all(shaped, ('shard', 'tensor'), split_axis=1, concat_axis=1,...  10 us
    all_to_all x1, starting transfers between devices, per_device(): lax.all_to_all(shaped, ('shard', 'tensor'), split_axis=1, concat_axis=1,...  5.7 us
    dot_general x1, matrix products, per_device(): jnp.einsum('cib,cjb->cij', block_grads, block_grads, preferred_element_ty...  4.12 us
    reduce_sum x2, other arithmetic, per_device(): jnp.sum(jnp.square(direction).reshape(layer_count, row_count, block_count...  2.87 us
    dot_general x1, matrix products, per_device(): jnp.einsum('cib,cid->cbd', block_grads, block_grads, preferred_element_ty...  1.91 us
    dot_general x1, matrix products, per_device(): jnp.einsum('lnqd,qdrb->lnrb', placer, returned, precision=NEAR, preferred...  1.58 us
  transfers between devices with their start and end apart: 2, of which 2 were waited for; matrix products, arithmetic and copies ran while one was open for 12% of the time, Pallas kernels for 0%

profile of v15, /device:TPU:1, one launch (start us, length us, event | category | flops | bytes accessed | tf_op | source)
XLA Modules:
  0.0 65.6 jit_solution(11587926350873080323)
XLA Ops:
  0.7 2.8 %multiply_reduce_fusion.1 = (f32[4,6144]{1,0:T(4,128)S(1)}, f32[4,4,6144]{2,1,0:T(4,128)}, f32[4,4,6144]{2,1,0:T(4,128)}) fusion(bf16[4,4,6144]{2,1,0:T(4,128)(2,1)} %param.11, f32[4,4,6144]{2,1,0:T(4,128)} %param.13, f32[4,4,6144]{2,1,0:T(4,128)} %param.12), kind=kLoop, calls=%fused_computation.19 | loop fusion | flops 1155072 | bytes 1867776 | tf_op jit(solution)/shard_map/reduce_sum | solution.py:49
  3.5 0.1 bitcast_reduce_fusion
  3.6 1.1 %reshape.189 = bf16[4,4,48,128]{3,2,1,0:T(8,128)(2,1)S(1)} reshape(bf16[4,4,6144]{2,1,0:T(4,128)(2,1)} %param.11) | data formatting | bytes 393216 | tf_op jit(solution)/shard_map/reshape | solution.py:66
  4.7 0.9 %convert_reduce_fusion = s32[192]{0:T(256)S(1)} fusion(s32[192]{0:T(256)} %param.18), kind=kLoop, calls=%fused_computation.28 | loop fusion | flops 184128 | bytes 1536 | tf_op jit(solution)/shard_map/reduce_sum | solution.py:39
  5.6 0.7 %multiply_add_fusion.1 = s32[192]{0:T(256)S(1)} fusion(s32[192]{0:T(256)} %param.18, s32[192]{0:T(256)S(1)} %convert_reduce_fusion), kind=kLoop, calls=%fused_computation.49 | loop fusion | flops 384 | bytes 2304 | tf_op jit(solution)/shard_map/add | solution.py:40
  6.3 0.1 eq.124
  6.4 0.2 fusion.4
  6.6 0.1 copy.54
  6.8 0.1 copy.53
  6.9 0.4 fusion.2
  7.3 0.3 copy.55
  7.7 0.3 select_select_fusion
  8.0 1.3 %pad_maximum_fusion = bf16[3,128,5,128]{3,0,2,1:T(4,128)(2,1)} fusion(bf16[3,128,1,128]{3,0,2,1:T(4,128)(2,1)S(1)} %select_select_fusion, bf16[3,128,4,128]{3,0,2,1:T(4,128)(2,1)S(1)} %copy.55), kind=kLoop, calls=%fused_computation.13 | loop fusion | flops 245760 | bytes 983040 | tf_op jit(solution)/shard_map/concatenate | solution.py:70
  9.3 11.9 %all-to-all-start = ((bf16[3,128,5,128]{3,0,2,1:T(4,128)(2,1)}), bf16[3,128,5,128]{3,0,2,1:T(4,128)(2,1)}, u32[]{:S(2)}, u32[]{:S(2)}) async-start(bf16[3,128,5,128]{3,0,2,1:T(4,128)(2,1)} %pad_maximum_fusion), calls=%async_computation | async-start | bytes 1310720 | tf_op jit(solution)/shard_map/all_to_all | solution.py:72
  21.2 0.1 eq.119
  21.3 0.1 eq.115
  21.4 0.7 %iota_compare_fusion.4 = pred[4,48,128]{2,1,0:T(8,128)(4,1)} fusion(s32[4,48]{1,0:T(4,128)S(1)} %eq.119), kind=kLoop, calls=%fused_computation.37 | loop fusion | flops 24576 | bytes 25344 | tf_op jit(solution)/shard_map/eq | solution.py:106
  22.1 0.6 add_divide_fusion
  22.7 13.0 %all-to-all-done = bf16[3,128,5,128]{3,0,2,1:T(4,128)(2,1)} async-done(((bf16[3,128,5,128]{3,0,2,1:T(4,128)(2,1)}), bf16[3,128,5,128]{3,0,2,1:T(4,128)(2,1)}, u32[]{:S(2)}, u32[]{:S(2)}) %all-to-all-start) | async-done | bytes 491552 | tf_op jit(solution)/shard_map/all_to_all | solution.py:72
  35.7 1.3 %slice.22 = bf16[3,128,4,128]{3,0,2,1:T(4,128)(2,1)S(1)} slice(bf16[3,128,5,128]{3,0,2,1:T(4,128)(2,1)} %all-to-all-done), slice={[0:3], [0:128], [0:4], [0:128]} | slice | bytes 786432 | tf_op jit(solution)/shard_map/slice | solution.py:75
  37.0 0.2 copy.56
  37.2 1.0 %fusion = f32[3,128,512]{1,2,0:T(8,128)S(1)} fusion(bf16[3,512,128]{2,1,0:T(8,128)(2,1)S(1)} %bitcast.62, f32[1,3,512,512]{3,2,1,0:T(8,128)S(1)} %copy-done), kind=kOutput, calls=%fused_computation.1 | convolution fusion | flops 603979776 | bytes 4325376 | tf_op jit(solution)/shard_map/cij,cjb->cib/dot_general | solution.py:93
  38.2 0.6 multiply_reduce_fusion
  38.8 1.3 %add_reduce_fusion = f32[3]{0:T(128)S(1)} fusion(bf16[3,128,5,128]{3,0,2,1:T(4,128)(2,1)} %all-to-all-done), kind=kLoop, calls=%fused_computation.25 | loop fusion | flops 1533 | bytes 1548 | tf_op jit(solution)/shard_map/reduce_sum | solution.py:76
  40.1 0.1 broadcast_multiply_fusion
  40.2 1.0 %copy.59 = f32[3,128,4,128]{3,2,0,1:T(4,128)} copy(f32[3,128,4,128]{3,2,1,0:T(4,128)S(1)} %bitcast.65) | data formatting | bytes 1572864 | tf_op jit(solution)/shard_map/reshape | solution.py:100
  41.3 5.7 %all-to-all-start.1 = ((f32[3,128,4,128]{3,2,0,1:T(4,128)}), f32[3,128,4,128]{3,2,0,1:T(4,128)}, u32[]{:S(2)}, u32[]{:S(2)}) async-start(f32[3,128,4,128]{3,2,0,1:T(4,128)} %copy.59), calls=%async_computation.1 | async-start | bytes 1572864 | tf_op jit(solution)/shard_map/all_to_all | solution.py:101
  47.0 1.9 %fusion.3 = f32[1,3,128,128]{3,2,1,0:T(8,128)} fusion(f32[1,3,128,128]{3,2,1,0:T(8,128)} %param.15, bf16[3,512,128]{2,1,0:T(8,128)(2,1)S(1)} %bitcast.63), kind=kOutput, calls=%fused_computation.7 | convolution fusion | flops 50380800 | bytes 786432 | tf_op jit(solution)/shard_map/cib,cid->cbd/dot_general | solution.py:89
  48.9 4.1 %bitcast_add_fusion = f32[1,3,512,512]{3,2,1,0:T(8,128)} fusion(f32[1,3,512,512]{3,2,1,0:T(8,128)} %param.14, bf16[3,512,128]{2,1,0:T(8,128)(2,1)S(1)} %bitcast.64), kind=kOutput, calls=%fused_computation | convolution fusion | flops 202113024 | bytes 6684672 | tf_op jit(solution)/shard_map/cib,cjb->cij/dot_general | solution.py:83
  53.0 10.0 %all-to-all-done.1 = f32[3,128,4,128]{3,2,0,1:T(4,128)} async-done(((f32[3,128,4,128]{3,2,0,1:T(4,128)}), f32[3,128,4,128]{3,2,0,1:T(4,128)}, u32[]{:S(2)}, u32[]{:S(2)}) %all-to-all-start.1) | async-done | bytes 786464 | tf_op jit(solution)/shard_map/all_to_all | solution.py:101
  63.1 1.6 %convolution_bitcast_fusion.1 = f32[4,4,48,128]{3,2,1,0:T(8,128)S(1)} fusion(f32[3,128,4,128]{3,2,0,1:T(4,128)} %all-to-all-done.1, pred[4,48,128]{2,1,0:T(8,128)(4,1)} %iota_compare_fusion.4, pred[4,48,3]{1,2,0:T(4,128)(4,1)S(1)} %iota_compare_fusion.5), kind=kOutput, calls=%fused_computation.5 | convolution fusion | flops 226566144 | bytes 1204800 | tf_op jit(solution)/shard_map/lnqd,qdrb->lnrb/dot_general | solution.py:109
  64.7 0.9 %reshape.192 = f32[4,4,6144]{2,1,0:T(4,128)} reshape(f32[4,4,48,128]{3,2,1,0:T(8,128)S(1)} %convolution_bitcast_fusion.1) | data formatting | bytes 786432 | tf_op jit(solution)/shard_map/reshape | solution.py:114
  (18 shorter events, 0.1 us)
Async XLA Ops:
  0.6 36.6 %copy-start = (f32[1,3,512,512]{3,2,1,0:T(8,128)S(1)}, f32[1,3,512,512]{3,2,1,0:T(8,128)}, u32[]{:S(2)}) copy-start(f32[1,3,512,512]{3,2,1,0:T(8,128)} %param.16) | copy-start | bytes 9437188
  3.4 17.8 %copy-start.5 = (s32[192]{0:T(256)S(1)}, s32[192]{0:T(256)}, u32[]{:S(2)}) copy-start(s32[192]{0:T(256)} %param.18) | copy-start | bytes 2308
  3.4 18.6 %copy-start.2 = (f32[6336]{0:T(1024)S(1)}, f32[6336]{0:T(1024)}, u32[]{:S(2)}) copy-start(f32[6336]{0:T(1024)} %param.19) | copy-start | bytes 76036
  3.5 18.6 %copy-start.3 = (f32[6336]{0:T(1024)S(1)}, f32[6336]{0:T(1024)}, u32[]{:S(2)}) copy-start(f32[6336]{0:T(1024)} %param.21) | copy-start | bytes 76036
  3.5 18.6 %copy-start.4 = (f32[6336]{0:T(1024)S(1)}, f32[6336]{0:T(1024)}, u32[]{:S(2)}) copy-start(f32[6336]{0:T(1024)} %param.20) | copy-start | bytes 76036
  9.3 26.5 %all-to-all-start = ((bf16[3,128,5,128]{3,0,2,1:T(4,128)(2,1)}), bf16[3,128,5,128]{3,0,2,1:T(4,128)(2,1)}, u32[]{:S(2)}, u32[]{:S(2)}) async-start(bf16[3,128,5,128]{3,0,2,1:T(4,128)(2,1)} %pad_maximum_fusion), calls=%async_computation | async-start | bytes 1310720 | tf_op jit(solution)/shard_map/all_to_all | solution.py:72
  35.7 2.5 %copy-start.1 = (f32[1,3,128,128]{3,2,1,0:T(8,128)S(1)}, f32[1,3,128,128]{3,2,1,0:T(8,128)}, u32[]{:S(2)}) copy-start(f32[1,3,128,128]{3,2,1,0:T(8,128)} %param.17) | copy-start | bytes 589828
  41.3 21.8 %all-to-all-start.1 = ((f32[3,128,4,128]{3,2,0,1:T(4,128)}), f32[3,128,4,128]{3,2,0,1:T(4,128)}, u32[]{:S(2)}, u32[]{:S(2)}) async-start(f32[3,128,4,128]{3,2,0,1:T(4,128)} %copy.59), calls=%async_computation.1 | async-start | bytes 1572864 | tf_op jit(solution)/shard_map/all_to_all | solution.py:101

commit v16 on v14

--- a/solution.py
+++ b/solution.py
@@ -36,7 +36,10 @@
     total_blocks = owners.shape[0]
     positions = jnp.arange(total_blocks, dtype=jnp.int32)
     earlier = (owners[:, None] == owners[None, :]) & (positions[None, :] < positions[:, None])
-    slot_index = jnp.sum(earlier.astype(jnp.int32), axis=1)
+    slot_index = jnp.dot(
+        earlier.astype(jnp.bfloat16), jnp.ones((total_blocks,), jnp.bfloat16),
+        preferred_element_type=jnp.float32,
+    ).astype(jnp.int32)
     target = slot_index * devices + owners
     places = jnp.arange(slot_count * devices, dtype=jnp.int32)
     picker = (

time: 66.1 us -> 66.1 us (level)
  matrix products: 9.93 us -> 10.9 us
  other arithmetic: 8.91 us -> 8 us
    dot_general x0 -> x1, matrix products: none -> 0.97 us  [per_device(): jnp.dot(earlier.astype(jnp.bfloat16), jnp.ones((total_blocks,), jnp.bfloa...]
    reduce_sum x1 -> x0, other arithmetic: 0.94 us -> none  [per_device(): slot_index = jnp.sum(earlier.astype(jnp.int32), axis=1)]
  transfers between devices with their start and end apart: 2 -> 2, of which waited for: 2 -> 2; matrix products, arithmetic and copies ran while one was open for 11% -> 12% of each run, Pallas kernels for 0% -> 0%
where the time goes in v16:
time: 66.1 us; the launch traced here: 65.7 us
  waiting for transfers between devices  23.1 us (35%)
  starting transfers between devices  17.6 us (27%)
  matrix products  10.9 us (16%)
  other arithmetic  8 us (12%)
  local copies, waits for them, and re-layouts  5.35 us (8%)
  between operations  0.83 us (1%)
    all_to_all x1, waiting for transfers between devices, per_device(): lax.all_to_all(outgoing, ('shard', 'tensor'), split_axis=1, concat_axis=1...  13 us
    all_to_all x1, starting transfers between devices, per_device(): lax.all_to_all(outgoing, ('shard', 'tensor'), split_axis=1, concat_axis=1...  11.9 us
    all_to_all x1, waiting for transfers between devices, per_device(): lax.all_to_all(shaped, ('shard', 'tensor'), split_axis=1, concat_axis=1,...  10 us
    all_to_all x1, starting transfers between devices, per_device(): lax.all_to_all(shaped, ('shard', 'tensor'), split_axis=1, concat_axis=1,...  5.7 us
    dot_general x1, matrix products, per_device(): jnp.einsum('cib,cjb->cij', block_grads, block_grads, preferred_element_ty...  4.12 us
    reduce_sum x2, other arithmetic, per_device(): jnp.sum(jnp.square(direction).reshape(layer_count, row_count, block_count...  2.87 us
    dot_general x1, matrix products, per_device(): jnp.einsum('cib,cid->cbd', block_grads, block_grads, preferred_element_ty...  1.91 us
    dot_general x1, matrix products, per_device(): jnp.einsum('lnqd,qdrb->lnrb', placer, returned, precision=PRECISE, prefer...  1.7 us
  transfers between devices with their start and end apart: 2, of which 2 were waited for; matrix products, arithmetic and copies ran while one was open for 12% of the time, Pallas kernels for 0%

profile of v16, /device:TPU:1, one launch (start us, length us, event | category | flops | bytes accessed | tf_op | source)
XLA Modules:
  0.0 65.7 jit_solution(13508216350308273994)
XLA Ops:
  0.7 2.8 %multiply_reduce_fusion.1 = (f32[4,6144]{1,0:T(4,128)S(1)}, f32[4,4,6144]{2,1,0:T(4,128)}, f32[4,4,6144]{2,1,0:T(4,128)}) fusion(bf16[4,4,6144]{2,1,0:T(4,128)(2,1)} %param.11, f32[4,4,6144]{2,1,0:T(4,128)} %param.13, f32[4,4,6144]{2,1,0:T(4,128)} %param.12), kind=kLoop, calls=%fused_computation.19 | loop fusion | flops 1155072 | bytes 1867776 | tf_op jit(solution)/shard_map/reduce_sum | solution.py:52
  3.5 0.1 bitcast_reduce_fusion
  3.6 1.1 %reshape.189 = bf16[4,4,48,128]{3,2,1,0:T(8,128)(2,1)S(1)} reshape(bf16[4,4,6144]{2,1,0:T(4,128)(2,1)} %param.11) | data formatting | bytes 393216 | tf_op jit(solution)/shard_map/reshape | solution.py:69
  4.7 1.0 %fusion.16 = f32[1,192]{1,0:T(1,128)S(1)} fusion(s32[192]{0:T(256)} %param.18), kind=kOutput, calls=%fused_computation.30 | convolution fusion | flops 184320 | bytes 1536 | tf_op jit(solution)/shard_map/dot_general | solution.py:39
  5.6 0.7 %multiply_add_fusion.1 = s32[192]{0:T(256)S(1)} fusion(s32[192]{0:T(256)} %param.18, f32[192]{0:T(256)S(1)} %bitcast.73), kind=kLoop, calls=%fused_computation.51 | loop fusion | flops 576 | bytes 2304 | tf_op jit(solution)/shard_map/add | solution.py:43
  6.3 0.1 eq.124
  6.4 0.2 fusion.4
  6.7 0.1 copy.54
  6.8 0.1 copy.53
  7.0 0.4 fusion.2
  7.4 0.3 copy.55
  7.7 0.3 select_select_fusion
  8.1 1.3 %pad_maximum_fusion = bf16[3,128,5,128]{3,0,2,1:T(4,128)(2,1)} fusion(bf16[3,128,1,128]{3,0,2,1:T(4,128)(2,1)S(1)} %select_select_fusion, bf16[3,128,4,128]{3,0,2,1:T(4,128)(2,1)S(1)} %copy.55), kind=kLoop, calls=%fused_computation.13 | loop fusion | flops 245760 | bytes 983040 | tf_op jit(solution)/shard_map/concatenate | solution.py:73
  9.3 11.9 %all-to-all-start = ((bf16[3,128,5,128]{3,0,2,1:T(4,128)(2,1)}), bf16[3,128,5,128]{3,0,2,1:T(4,128)(2,1)}, u32[]{:S(2)}, u32[]{:S(2)}) async-start(bf16[3,128,5,128]{3,0,2,1:T(4,128)(2,1)} %pad_maximum_fusion), calls=%async_computation | async-start | bytes 1310720 | tf_op jit(solution)/shard_map/all_to_all | solution.py:75
  21.2 0.1 eq.119
  21.3 0.1 eq.115
  21.4 0.7 %iota_compare_fusion.4 = pred[4,48,128]{2,1,0:T(8,128)(4,1)} fusion(s32[4,48]{1,0:T(4,128)S(1)} %eq.119), kind=kLoop, calls=%fused_computation.37 | loop fusion | flops 24576 | bytes 25344 | tf_op jit(solution)/shard_map/eq | solution.py:109
  22.1 0.6 add_divide_fusion
  22.8 13.0 %all-to-all-done = bf16[3,128,5,128]{3,0,2,1:T(4,128)(2,1)} async-done(((bf16[3,128,5,128]{3,0,2,1:T(4,128)(2,1)}), bf16[3,128,5,128]{3,0,2,1:T(4,128)(2,1)}, u32[]{:S(2)}, u32[]{:S(2)}) %all-to-all-start) | async-done | bytes 491552 | tf_op jit(solution)/shard_map/all_to_all | solution.py:75
  35.8 1.3 %slice.22 = bf16[3,128,4,128]{3,0,2,1:T(4,128)(2,1)S(1)} slice(bf16[3,128,5,128]{3,0,2,1:T(4,128)(2,1)} %all-to-all-done), slice={[0:3], [0:128], [0:4], [0:128]} | slice | bytes 786432 | tf_op jit(solution)/shard_map/slice | solution.py:78
  37.1 0.2 copy.56
  37.3 1.0 %fusion = f32[3,128,512]{1,2,0:T(8,128)S(1)} fusion(bf16[3,512,128]{2,1,0:T(8,128)(2,1)S(1)} %bitcast.63, f32[1,3,512,512]{3,2,1,0:T(8,128)S(1)} %copy-done), kind=kOutput, calls=%fused_computation.1 | convolution fusion | flops 603979776 | bytes 4325376 | tf_op jit(solution)/shard_map/cij,cjb->cib/dot_general | solution.py:96
  38.3 0.6 multiply_reduce_fusion
  38.8 1.3 %add_reduce_fusion = f32[3]{0:T(128)S(1)} fusion(bf16[3,128,5,128]{3,0,2,1:T(4,128)(2,1)} %all-to-all-done), kind=kLoop, calls=%fused_computation.25 | loop fusion | flops 1533 | bytes 1548 | tf_op jit(solution)/shard_map/reduce_sum | solution.py:79
  40.1 0.1 broadcast_multiply_fusion
  40.3 1.0 %copy.59 = f32[3,128,4,128]{3,2,0,1:T(4,128)} copy(f32[3,128,4,128]{3,2,1,0:T(4,128)S(1)} %bitcast.66) | data formatting | bytes 1572864 | tf_op jit(solution)/shard_map/reshape | solution.py:103
  41.3 5.7 %all-to-all-start.1 = ((f32[3,128,4,128]{3,2,0,1:T(4,128)}), f32[3,128,4,128]{3,2,0,1:T(4,128)}, u32[]{:S(2)}, u32[]{:S(2)}) async-start(f32[3,128,4,128]{3,2,0,1:T(4,128)} %copy.59), calls=%async_computation.1 | async-start | bytes 1572864 | tf_op jit(solution)/shard_map/all_to_all | solution.py:104
  47.0 1.9 %fusion.3 = f32[1,3,128,128]{3,2,1,0:T(8,128)} fusion(f32[1,3,128,128]{3,2,1,0:T(8,128)} %param.15, bf16[3,512,128]{2,1,0:T(8,128)(2,1)S(1)} %bitcast.64), kind=kOutput, calls=%fused_computation.7 | convolution fusion | flops 50380800 | bytes 786432 | tf_op jit(solution)/shard_map/cib,cid->cbd/dot_general | solution.py:92
  49.0 4.1 %bitcast_add_fusion = f32[1,3,512,512]{3,2,1,0:T(8,128)} fusion(f32[1,3,512,512]{3,2,1,0:T(8,128)} %param.14, bf16[3,512,128]{2,1,0:T(8,128)(2,1)S(1)} %bitcast.65), kind=kOutput, calls=%fused_computation | convolution fusion | flops 202113024 | bytes 6684672 | tf_op jit(solution)/shard_map/cib,cjb->cij/dot_general | solution.py:86
  53.1 10.0 %all-to-all-done.1 = f32[3,128,4,128]{3,2,0,1:T(4,128)} async-done(((f32[3,128,4,128]{3,2,0,1:T(4,128)}), f32[3,128,4,128]{3,2,0,1:T(4,128)}, u32[]{:S(2)}, u32[]{:S(2)}) %all-to-all-start.1) | async-done | bytes 786464 | tf_op jit(solution)/shard_map/all_to_all | solution.py:104
  63.1 1.7 %convolution_bitcast_fusion.1 = f32[4,4,48,128]{3,2,1,0:T(8,128)S(1)} fusion(f32[3,128,4,128]{3,2,0,1:T(4,128)} %all-to-all-done.1, pred[4,48,128]{2,1,0:T(8,128)(4,1)} %iota_compare_fusion.4, pred[4,48,3]{1,2,0:T(4,128)(4,1)S(1)} %iota_compare_fusion.5), kind=kOutput, calls=%fused_computation.5 | convolution fusion | flops 453058560 | bytes 1204800 | tf_op jit(solution)/shard_map/lnqd,qdrb->lnrb/dot_general | solution.py:112
  64.8 0.9 %reshape.192 = f32[4,4,6144]{2,1,0:T(4,128)} reshape(f32[4,4,48,128]{3,2,1,0:T(8,128)S(1)} %convolution_bitcast_fusion.1) | data formatting | bytes 786432 | tf_op jit(solution)/shard_map/reshape | solution.py:117
  (19 shorter events, 0.1 us)
Async XLA Ops:
  0.6 36.6 %copy-start = (f32[1,3,512,512]{3,2,1,0:T(8,128)S(1)}, f32[1,3,512,512]{3,2,1,0:T(8,128)}, u32[]{:S(2)}) copy-start(f32[1,3,512,512]{3,2,1,0:T(8,128)} %param.16) | copy-start | bytes 9437188
  3.4 17.8 %copy-start.5 = (s32[192]{0:T(256)S(1)}, s32[192]{0:T(256)}, u32[]{:S(2)}) copy-start(s32[192]{0:T(256)} %param.18) | copy-start | bytes 2308
  3.4 18.7 %copy-start.2 = (f32[6336]{0:T(1024)S(1)}, f32[6336]{0:T(1024)}, u32[]{:S(2)}) copy-start(f32[6336]{0:T(1024)} %param.19) | copy-start | bytes 76036
  3.5 18.7 %copy-start.3 = (f32[6336]{0:T(1024)S(1)}, f32[6336]{0:T(1024)}, u32[]{:S(2)}) copy-start(f32[6336]{0:T(1024)} %param.21) | copy-start | bytes 76036
  3.5 18.7 %copy-start.4 = (f32[6336]{0:T(1024)S(1)}, f32[6336]{0:T(1024)}, u32[]{:S(2)}) copy-start(f32[6336]{0:T(1024)} %param.20) | copy-start | bytes 76036
  9.3 26.5 %all-to-all-start = ((bf16[3,128,5,128]{3,0,2,1:T(4,128)(2,1)}), bf16[3,128,5,128]{3,0,2,1:T(4,128)(2,1)}, u32[]{:S(2)}, u32[]{:S(2)}) async-start(bf16[3,128,5,128]{3,0,2,1:T(4,128)(2,1)} %pad_maximum_fusion), calls=%async_computation | async-start | bytes 1310720 | tf_op jit(solution)/shard_map/all_to_all | solution.py:75
  35.8 2.5 %copy-start.1 = (f32[1,3,128,128]{3,2,1,0:T(8,128)S(1)}, f32[1,3,128,128]{3,2,1,0:T(8,128)}, u32[]{:S(2)}) copy-start(f32[1,3,128,128]{3,2,1,0:T(8,128)} %param.17) | copy-start | bytes 589828
  41.3 21.8 %all-to-all-start.1 = ((f32[3,128,4,128]{3,2,0,1:T(4,128)}), f32[3,128,4,128]{3,2,0,1:T(4,128)}, u32[]{:S(2)}, u32[]{:S(2)}) async-start(f32[3,128,4,128]{3,2,0,1:T(4,128)} %copy.59), calls=%async_computation.1 | async-start | bytes 1572864 | tf_op jit(solution)/shard_map/all_to_all | solution.py:104

commit v17 on v14

--- a/solution.py
+++ b/solution.py
@@ -73,11 +73,7 @@
         outgoing, ("shard", "tensor"), split_axis=1, concat_axis=1, tiled=True
     )
     block_grads = incoming[:, :, :row_count, :].reshape(slot_count, devices * row_count, BLOCK)
-    adam_sums = jnp.sum(
-        incoming[:, :, row_count, 0].astype(jnp.float32)
-        + incoming[:, :, row_count, 1].astype(jnp.float32),
-        axis=1,
-    )
+    adam_sums = jnp.sum(incoming[:, :, row_count, 0:2].astype(jnp.float32), axis=(1, 2))
     left_out = (
         stat_left
         + jnp.einsum("cib,cjb->cij", block_grads, block_grads, preferred_element_type=jnp.float32)[

time: 66.1 us -> 65.9 us (level)
  transfers between devices with their start and end apart: 2 -> 2, of which waited for: 2 -> 2; matrix products, arithmetic and copies ran while one was open for 11% -> 12% of each run, Pallas kernels for 0% -> 0%
where the time goes in v17:
time: 65.9 us; the launch traced here: 65.5 us
  waiting for transfers between devices  23.1 us (35%)
  starting transfers between devices  17.6 us (27%)
  matrix products  9.93 us (15%)
  other arithmetic  8.77 us (13%)
  local copies, waits for them, and re-layouts  5.35 us (8%)
  between operations  0.83 us (1%)
    all_to_all x1, waiting for transfers between devices, per_device(): lax.all_to_all(outgoing, ('shard', 'tensor'), split_axis=1, concat_axis=1...  13 us
    all_to_all x1, starting transfers between devices, per_device(): lax.all_to_all(outgoing, ('shard', 'tensor'), split_axis=1, concat_axis=1...  11.9 us
    all_to_all x1, waiting for transfers between devices, per_device(): lax.all_to_all(shaped, ('shard', 'tensor'), split_axis=1, concat_axis=1,...  10 us
    all_to_all x1, starting transfers between devices, per_device(): lax.all_to_all(shaped, ('shard', 'tensor'), split_axis=1, concat_axis=1,...  5.7 us
    dot_general x1, matrix products, per_device(): jnp.einsum('cib,cjb->cij', block_grads, block_grads, preferred_element_ty...  4.13 us
    reduce_sum x2, other arithmetic, per_device(): jnp.sum(jnp.square(direction).reshape(layer_count, row_count, block_count...  2.87 us
    dot_general x1, matrix products, per_device(): jnp.einsum('cib,cid->cbd', block_grads, block_grads, preferred_element_ty...  1.92 us
    dot_general x1, matrix products, per_device(): jnp.einsum('lnqd,qdrb->lnrb', placer, returned, precision=PRECISE, prefer...  1.7 us
  transfers between devices with their start and end apart: 2, of which 2 were waited for; matrix products, arithmetic and copies ran while one was open for 12% of the time, Pallas kernels for 0%

profile of v17, /device:TPU:1, one launch (start us, length us, event | category | flops | bytes accessed | tf_op | source)
XLA Modules:
  0.0 65.5 jit_solution(18056046608582940866)
XLA Ops:
  0.7 2.8 %multiply_reduce_fusion.1 = (f32[4,6144]{1,0:T(4,128)S(1)}, f32[4,4,6144]{2,1,0:T(4,128)}, f32[4,4,6144]{2,1,0:T(4,128)}) fusion(bf16[4,4,6144]{2,1,0:T(4,128)(2,1)} %param.11, f32[4,4,6144]{2,1,0:T(4,128)} %param.13, f32[4,4,6144]{2,1,0:T(4,128)} %param.12), kind=kLoop, calls=%fused_computation.19 | loop fusion | flops 1155072 | bytes 1867776 | tf_op jit(solution)/shard_map/reduce_sum | solution.py:49
  3.5 0.1 bitcast_reduce_fusion
  3.6 1.1 %reshape.187 = bf16[4,4,48,128]{3,2,1,0:T(8,128)(2,1)S(1)} reshape(bf16[4,4,6144]{2,1,0:T(4,128)(2,1)} %param.11) | data formatting | bytes 393216 | tf_op jit(solution)/shard_map/reshape | solution.py:66
  4.7 0.9 %convert_reduce_fusion.1 = s32[192]{0:T(256)S(1)} fusion(s32[192]{0:T(256)} %param.18), kind=kLoop, calls=%fused_computation.28 | loop fusion | flops 184128 | bytes 1536 | tf_op jit(solution)/shard_map/reduce_sum | solution.py:39
  5.6 0.7 %multiply_add_fusion.1 = s32[192]{0:T(256)S(1)} fusion(s32[192]{0:T(256)} %param.18, s32[192]{0:T(256)S(1)} %convert_reduce_fusion.1), kind=kLoop, calls=%fused_computation.49 | loop fusion | flops 384 | bytes 2304 | tf_op jit(solution)/shard_map/add | solution.py:40
  6.3 0.1 eq.124
  6.4 0.2 fusion.4
  6.6 0.1 copy.54
  6.8 0.1 copy.53
  6.9 0.4 fusion.2
  7.3 0.3 copy.55
  7.7 0.3 select_select_fusion
  8.0 1.3 %pad_maximum_fusion = bf16[3,128,5,128]{3,0,2,1:T(4,128)(2,1)} fusion(bf16[3,128,1,128]{3,0,2,1:T(4,128)(2,1)S(1)} %select_select_fusion, bf16[3,128,4,128]{3,0,2,1:T(4,128)(2,1)S(1)} %copy.55), kind=kLoop, calls=%fused_computation.13 | loop fusion | flops 245760 | bytes 983040 | tf_op jit(solution)/shard_map/concatenate | solution.py:70
  9.3 11.9 %all-to-all-start = ((bf16[3,128,5,128]{3,0,2,1:T(4,128)(2,1)}), bf16[3,128,5,128]{3,0,2,1:T(4,128)(2,1)}, u32[]{:S(2)}, u32[]{:S(2)}) async-start(bf16[3,128,5,128]{3,0,2,1:T(4,128)(2,1)} %pad_maximum_fusion), calls=%async_computation | async-start | bytes 1310720 | tf_op jit(solution)/shard_map/all_to_all | solution.py:72
  21.2 0.1 eq.119
  21.3 0.1 eq.115
  21.4 0.7 %iota_compare_fusion.4 = pred[4,48,128]{2,1,0:T(8,128)(4,1)} fusion(s32[4,48]{1,0:T(4,128)S(1)} %eq.119), kind=kLoop, calls=%fused_computation.37 | loop fusion | flops 24576 | bytes 25344 | tf_op jit(solution)/shard_map/eq | solution.py:102
  22.1 0.6 add_divide_fusion
  22.7 13.0 %all-to-all-done = bf16[3,128,5,128]{3,0,2,1:T(4,128)(2,1)} async-done(((bf16[3,128,5,128]{3,0,2,1:T(4,128)(2,1)}), bf16[3,128,5,128]{3,0,2,1:T(4,128)(2,1)}, u32[]{:S(2)}, u32[]{:S(2)}) %all-to-all-start) | async-done | bytes 491552 | tf_op jit(solution)/shard_map/all_to_all | solution.py:72
  35.7 1.3 %slice.18 = bf16[3,128,4,128]{3,0,2,1:T(4,128)(2,1)S(1)} slice(bf16[3,128,5,128]{3,0,2,1:T(4,128)(2,1)} %all-to-all-done), slice={[0:3], [0:128], [0:4], [0:128]} | slice | bytes 786432 | tf_op jit(solution)/shard_map/slice | solution.py:75
  37.0 0.2 copy.56
  37.2 1.0 %fusion = f32[3,128,512]{1,2,0:T(8,128)S(1)} fusion(bf16[3,512,128]{2,1,0:T(8,128)(2,1)S(1)} %bitcast.62, f32[1,3,512,512]{3,2,1,0:T(8,128)S(1)} %copy-done), kind=kOutput, calls=%fused_computation.1 | convolution fusion | flops 603979776 | bytes 4325376 | tf_op jit(solution)/shard_map/cij,cjb->cib/dot_general | solution.py:89
  38.2 0.6 multiply_reduce_fusion
  38.8 1.2 %convert_reduce_fusion = f32[3]{0:T(128)S(1)} fusion(bf16[3,128,5,128]{3,0,2,1:T(4,128)(2,1)} %all-to-all-done), kind=kLoop, calls=%fused_computation.25 | loop fusion | flops 1533 | bytes 1548 | tf_op jit(solution)/shard_map/reduce_sum | solution.py:76
  40.0 0.1 broadcast_multiply_fusion
  40.1 1.0 %copy.59 = f32[3,128,4,128]{3,2,0,1:T(4,128)} copy(f32[3,128,4,128]{3,2,1,0:T(4,128)S(1)} %bitcast.65) | data formatting | bytes 1572864 | tf_op jit(solution)/shard_map/reshape | solution.py:96
  41.1 5.7 %all-to-all-start.1 = ((f32[3,128,4,128]{3,2,0,1:T(4,128)}), f32[3,128,4,128]{3,2,0,1:T(4,128)}, u32[]{:S(2)}, u32[]{:S(2)}) async-start(f32[3,128,4,128]{3,2,0,1:T(4,128)} %copy.59), calls=%async_computation.1 | async-start | bytes 1572864 | tf_op jit(solution)/shard_map/all_to_all | solution.py:97
  46.9 1.9 %fusion.3 = f32[1,3,128,128]{3,2,1,0:T(8,128)} fusion(f32[1,3,128,128]{3,2,1,0:T(8,128)} %param.15, bf16[3,512,128]{2,1,0:T(8,128)(2,1)S(1)} %bitcast.63), kind=kOutput, calls=%fused_computation.7 | convolution fusion | flops 50380800 | bytes 786432 | tf_op jit(solution)/shard_map/cib,cid->cbd/dot_general | solution.py:85
  48.8 4.1 %bitcast_add_fusion = f32[1,3,512,512]{3,2,1,0:T(8,128)} fusion(f32[1,3,512,512]{3,2,1,0:T(8,128)} %param.14, bf16[3,512,128]{2,1,0:T(8,128)(2,1)S(1)} %bitcast.64), kind=kOutput, calls=%fused_computation | convolution fusion | flops 202113024 | bytes 6684672 | tf_op jit(solution)/shard_map/cib,cjb->cij/dot_general | solution.py:79
  52.9 10.0 %all-to-all-done.1 = f32[3,128,4,128]{3,2,0,1:T(4,128)} async-done(((f32[3,128,4,128]{3,2,0,1:T(4,128)}), f32[3,128,4,128]{3,2,0,1:T(4,128)}, u32[]{:S(2)}, u32[]{:S(2)}) %all-to-all-start.1) | async-done | bytes 786464 | tf_op jit(solution)/shard_map/all_to_all | solution.py:97
  62.9 1.7 %convolution_bitcast_fusion.1 = f32[4,4,48,128]{3,2,1,0:T(8,128)S(1)} fusion(f32[3,128,4,128]{3,2,0,1:T(4,128)} %all-to-all-done.1, pred[4,48,128]{2,1,0:T(8,128)(4,1)} %iota_compare_fusion.4, pred[4,48,3]{1,2,0:T(4,128)(4,1)S(1)} %iota_compare_fusion.5), kind=kOutput, calls=%fused_computation.5 | convolution fusion | flops 453058560 | bytes 1204800 | tf_op jit(solution)/shard_map/lnqd,qdrb->lnrb/dot_general | solution.py:105
  64.6 0.9 %reshape.190 = f32[4,4,6144]{2,1,0:T(4,128)} reshape(f32[4,4,48,128]{3,2,1,0:T(8,128)S(1)} %convolution_bitcast_fusion.1) | data formatting | bytes 786432 | tf_op jit(solution)/shard_map/reshape | solution.py:110
  (18 shorter events, 0.1 us)
Async XLA Ops:
  0.6 36.6 %copy-start = (f32[1,3,512,512]{3,2,1,0:T(8,128)S(1)}, f32[1,3,512,512]{3,2,1,0:T(8,128)}, u32[]{:S(2)}) copy-start(f32[1,3,512,512]{3,2,1,0:T(8,128)} %param.16) | copy-start | bytes 9437188
  3.4 17.8 %copy-start.5 = (s32[192]{0:T(256)S(1)}, s32[192]{0:T(256)}, u32[]{:S(2)}) copy-start(s32[192]{0:T(256)} %param.18) | copy-start | bytes 2308
  3.4 18.6 %copy-start.2 = (f32[6336]{0:T(1024)S(1)}, f32[6336]{0:T(1024)}, u32[]{:S(2)}) copy-start(f32[6336]{0:T(1024)} %param.19) | copy-start | bytes 76036
  3.5 18.6 %copy-start.3 = (f32[6336]{0:T(1024)S(1)}, f32[6336]{0:T(1024)}, u32[]{:S(2)}) copy-start(f32[6336]{0:T(1024)} %param.21) | copy-start | bytes 76036
  3.5 18.6 %copy-start.4 = (f32[6336]{0:T(1024)S(1)}, f32[6336]{0:T(1024)}, u32[]{:S(2)}) copy-start(f32[6336]{0:T(1024)} %param.20) | copy-start | bytes 76036
  9.3 26.5 %all-to-all-start = ((bf16[3,128,5,128]{3,0,2,1:T(4,128)(2,1)}), bf16[3,128,5,128]{3,0,2,1:T(4,128)(2,1)}, u32[]{:S(2)}, u32[]{:S(2)}) async-start(bf16[3,128,5,128]{3,0,2,1:T(4,128)(2,1)} %pad_maximum_fusion), calls=%async_computation | async-start | bytes 1310720 | tf_op jit(solution)/shard_map/all_to_all | solution.py:72
  35.7 2.5 %copy-start.1 = (f32[1,3,128,128]{3,2,1,0:T(8,128)S(1)}, f32[1,3,128,128]{3,2,1,0:T(8,128)}, u32[]{:S(2)}) copy-start(f32[1,3,128,128]{3,2,1,0:T(8,128)} %param.17) | copy-start | bytes 589828
  41.1 21.8 %all-to-all-start.1 = ((f32[3,128,4,128]{3,2,0,1:T(4,128)}), f32[3,128,4,128]{3,2,0,1:T(4,128)}, u32[]{:S(2)}, u32[]{:S(2)}) async-start(f32[3,128,4,128]{3,2,0,1:T(4,128)} %copy.59), calls=%async_computation.1 | async-start | bytes 1572864 | tf_op jit(solution)/shard_map/all_to_all | solution.py:97
